TPU v7x, 32 devices: a whole 2x2x4 slice. The times are simulated.
32 devices in a mesh: rows: 16 (over z, x, core), probe: 2 (over y).
Axes of the slice: x: 2, y: 2, z: 4, core: 2. Of those that a mesh axis runs over, the one named last changes fastest.
Arguments:
- targets: float32 [3, 4096], P(None, 'rows'), may hold values from 0 to 1
- sources: bfloat16 [3, 2048], P(None, 'rows'), may hold values from 0 to 1
- probes: bfloat16 [256, 2048], P('probe', 'rows'), may hold values from -6 to 6
- cluster_sizes: int32 [32], P(('rows', 'probe')), may hold values from 64 to 128, as said below
- leaf_ranks: int32 [32], P(('rows', 'probe')), may hold values from 128 to 256, as said below
Outputs:
- leaf_basis: float32 [256, 2, 4096], P(None, None, ('rows', 'probe'))
- top_factor: float32 [32, 256, 256], P(('rows', 'probe'))
Inputs may be any that keep to these rules, and one draw needn't show every extreme that they name: `cluster_sizes`: some leaf uses all 128 points in every draw. `leaf_ranks`: some leaf keeps all 256 rows in every draw.
All inputs are finite; a program needn't handle non-finite values.
Results may differ from a plain program's by a relative error of at most 0.0033.
Values may be sent and summed in bfloat16 or wider, within the bound.
No kernel may reach another device: no remote copies, remote signals or barrier semaphores. Data moves between devices by JAX's collectives and lax.ppermute only.
A program may use at most 64 MiB of HBM per device.

v0:
```python
import math

import jax
import jax.numpy as jnp
from jax import lax
from jax.sharding import PartitionSpec as P

wavenumber = 30.0
softening = 0.02


def partner_2(value, axis, apart):
    mask = 2**apart
    pairs = [(source, source ^ mask) for source in range(lax.axis_size(axis))]
    return lax.ppermute(value, axis, pairs)


def kernel_pair(source_pts, target_pts, col_total):
    diff_x = source_pts[0][:, None] - target_pts[0][None, :]
    diff_y = source_pts[1][:, None] - target_pts[1][None, :]
    diff_z = source_pts[2][:, None] - target_pts[2][None, :]
    distance = jnp.sqrt(diff_x * diff_x + diff_y * diff_y + diff_z * diff_z + softening * softening)
    amplitude = 1.0 / (distance * jnp.sqrt(jnp.float32(col_total)))
    kernel_cos = (amplitude * jnp.cos(wavenumber * distance)).astype(jnp.bfloat16)
    kernel_sin = (amplitude * jnp.sin(wavenumber * distance)).astype(jnp.bfloat16)
    return (kernel_cos, kernel_sin)


def sample_block(probe_piece, source_piece, target_pts, col_total):
    columns = probe_piece.shape[1]
    block_cols = math.gcd(columns, 256)
    block_count = columns // block_cols
    probe_parts = probe_piece.reshape(probe_piece.shape[0], block_count, block_cols).transpose(
        1, 0, 2
    )
    source_parts = source_piece.reshape(3, block_count, block_cols).transpose(1, 0, 2)

    def advance(running, pieces):
        probe_part, source_part = pieces
        kernel_cos, kernel_sin = kernel_pair(source_part.astype(jnp.float32), target_pts, col_total)
        part_cos = jnp.dot(probe_part, kernel_cos, preferred_element_type=jnp.float32)
        part_sin = jnp.dot(probe_part, kernel_sin, preferred_element_type=jnp.float32)
        return (running + jnp.stack([part_cos, part_sin]), None)

    starting = jnp.zeros((2, probe_piece.shape[0], target_pts.shape[1]), jnp.float32)
    result, _ = lax.scan(advance, starting, (probe_parts, source_parts))
    return result


def make_adder(target_pts, col_total):

    def add_columns(running, pieces, offset_col):
        return sample_block(pieces[0], pieces[1], target_pts, col_total)

    return add_columns


def cholesky_basis(matrix, nprobe_total):
    gram_matrix = jnp.dot(matrix, matrix.T, precision=lax.Precision.HIGHEST)
    shift_value = jnp.trace(gram_matrix) / nprobe_total
    factor = jnp.linalg.cholesky(
        gram_matrix + shift_value * jnp.eye(nprobe_total, dtype=matrix.dtype)
    )
    return jax.scipy.linalg.solve_triangular(factor, matrix, lower=True)


def per_device(targets, sources, probes, cluster_sizes, leaf_ranks):
    col_total = sources.shape[1] * lax.axis_size("rows")
    nprobe_total = probes.shape[0] * lax.axis_size("probe")
    leaf_rows = targets.shape[1] // lax.axis_size("probe")
    adder = make_adder(targets, col_total)
    starting = jnp.zeros((2, probes.shape[0], targets.shape[1]), jnp.float32)
    slab_samples = adder(
        starting,
        (
            lax.all_gather(probes, "rows", axis=1, tiled=True),
            lax.all_gather(sources, "rows", axis=1, tiled=True),
        ),
        jnp.int32(0),
    )
    samples = lax.all_to_all(slab_samples, "probe", split_axis=2, concat_axis=1, tiled=True)
    kept_rows = (jnp.arange(leaf_rows) < cluster_sizes[0]).astype(jnp.float32)
    matrix = jnp.concatenate([samples[0] * kept_rows, samples[1] * kept_rows], axis=1)
    basis_rows = cholesky_basis(matrix, nprobe_total)
    rank_rows = (jnp.arange(nprobe_total) < leaf_ranks[0]).astype(jnp.float32)
    basis_rows = basis_rows * rank_rows[:, None]
    projected = jnp.dot(matrix, basis_rows.T, precision=lax.Precision.HIGHEST)
    row_index = lax.axis_index("rows")
    for tree_bit in range(2):
        partner = partner_2(projected, "rows", tree_bit)
        is_left = row_index >> tree_bit & 1 == 0
        left_part = jnp.where(is_left, projected, partner)
        right_part = jnp.where(is_left, partner, projected)
        stacked = jnp.concatenate([left_part, right_part], axis=1)
        node_basis = cholesky_basis(stacked, nprobe_total)
        projected = jnp.dot(stacked, node_basis.T, precision=lax.Precision.HIGHEST)
    return (basis_rows.reshape(nprobe_total, 2, leaf_rows), projected[None])


def solution(mesh):
    return jax.shard_map(
        per_device,
        mesh=mesh,
        in_specs=(
            P(None, "rows"),
            P(None, "rows"),
            P("probe", "rows"),
            P(("rows", "probe")),
            P(("rows", "probe")),
        ),
        out_specs=(P(None, None, ("rows", "probe")), P(("rows", "probe"), None, None)),
        check_vma=False,
    )
```

profile of v0, /device:TPU:0, one launch (start us, length us, event | category | flops | bytes accessed | tf_op | source)
XLA Modules:
  0.0 280.5 jit_solution(17800109075621623467)
XLA Ops:
  1.5 24.6 %all_gather.6 = bf16[128,2048]{0,1:T(8,128)(2,1)S(1)} all-gather(bf16[128,128]{0,1:T(8,128)(2,1)S(1)} %copy.55), channel_id=1, replica_groups=mesh['rows'=16,'probe'=2] {'rows'}, dimensions={1}, use_global_device_ids=true | all-gather | bytes 557056 | tf_op jit(solution)/shard_map/all_gather | solution.py:76
  26.1 17.6 %all_gather.7 = bf16[3,2048]{1,0:T(4,128)(2,1)S(1)} all-gather(bf16[3,128]{1,0:T(4,128)(2,1)S(1)} %copy-done.1), channel_id=1, replica_groups=mesh['rows'=16,'probe'=2] {'rows'}, dimensions={1}, use_global_device_ids=true | all-gather | bytes 13056 | tf_op jit(solution)/shard_map/all_gather | solution.py:77
  43.7 21.9 %while.17 = (s32[]{:T(128)}, f32[2,128,256]{2,1,0:T(8,128)S(1)}, bf16[8,128,256]{1,2,0:T(8,128)(2,1)S(1)}, bf16[8,3,256]{2,1,0:T(4,128)(2,1)S(1)}, f32[3,256]{1,0:T(4,128)S(1)}, /*index=5*/s32[]{:T(128)}, s32[]{:T(128)}) while((s32[]{:T(128)}, f32[2,128,256]{2,1,0:T(8,128)S(1)}, bf16[8,128,256]{1,2,0:T(8,128)(2,1)S(1)}, ...), condition=%wide.region_1.2_spmd.clone, body=%wide.region_0.1_spmd.clone.sunk | while | flops 35586816 | bytes 1208939 | solution.py:46
  66.5 3.6 %all-to-all-start = ((f32[2,128,256]{1,0,2:T(2,128)}), f32[2,128,256]{1,0,2:T(2,128)S(1)}, u32[]{:S(2)}, u32[]{:S(2)}) async-start(f32[2,128,256]{1,0,2:T(2,128)} %copy.57), calls=%async_computation | async-start | bytes 524288 | tf_op jit(solution)/shard_map/all_to_all | solution.py:81
  71.4 4.6 %all-to-all-done = f32[2,128,256]{1,0,2:T(2,128)S(1)} async-done(((f32[2,128,256]{1,0,2:T(2,128)}), f32[2,128,256]{1,0,2:T(2,128)S(1)}, u32[]{:S(2)}, u32[]{:S(2)}) %all-to-all-start) | async-done | bytes 262176 | tf_op jit(solution)/shard_map/all_to_all | solution.py:81
  78.2 11.7 %cholesky.172 = f32[128,128]{1,0:T(8,128)S(1)} custom-call(f32[128,128]{1,0:T(8,128)S(1)} %cholesky.270), custom_call_target="Cholesky" | custom-call | tf_op jit(solution)/shard_map/jit(cholesky)/cholesky | solution.py:61
  90.1 9.8 %custom-call.20 = f32[1,128,128]{1,2,0:T(8,128)S(1)} custom-call(f32[1,128,128]{2,1,0:T(8,128)S(1)} %get-tuple-element.166), custom_call_target="InvertDiagBlocksLowerTriangular" | custom-call | tf_op jit(solution)/shard_map/jit(cholesky)/cholesky | solution.py:61
  100.5 11.7 %cholesky.189 = f32[128,128]{1,0:T(8,128)S(1)} custom-call(f32[128,128]{1,0:T(8,128)S(1)} %convolution_subtract_fusion.3), custom_call_target="Cholesky" | custom-call | tf_op jit(solution)/shard_map/jit(cholesky)/cholesky | solution.py:61
  114.3 4.1 %while.16 = (s32[]{:T(128)}, f32[256,256]{0,1:T(8,128)S(1)}, s32[2,2]{1,0:T(2,128)S(1)}, f32[2,128,128]{2,1,0:T(8,128)S(1)}, s32[]{:T(128)}) while((s32[]{:T(128)}, f32[256,256]{0,1:T(8,128)S(1)}, s32[2,2]{1,0:T(2,128)S(1)}, f32[2,128,128]{2,1,0:T(8,128)S(1)}, s32[]{:T(128)}) %tuple.104), condition=%wide.while_cond.1, body=%wide.while_body.1.sunk | while | flops 2 | bytes 393329 | solution.py:64
  114.9 1.3 dynamic-slice.20
  117.0 1.3 dynamic-slice.20
  118.4 20.1 %custom-call.15 = f32[2,128,128]{1,2,0:T(8,128)S(1)} custom-call(f32[2,128,128]{2,1,0:T(8,128)S(1)} %get-tuple-element.47), custom_call_target="InvertDiagBlocksLowerTriangular" | custom-call | tf_op jit(solution)/shard_map/jit(_solve_triangular)/triangular_solve | solution.py:64
  140.0 1.5 collective-permute-done
  141.5 1.6 select_reduce_fusion.1
  144.0 11.7 %cholesky.206 = f32[128,128]{1,0:T(8,128)S(1)} custom-call(f32[128,128]{1,0:T(8,128)S(1)} %cholesky.273), custom_call_target="Cholesky" | custom-call | tf_op jit(solution)/shard_map/jit(cholesky)/cholesky | solution.py:61
  155.8 9.8 %custom-call.21 = f32[1,128,128]{1,2,0:T(8,128)S(1)} custom-call(f32[1,128,128]{2,1,0:T(8,128)S(1)} %get-tuple-element.164), custom_call_target="InvertDiagBlocksLowerTriangular" | custom-call | tf_op jit(solution)/shard_map/jit(cholesky)/cholesky | solution.py:61
  166.1 11.9 %cholesky.223 = f32[128,128]{1,0:T(8,128)S(1)} custom-call(f32[128,128]{1,0:T(8,128)S(1)} %convolution_subtract_fusion.2), custom_call_target="Cholesky" | custom-call | tf_op jit(solution)/shard_map/jit(cholesky)/cholesky | solution.py:61
  180.5 3.8 %while.18 = (s32[]{:T(128)}, f32[256,256]{1,0:T(8,128)S(1)}, s32[2,2]{1,0:T(2,128)S(1)}, f32[2,128,128]{2,1,0:T(8,128)S(1)}, s32[]{:T(128)}) while((s32[]{:T(128)}, f32[256,256]{1,0:T(8,128)S(1)}, s32[2,2]{1,0:T(2,128)S(1)}, f32[2,128,128]{2,1,0:T(8,128)S(1)}, s32[]{:T(128)}) %tuple.116), condition=%wide.while_cond, body=%wide.while_body.sunk | while | flops 2 | bytes 131189 | solution.py:64
  181.1 1.3 bitcast_dynamic-update-slice_fusion.7
  183.0 1.3 bitcast_dynamic-update-slice_fusion.7
  184.3 19.7 %custom-call.22 = f32[2,128,128]{1,2,0:T(8,128)S(1)} custom-call(f32[2,128,128]{2,1,0:T(8,128)S(1)} %get-tuple-element.72), custom_call_target="InvertDiagBlocksLowerTriangular" | custom-call | tf_op jit(solution)/shard_map/jit(_solve_triangular)/triangular_solve | solution.py:64
  206.1 1.7 collective-permute-start.1
  209.1 5.5 %collective-permute-done.1 = f32[256,256]{0,1:T(8,128)S(1)} collective-permute-done((f32[256,256]{0,1:T(8,128)S(1)}, f32[256,256]{0,1:T(8,128)S(1)}, u32[]{:S(2)}, u32[]{:S(2)}) %collective-permute-start.1) | collective-permute-done | bytes 262176 | tf_op jit(solution)/shard_map/ppermute | solution.py:15
  214.6 1.6 select_reduce_fusion
  217.1 11.7 %cholesky.240 = f32[128,128]{1,0:T(8,128)S(1)} custom-call(f32[128,128]{1,0:T(8,128)S(1)} %cholesky.276), custom_call_target="Cholesky" | custom-call | tf_op jit(solution)/shard_map/jit(cholesky)/cholesky | solution.py:61
  228.8 9.8 %custom-call.23 = f32[1,128,128]{1,2,0:T(8,128)S(1)} custom-call(f32[1,128,128]{2,1,0:T(8,128)S(1)} %get-tuple-element.160), custom_call_target="InvertDiagBlocksLowerTriangular" | custom-call | tf_op jit(solution)/shard_map/jit(cholesky)/cholesky | solution.py:61
  239.1 11.9 %cholesky.257 = f32[128,128]{1,0:T(8,128)S(1)} custom-call(f32[128,128]{1,0:T(8,128)S(1)} %convolution_subtract_fusion.1), custom_call_target="Cholesky" | custom-call | tf_op jit(solution)/shard_map/jit(cholesky)/cholesky | solution.py:61
  253.6 3.8 %while.19 = (s32[]{:T(128)}, f32[256,256]{1,0:T(8,128)S(1)}, s32[2,2]{1,0:T(2,128)S(1)}, f32[2,128,128]{2,1,0:T(8,128)S(1)}, s32[]{:T(128)}) while((s32[]{:T(128)}, f32[256,256]{1,0:T(8,128)S(1)}, s32[2,2]{1,0:T(2,128)S(1)}, f32[2,128,128]{2,1,0:T(8,128)S(1)}, s32[]{:T(128)}) %tuple.117), condition=%wide.while_cond.clone, body=%wide.while_body.clone.sunk | while | flops 2 | bytes 131189 | solution.py:64
  254.2 1.3 bitcast_dynamic-update-slice_fusion.8
  256.1 1.3 bitcast_dynamic-update-slice_fusion.8
  257.5 19.7 %custom-call.24 = f32[2,128,128]{1,2,0:T(8,128)S(1)} custom-call(f32[2,128,128]{2,1,0:T(8,128)S(1)} %get-tuple-element.73), custom_call_target="InvertDiagBlocksLowerTriangular" | custom-call | tf_op jit(solution)/shard_map/jit(_solve_triangular)/triangular_solve | solution.py:64
  278.6 1.7 convolution_bitcast_fusion.2
  (141 shorter events, 40.3 us)
Async XLA Ops:
  1.5 24.6 %copy-start.1 = (bf16[3,128]{1,0:T(4,128)(2,1)S(1)}, bf16[3,128]{1,0:T(4,128)(2,1)}, u32[]{:S(2)}) copy-start(bf16[3,128]{1,0:T(4,128)(2,1)} %param.11) | copy-start | bytes 2308
  26.1 17.6 %copy-start = (f32[3,256]{1,0:T(4,128)S(1)}, f32[3,256]{1,0:T(4,128)}, u32[]{:S(2)}) copy-start(f32[3,256]{1,0:T(4,128)} %param.10) | copy-start | bytes 9220
  66.5 9.6 %all-to-all-start = ((f32[2,128,256]{1,0,2:T(2,128)}), f32[2,128,256]{1,0,2:T(2,128)S(1)}, u32[]{:S(2)}, u32[]{:S(2)}) async-start(f32[2,128,256]{1,0,2:T(2,128)} %copy.57), calls=%async_computation | async-start | bytes 524288 | tf_op jit(solution)/shard_map/all_to_all | solution.py:81
  139.9 1.6 collective-permute-start
  206.1 8.4 %collective-permute-start.1 = (f32[256,256]{0,1:T(8,128)S(1)}, f32[256,256]{0,1:T(8,128)S(1)}, u32[]{:S(2)}, u32[]{:S(2)}) collective-permute-start(f32[256,256]{0,1:T(8,128)S(1)} %fusion.14), channel_id=1, source_target_pairs={{0,4},{2,6},{4,0},{6,2},{8,12},{10,14},{12,8},{14,10},{16,20},{18,... | collective-permute-start | bytes 786440 | tf_op jit(solution)/shard_map/ppermute | solution.py:15
where the time goes:
time: 284 us; the launch traced here: 281 us
  other arithmetic  165 us (58%)
  blocking collectives  42.2 us (15%)
  matrix products  32.9 us (12%)
  local copies, waits for them, and re-layouts  14.5 us (5%)
  waiting for transfers between devices  11.6 us (4%)
  between operations  8.26 us (3%)
  starting transfers between devices  5.43 us (2%)
    another operation x20, other arithmetic, cholesky_basis(): jnp.linalg.cholesky(gram_matrix + shift_value * jnp.eye(nprobe_total, dty...  103 us
    another operation x7, other arithmetic, cholesky_basis(): return jax.scipy.linalg.solve_triangular(factor, matrix, lower=True)  59.5 us
    all_gather x1, blocking collectives, per_device(): lax.all_gather(probes, 'rows', axis=1, tiled=True)  24.6 us
    all_gather x1, blocking collectives, per_device(): lax.all_gather(sources, 'rows', axis=1, tiled=True)  17.6 us
    dot_general x8, matrix products, advance(): jnp.dot(probe_part, kernel_sin, preferred_element_type=jnp.float32)  10.3 us
    dot_general x8, matrix products, advance(): jnp.dot(probe_part, kernel_cos, preferred_element_type=jnp.float32)  10.3 us
    another operation x15, local copies, waits for them, and re-layouts, cholesky_basis(): return jax.scipy.linalg.solve_triangular(factor, matrix, lower=True)  7.76 us
    ppermute x2, waiting for transfers between devices, partner_2(): return lax.ppermute(value, axis, pairs)  6.99 us
  transfers between devices with their start and end apart: 3, of which 3 were waited for; matrix products, arithmetic and copies ran while one was open for 0% of the time, Pallas kernels for 0%

commit v1 on v0

v1 whole, which is shorter than its diff:
```python
import math

import jax
import jax.numpy as jnp
from jax import lax
from jax.experimental import pallas as pl
from jax.experimental.pallas import tpu as pltpu
from jax.sharding import PartitionSpec as P

wavenumber = 30.0
softening = 0.02

F32 = jnp.float32
BF16 = jnp.bfloat16
VMEM = pl.BlockSpec(memory_space=pltpu.VMEM)
SMEM = pl.BlockSpec(memory_space=pltpu.SMEM)
NN = ((1,), (0,))
NT = ((1,), (1,))
TN = ((0,), (0,))

LANES = 128
PANEL = 32
GROUP = 8


def split_bf16(value):
    high = value.astype(BF16)
    return high, (value - high.astype(F32)).astype(BF16)


def mxu(left, right, dims):
    return lax.dot_general(left, right, (dims, ((), ())), preferred_element_type=F32)


def dot3(left, right, dims):
    lh, ll = split_bf16(left)
    rh, rl = split_bf16(right)
    return mxu(lh, rh, dims) + (mxu(lh, rl, dims) + mxu(ll, rh, dims))


def pick_lane(tile, lane):
    where = jnp.full(tile.shape, lane, jnp.int32)
    return jnp.take_along_axis(tile, where, axis=1, mode="promise_in_bounds")


def pick_row(tile, row):
    return jnp.broadcast_to(tile[row : row + 1, :], tile.shape)


def sweep(t_ref):
    n = t_ref.shape[0]
    tiles = n // LANES
    steps = PANEL // 8
    lane = lax.broadcasted_iota(jnp.int32, (8, LANES), 1)
    row = lax.broadcasted_iota(jnp.int32, (8, LANES), 0)
    along_lanes = [jnp.ones((8, LANES), F32) for _ in range(tiles)]
    along_rows = []
    for start in range(0, n, PANEL):
        at, low = divmod(start, LANES)
        block = [
            [t_ref[start + 8 * i : start + 8 * i + 8, LANES * t : LANES * (t + 1)] for t in range(tiles)]
            for i in range(steps)
        ]
        pivots = [jnp.zeros((8, LANES), F32) for _ in range(steps)]
        for first in range(0, PANEL, GROUP):
            i0 = first // 8
            cols = [[pick_lane(block[i][at], low + first + a) for i in range(i0, steps)] for a in range(GROUP)]
            rows = [[pick_row(block[i0][t], a) for t in range(tiles)] for a in range(GROUP)]
            for a in range(GROUP):
                here = lane == low + first + a
                pivot = pick_row(cols[a][0], a)
                inverse = 1.0 / pivot
                along_lanes[at] = jnp.where(here, pivot, along_lanes[at])
                pivots[i0] = jnp.where(row == a, pivot, pivots[i0])
                swept = list(rows[a])
                swept[at] = jnp.where(here, 2.0 * swept[at], swept[at])
                factors = [c * inverse for c in cols[a]]
                factors[0] = jnp.where(row > a, factors[0], 0.0)
                for b in range(a + 1, GROUP):
                    entry = pick_row(cols[b][0], a)
                    factor = pick_row(factors[0], b)
                    cols[b] = [c - f * entry for c, f in zip(cols[b], factors)]
                    rows[b] = [r - factor * s for r, s in zip(rows[b], swept)]
                for x, i in enumerate(range(i0, steps)):
                    for t in range(tiles):
                        block[i][t] = block[i][t] - factors[x] * swept[t]
        for i in range(steps):
            for t in range(tiles):
                t_ref[start + 8 * i : start + 8 * i + 8, LANES * t : LANES * (t + 1)] = block[i][t]
        along_rows += pivots
        end = start + PANEL
        if end < n:
            whole = t_ref[start:end, :]
            rowi = lax.broadcasted_iota(jnp.int32, (PANEL, n), 0)
            coli = lax.broadcasted_iota(jnp.int32, (PANEL, n), 1)
            kept = jnp.where((coli < end) & (coli - start > rowi), 0.0, whole)
            scale = 1.0 / jnp.concatenate(pivots, axis=0)
            factors = (whole * jnp.concatenate([scale] * tiles, axis=1)).T
            colr = lax.broadcasted_iota(jnp.int32, (n - end, n), 1)
            rest = t_ref[end:n, :]
            rest = jnp.where((colr >= start) & (colr < end), 0.0, rest)
            t_ref[end:n, :] = rest - dot3(factors[end:n, :], kept, NN)
    return along_lanes, along_rows


def grids(n):
    rows = lax.broadcasted_iota(jnp.int32, (n, n), 0)
    cols = lax.broadcasted_iota(jnp.int32, (n, n), 1)
    return rows, cols


def factorize(gram, t_ref):
    n = gram.shape[0]
    rows, cols = grids(n)
    diagonal = jnp.where(rows == cols, gram, 0.0)
    shift = jnp.sum(jnp.sum(diagonal, axis=0, keepdims=True), axis=1, keepdims=True) / n
    t_ref[...] = gram / shift + jnp.where(rows == cols, 1.0, 0.0)
    along_lanes, along_rows = sweep(t_ref)
    by_col = jnp.concatenate([jnp.broadcast_to(x[0:1, :], (n, LANES)) for x in along_lanes], axis=1)
    by_row = jnp.concatenate([jnp.concatenate([x] * (n // LANES), axis=1) for x in along_rows], axis=0)
    return shift, by_row, by_col


def projected_rows(t_ref, by_row, by_col):
    rows, cols = grids(t_ref.shape[0])
    held = t_ref[...]
    return lax.rsqrt(by_row) * jnp.where(
        rows < cols, held, jnp.where(rows > cols, -held / by_col, by_row - 1.0)
    )


def inverse_factor(t_ref, by_row, by_col):
    rows, cols = grids(t_ref.shape[0])
    held = t_ref[...]
    return lax.rsqrt(by_row) * jnp.where(rows > cols, held / by_col, jnp.where(rows == cols, 1.0, 0.0))


def fold(full_ref, packed_ref):
    n = full_ref.shape[0]
    half = n // 2
    rows, cols = grids(half)
    upper = full_ref[0:half, 0:half]
    lower = full_ref[half:n, half:n]
    packed_ref[0:half, :] = full_ref[0:half, half:n]
    packed_ref[half:n, :] = jnp.where(rows <= cols, upper, lower)
    packed_ref[n : n + 8, :] = jnp.broadcast_to(
        jnp.sum(jnp.where(rows == cols, lower, 0.0), axis=0, keepdims=True), (8, half)
    )


def unfold_add(packed_ref, full_ref):
    n = full_ref.shape[0]
    half = n // 2
    rows, cols = grids(half)
    corner = packed_ref[0:half, :]
    both = packed_ref[half:n, :]
    turned = both.T
    line = jnp.broadcast_to(packed_ref[n : n + 1, :], (half, half))
    upper = jnp.where(rows <= cols, both, turned)
    lower = jnp.where(rows == cols, line, jnp.where(rows > cols, both, turned))
    top = jnp.concatenate([upper, corner], axis=1)
    bottom = jnp.concatenate([corner.T, lower], axis=1)
    return full_ref[...] + jnp.concatenate([top, bottom], axis=0)


def kernel_body(col_total, targets_ref, sources_ref, out_ref):
    pieces, _, width = sources_ref.shape
    m = targets_ref.shape[1]
    turned = jnp.concatenate([targets_ref[...], jnp.zeros((m - 8, m), F32)], axis=0).T
    points = [jnp.broadcast_to(turned[:, c : c + 1], (m, width)) for c in range(3)]
    size = 1.0 / math.sqrt(col_total)
    turns = wavenumber * 2.0 / math.pi
    h = math.pi / 2
    for i in range(pieces):
        source = sources_ref[i].astype(F32)
        square = softening * softening
        for c in range(3):
            diff = source[c : c + 1, :] - points[c]
            square = square + diff * diff
        near = lax.rsqrt(square)
        amplitude = near * size
        quarter = (square * near) * turns
        whole = jnp.round(quarter)
        rest = quarter - whole
        r2 = rest * rest
        sine = rest * (h + r2 * (-(h**3) / 6 + r2 * (h**5 / 120 + r2 * (-(h**7) / 5040))))
        cosine = 1.0 + r2 * (-(h**2) / 2 + r2 * (h**4 / 24 + r2 * (-(h**6) / 720 + r2 * (h**8 / 40320))))
        count = whole.astype(jnp.int32)
        odd = (count & 1) == 1
        first = jnp.where(odd, sine, cosine)
        second = jnp.where(odd, cosine, sine)
        first = jnp.where(((count + 1) & 2) == 0, first, -first)
        second = jnp.where((count & 2) == 0, second, -second)
        out_ref[i, 0:m, :] = (amplitude * first).astype(BF16)
        out_ref[i, m : 2 * m, :] = (amplitude * second).astype(BF16)


def accumulate(probe_ref, kernel_ref, total):
    pieces = probe_ref.shape[0]
    both = 2 if pieces % 2 == 0 else 1

    def one(i, total):
        left = jnp.concatenate([probe_ref[both * i + k] for k in range(both)], axis=1)
        right = jnp.concatenate([kernel_ref[both * i + k] for k in range(both)], axis=1)
        return total + mxu(left, right, NT)

    count = pieces // both
    return lax.fori_loop(0, count, one, total, unroll=count <= 8)


def leaf_body(blocks, place_ref, sizes_ref, ranks_ref, *refs):
    near, far = refs[:blocks], refs[blocks : 2 * blocks]
    near_kernel, far_kernel, h_ref, w_ref, m_ref, t_ref = refs[2 * blocks :]
    n = h_ref.shape[0]
    rows, cols = grids(n)
    high = n // blocks
    for o in range(blocks):
        total = jnp.zeros((high, n), F32)
        total = accumulate(near[o], near_kernel, total)
        total = accumulate(far[o], far_kernel, total)
        at = pl.multiple_of((place_ref[0] ^ o) * high, high)
        m_ref[pl.ds(at, high), :] = total
    used = sizes_ref[0]
    half = n // 2
    inside = cols - jnp.where(cols >= half, half, 0) < used
    matrix = jnp.where(inside, m_ref[...], 0.0)
    m_ref[...] = matrix
    gram = dot3(matrix, matrix, NT)
    shift, by_row, by_col = factorize(gram, t_ref)
    in_rank = rows < ranks_ref[0]
    value = jnp.where(in_rank, projected_rows(t_ref, by_row, by_col), 0.0)
    h_ref[...] = dot3(value, value, TN) * shift
    w_ref[...] = jnp.where(in_rank, inverse_factor(t_ref, by_row, by_col) * lax.rsqrt(shift), 0.0)


def basis_body(w_ref, m_ref, b_ref):
    b_ref[...] = dot3(w_ref[...], m_ref[...], NN)


def node_body(own_ref, other_ref, h_ref, packed_ref, t_ref):
    shift, by_row, by_col = factorize(own_ref[...] + other_ref[...], t_ref)
    value = projected_rows(t_ref, by_row, by_col)
    h_ref[...] = dot3(value, value, TN) * shift
    fold(h_ref, packed_ref)


def top_body(own_ref, other_ref, z_ref, t_ref):
    shift, by_row, by_col = factorize(unfold_add(other_ref, own_ref), t_ref)
    value = projected_rows(t_ref, by_row, by_col)
    z_ref[...] = (value * jnp.sqrt(shift)).T


def call(body, name, outs, operands, specs=None, scratch=(), flops=0):
    bytes_used = sum(x.size * x.dtype.itemsize for x in (*outs, *operands))
    return pl.pallas_call(
        body,
        name=name,
        out_shape=list(outs),
        in_specs=list(specs or [VMEM] * len(operands)),
        out_specs=[VMEM] * len(outs),
        scratch_shapes=list(scratch),
        cost_estimate=pl.CostEstimate(flops=flops, bytes_accessed=bytes_used, transcendentals=0),
    )(*operands)


def flip(value, axis, mask):
    pairs = [(source, source ^ mask) for source in range(lax.axis_size(axis))]
    return lax.ppermute(value, axis, pairs)


def per_device(targets, sources, probes, cluster_sizes, leaf_ranks):
    rows_size = lax.axis_size("rows")
    probe_size = lax.axis_size("probe")
    col_total = sources.shape[1] * rows_size
    n = probes.shape[0] * probe_size
    leaf_rows = targets.shape[1] // probe_size
    place = lax.axis_index("probe")

    points = lax.dynamic_slice_in_dim(targets, place * leaf_rows, leaf_rows, 1)
    points = jnp.pad(points, ((0, 8 - points.shape[0]), (0, 0)))

    def evaluate(pieces):
        out = jax.ShapeDtypeStruct((pieces.shape[0], 2 * leaf_rows, pieces.shape[2]), BF16)
        return call(
            lambda *refs: kernel_body(col_total, *refs), "kernel_values", [out], [points, pieces],
            flops=100 * out.size,
        )[0]

    mask = rows_size // 2
    held, held_sources = probes[None], sources[None]
    values = []
    done = 0
    while mask > 1:
        more_sources = flip(held_sources, "rows", mask)
        more = flip(held, "rows", mask)
        held = jnp.concatenate([held, more], axis=0)
        held_sources = jnp.concatenate([held_sources, more_sources], axis=0)
        mask //= 2
    near = [held]
    far_sources = flip(held_sources, "rows", 1)
    bit = 1
    while bit < probe_size:
        near += [flip(x, "probe", bit) for x in near]
        bit *= 2
    far = [flip(x, "rows", 1) for x in near]
    near_kernel = evaluate(held_sources)
    far_kernel = evaluate(far_sources)

    square = jax.ShapeDtypeStruct((n, n), F32)
    scratch = [pltpu.VMEM((n, n), F32)]
    blocks = len(near)
    h, w, m = call(
        lambda *refs: leaf_body(blocks, *refs), "leaf", [square] * 3,
        [place[None], cluster_sizes, leaf_ranks, *near, *far, near_kernel, far_kernel],
        specs=[SMEM] * 3 + [VMEM] * (2 * blocks + 2), scratch=scratch, flops=n**3,
    )
    other = flip(h, "rows", 1)
    basis = call(basis_body, "basis", [square], [w, m], flops=6 * n**3)[0]
    packed = jax.ShapeDtypeStruct((n + 8, n // 2), F32)
    h, sent = call(node_body, "node", [square, packed], [h, other], scratch=scratch, flops=n**3)
    other = flip(sent, "rows", 2)
    top = call(top_body, "top", [square], [h, other], scratch=scratch, flops=n**3)[0]
    return (basis.reshape(n, 2, leaf_rows), top[None])


def solution(mesh):
    return jax.shard_map(
        per_device,
        mesh=mesh,
        in_specs=(
            P(None, "rows"),
            P(None, "rows"),
            P("probe", "rows"),
            P(("rows", "probe")),
            P(("rows", "probe")),
        ),
        out_specs=(P(None, None, ("rows", "probe")), P(("rows", "probe"), None, None)),
        check_vma=False,
    )
```

time: 284 us -> 79.4 us (0.28); the launches traced: 281 us -> 79 us
  other arithmetic: 165 us -> 0.84 us
  blocking collectives: 42.2 us -> 0 us
  Pallas kernels: 0 us -> 37.3 us
  matrix products: 32.9 us -> 0 us
  starting transfers between devices: 5.43 us -> 17.1 us
  local copies, waits for them, and re-layouts: 14.5 us -> 5.16 us
  between operations: 8.26 us -> 2.05 us
  waiting for transfers between devices: 11.6 us -> 16.5 us
    another operation x27 -> x0, other arithmetic: 163 us -> none  [the longest x20 103 us: cholesky_basis(): jnp.linalg.cholesky(gram_matrix + shift_value * jnp.eye(nprobe_total, dty...]
    all_gather x2 -> x0, blocking collectives: 42.2 us -> none  [the longest x1 24.6 us: per_device(): lax.all_gather(probes, 'rows', axis=1, tiled=True)]
    pallas_call x0 -> x6, Pallas kernels: none -> 37.3 us  [call(): pl.pallas_call(body, name=name, out_shape=list(outs), in_specs=list(specs...]
    dot_general x22 -> x0, matrix products: 27.6 us -> none  [the longest x8 10.3 us: advance(): jnp.dot(probe_part, kernel_sin, preferred_element_type=jnp.float32)]
    ppermute x2 -> x12, starting transfers between devices: 1.81 us -> 17.1 us  [flip(): return lax.ppermute(value, axis, pairs)]
    another operation x36 -> x0, local copies, waits for them, and re-layouts: 12.1 us -> none  [the longest x15 7.76 us: cholesky_basis(): return jax.scipy.linalg.solve_triangular(factor, matrix, lower=True)]
    ppermute x2 -> x12, waiting for transfers between devices: 6.99 us -> 16.5 us  [flip(): return lax.ppermute(value, axis, pairs)]
    another operation x15 -> x0, matrix products: 5.24 us -> none  [the longest x9 3.82 us: cholesky_basis(): return jax.scipy.linalg.solve_triangular(factor, matrix, lower=True)]
  transfers between devices with their start and end apart: 3 -> 12, of which waited for: 3 -> 8; matrix products, arithmetic and copies ran while one was open for 0% -> 3% of each run, Pallas kernels for 0% -> 9%
where the time goes in v1:
time: 79.4 us; the launch traced here: 79 us
  Pallas kernels  37.3 us (47%)
  starting transfers between devices  17.1 us (22%)
  waiting for transfers between devices  16.5 us (21%)
  local copies, waits for them, and re-layouts  5.16 us (6%)
  between operations  2.05 us (3%)
  other arithmetic  0.84 us (1%)
    pallas_call x6, Pallas kernels, call(): pl.pallas_call(body, name=name, out_shape=list(outs), in_specs=list(specs...  37.3 us
    ppermute x12, starting transfers between devices, flip(): return lax.ppermute(value, axis, pairs)  17.1 us
    ppermute x12, waiting for transfers between devices, flip(): return lax.ppermute(value, axis, pairs)  16.5 us
    unnamed x22, local copies, waits for them, and re-layouts  2.77 us
    reshape x1, local copies, waits for them, and re-layouts, per_device(): return (basis.reshape(n, 2, leaf_rows), top[None])  1.78 us
  transfers between devices with their start and end apart: 12, of which 8 were waited for; matrix products, arithmetic and copies ran while one was open for 3% of the time, Pallas kernels for 9%

profile of v1, /device:TPU:0, one launch (start us, length us, event | category | flops | bytes accessed | tf_op | source)
XLA Modules:
  0.0 79.0 jit_solution(12674284664914888058)
XLA Ops:
  0.7 4.1 %collective-permute-start = (bf16[1,128,128]{2,1,0:T(8,128)(2,1)}, bf16[1,128,128]{2,1,0:T(8,128)(2,1)S(1)}, u32[]{:S(2)}, u32[]{:S(2)}) collective-permute-start(bf16[1,128,128]{2,1,0:T(8,128)(2,1)} %bitcast.4), channel_id=1, source_target_pairs={{0,16},{2,18},{4,20},{6,22},{8,24},{10,26},{12,28},{14,30},{16,0},... | collective-permute-start | bytes 98312 | tf_op jit(solution)/shard_map/ppermute | solution.py:268
  4.8 2.5 %collective-permute-done = bf16[1,128,128]{2,1,0:T(8,128)(2,1)S(1)} collective-permute-done((bf16[1,128,128]{2,1,0:T(8,128)(2,1)}, bf16[1,128,128]{2,1,0:T(8,128)(2,1)S(1)}, u32[]{:S(2)}, u32[]{:S(2)}) %collective-permute-start) | collective-permute-done | bytes 32800 | tf_op jit(solution)/shard_map/ppermute | solution.py:268
  7.2 0.8 pad_maximum_fusion.2
  8.0 1.6 %collective-permute-start.1 = (bf16[2,128,128]{2,1,0:T(8,128)(2,1)S(1)}, bf16[2,128,128]{2,1,0:T(8,128)(2,1)S(1)}, u32[]{:S(2)}, u32[]{:S(2)}) collective-permute-start(bf16[2,128,128]{2,1,0:T(8,128)(2,1)S(1)} %pad_maximum_fusion.2), channel_id=1, source_target_pairs={{0,8},{2,10},{4,12},{6,14},{8,0},{10,2},{12,4},{14,6},{16,24},{18,... | collective-permute-start | bytes 196616 | tf_op jit(solution)/shard_map/ppermute | solution.py:268
  9.6 2.7 %collective-permute-done.1 = bf16[2,128,128]{2,1,0:T(8,128)(2,1)S(1)} collective-permute-done((bf16[2,128,128]{2,1,0:T(8,128)(2,1)S(1)}, bf16[2,128,128]{2,1,0:T(8,128)(2,1)S(1)}, u32[]{:S(2)}, u32[]{:S(2)}) %collective-permute-start.1) | collective-permute-done | bytes 65568 | tf_op jit(solution)/shard_map/ppermute | solution.py:268
  12.3 1.8 %collective-permute-start.2 = (bf16[4,128,128]{2,1,0:T(8,128)(2,1)S(1)}, bf16[4,128,128]{2,1,0:T(8,128)(2,1)S(1)}, u32[]{:S(2)}, u32[]{:S(2)}) collective-permute-start(bf16[4,128,128]{2,1,0:T(8,128)(2,1)S(1)} %pad_maximum_fusion.1), channel_id=1, source_target_pairs={{0,4},{2,6},{4,0},{6,2},{8,12},{10,14},{12,8},{14,10},{16,20},{18,... | collective-permute-start | bytes 393224 | tf_op jit(solution)/shard_map/ppermute | solution.py:268
  14.1 3.3 %collective-permute-done.2 = bf16[4,128,128]{2,1,0:T(8,128)(2,1)S(1)} collective-permute-done((bf16[4,128,128]{2,1,0:T(8,128)(2,1)S(1)}, bf16[4,128,128]{2,1,0:T(8,128)(2,1)S(1)}, u32[]{:S(2)}, u32[]{:S(2)}) %collective-permute-start.2) | collective-permute-done | bytes 131104 | tf_op jit(solution)/shard_map/ppermute | solution.py:268
  17.4 1.8 %collective-permute-start.3 = (bf16[8,128,128]{2,1,0:T(8,128)(2,1)S(1)}, bf16[8,128,128]{2,1,0:T(8,128)(2,1)S(1)}, u32[]{:S(2)}, u32[]{:S(2)}) collective-permute-start(bf16[8,128,128]{2,1,0:T(8,128)(2,1)S(1)} %pad_maximum_fusion.refs_3_), channel_id=1, source_target_pairs={{0,1},{1,0},{2,3},{3,2},{4,5},{5,4},{6,7},{7,6},{8,9},{9,8},{10,11... | collective-permute-start | bytes 786440 | tf_op jit(solution)/shard_map/ppermute | solution.py:268
  19.2 2.4 %collective-permute-start.6 = (bf16[1,3,128]{2,1,0:T(4,128)(2,1)S(1)}, bf16[1,3,128]{2,1,0:T(4,128)(2,1)S(1)}, u32[]{:S(2)}, u32[]{:S(2)}) collective-permute-start(bf16[1,3,128]{2,1,0:T(4,128)(2,1)S(1)} %bitcast.9), channel_id=1, source_target_pairs={{0,16},{2,18},{4,20},{6,22},{8,24},{10,26},{12,28},{14,30},{16,0},... | collective-permute-start | bytes 2312 | tf_op jit(solution)/shard_map/ppermute | solution.py:268
  21.6 2.1 %collective-permute-done.6 = bf16[1,3,128]{2,1,0:T(4,128)(2,1)S(1)} collective-permute-done((bf16[1,3,128]{2,1,0:T(4,128)(2,1)S(1)}, bf16[1,3,128]{2,1,0:T(4,128)(2,1)S(1)}, u32[]{:S(2)}, u32[]{:S(2)}) %collective-permute-start.6) | collective-permute-done | bytes 800 | tf_op jit(solution)/shard_map/ppermute | solution.py:268
  23.7 1.3 %collective-permute-start.7 = (bf16[2,3,128]{2,1,0:T(4,128)(2,1)S(1)}, bf16[2,3,128]{2,1,0:T(4,128)(2,1)S(1)}, u32[]{:S(2)}, u32[]{:S(2)}) collective-permute-start(bf16[2,3,128]{2,1,0:T(4,128)(2,1)S(1)} %pad_maximum_fusion.5), channel_id=1, source_target_pairs={{0,8},{2,10},{4,12},{6,14},{8,0},{10,2},{12,4},{14,6},{16,24},{18,... | collective-permute-start | bytes 4616 | tf_op jit(solution)/shard_map/ppermute | solution.py:268
  25.0 0.5 collective-permute-start.5
  25.5 1.7 %collective-permute-done.7 = bf16[2,3,128]{2,1,0:T(4,128)(2,1)S(1)} collective-permute-done((bf16[2,3,128]{2,1,0:T(4,128)(2,1)S(1)}, bf16[2,3,128]{2,1,0:T(4,128)(2,1)S(1)}, u32[]{:S(2)}, u32[]{:S(2)}) %collective-permute-start.7) | collective-permute-done | bytes 1568 | tf_op jit(solution)/shard_map/ppermute | solution.py:268
  27.3 1.6 %collective-permute-start.8 = (bf16[4,3,128]{2,1,0:T(4,128)(2,1)S(1)}, bf16[4,3,128]{2,1,0:T(4,128)(2,1)S(1)}, u32[]{:S(2)}, u32[]{:S(2)}) collective-permute-start(bf16[4,3,128]{2,1,0:T(4,128)(2,1)S(1)} %pad_maximum_fusion.4), channel_id=1, source_target_pairs={{0,4},{2,6},{4,0},{6,2},{8,12},{10,14},{12,8},{14,10},{16,20},{18,... | collective-permute-start | bytes 9224 | tf_op jit(solution)/shard_map/ppermute | solution.py:268
  28.8 2.1 %collective-permute-done.8 = bf16[4,3,128]{2,1,0:T(4,128)(2,1)S(1)} collective-permute-done((bf16[4,3,128]{2,1,0:T(4,128)(2,1)S(1)}, bf16[4,3,128]{2,1,0:T(4,128)(2,1)S(1)}, u32[]{:S(2)}, u32[]{:S(2)}) %collective-permute-start.8) | collective-permute-done | bytes 3104 | tf_op jit(solution)/shard_map/ppermute | solution.py:268
  32.4 0.6 pad.4.refs_0_
  33.0 2.5 %kernel_values.2.refs_7_ = bf16[8,256,128]{2,1,0:T(8,128)(2,1)} custom-call(f32[8,128]{1,0:T(8,128)} %pad.4.refs_0_, bf16[8,3,128]{2,1,0:T(4,128)(2,1)} %copy-done.8), custom_call_target="tpu_custom_call" | custom-call | flops 26214400 | bytes 534528 | tf_op jit(solution)/shard_map/kernel_values/pallas_call | solution.py:255
  35.5 0.6 copy-done.10
  36.1 2.5 %kernel_values.3.refs_8_ = bf16[8,256,128]{2,1,0:T(8,128)(2,1)} custom-call(f32[8,128]{1,0:T(8,128)} %pad.4.refs_0_, bf16[8,3,128]{2,1,0:T(4,128)(2,1)} %copy-done.10), custom_call_target="tpu_custom_call" | custom-call | flops 26214400 | bytes 534528 | tf_op jit(solution)/shard_map/kernel_values/pallas_call | solution.py:255
  38.6 0.7 copy-done.4
  39.3 0.1 copy-done.5
  39.4 11.3 %leaf.1 = (f32[256,256]{1,0:T(8,128)}, f32[256,256]{1,0:T(8,128)}, f32[256,256]{1,0:T(8,128)}) custom-call(s32[1]{0:T(128)} %bitcast.refs_0_, s32[1]{0:T(128)S(6)} %copy.7.refs_1_, s32[1]{0:T(128)S(6)} %copy.8.refs_2_, bf16[8,128,128]{2,1,0:T(8,128)(2,1)} %copy-done.1, bf16[8,128,128]{2,1,0:T(8,128)(2,1)} %copy-done.3, bf16[8,128,128]{2,1,0:T(8,128)(2,1)} %copy-done.4, ...), custom_call_target="tpu_custom_call" | custom-call | flops 16777216 | bytes 2883596 | tf_op jit(solution)/shard_map/leaf/pallas_call | solution.py:255
  50.7 0.5 collective-permute-start.10
  51.1 1.4 %collective-permute-done.10.other_ref = f32[256,256]{1,0:T(8,128)S(1)} collective-permute-done((f32[256,256]{1,0:T(8,128)}, f32[256,256]{1,0:T(8,128)S(1)}, u32[]{:S(2)}, u32[]{:S(2)}) %collective-permute-start.10) | collective-permute-done | bytes 262176 | tf_op jit(solution)/shard_map/ppermute | solution.py:268
  52.5 0.7 copy-done.6
  53.2 9.7 %node.1 = (f32[256,256]{1,0:T(8,128)}, f32[264,128]{1,0:T(8,128)}) custom-call(f32[256,256]{1,0:T(8,128)} %get-tuple-element.9.own_ref, f32[256,256]{1,0:T(8,128)} %copy-done.6), custom_call_target="tpu_custom_call" | custom-call | flops 16777216 | bytes 921600 | tf_op jit(solution)/shard_map/node/pallas_call | solution.py:255
  62.9 1.5 %collective-permute-start.11 = (f32[264,128]{1,0:T(8,128)}, f32[264,128]{1,0:T(8,128)S(1)}, u32[]{:S(2)}, u32[]{:S(2)}) collective-permute-start(f32[264,128]{1,0:T(8,128)} %get-tuple-element.11), channel_id=1, source_target_pairs={{0,4},{2,6},{4,0},{6,2},{8,12},{10,14},{12,8},{14,10},{16,20},{18,... | collective-permute-start | bytes 405512 | tf_op jit(solution)/shard_map/ppermute | solution.py:268
  64.4 2.0 %basis.1 = f32[256,256]{1,0:T(8,128)} custom-call(f32[256,256]{1,0:T(8,128)} %get-tuple-element.7.w_ref, f32[256,256]{1,0:T(8,128)} %get-tuple-element.8.m_ref), custom_call_target="tpu_custom_call" | custom-call | flops 100663296 | bytes 786432 | tf_op jit(solution)/shard_map/basis/pallas_call | solution.py:255
  66.4 1.8 %reshape.7 = f32[256,2,128]{2,1,0:T(2,128)} reshape(f32[256,256]{1,0:T(8,128)} %basis.1) | data formatting | bytes 524288 | tf_op jit(solution)/shard_map/reshape | solution.py:323
  68.2 0.8 %collective-permute-done.11.other_ref = f32[264,128]{1,0:T(8,128)S(1)} collective-permute-done((f32[264,128]{1,0:T(8,128)}, f32[264,128]{1,0:T(8,128)S(1)}, u32[]{:S(2)}, u32[]{:S(2)}) %collective-permute-start.11) | collective-permute-done | bytes 135200 | tf_op jit(solution)/shard_map/ppermute | solution.py:268
  69.0 0.7 copy-done.7
  69.6 9.3 %top.1 = f32[256,256]{1,0:T(8,128)} custom-call(f32[256,256]{1,0:T(8,128)} %get-tuple-element.10.own_ref, f32[264,128]{1,0:T(8,128)} %copy-done.7), custom_call_target="tpu_custom_call" | custom-call | flops 16777216 | bytes 659456 | tf_op jit(solution)/shard_map/top/pallas_call | solution.py:255
  (29 shorter events, 0.2 us)
Async XLA Ops:
  0.6 30.4 %copy-start = (f32[3,256]{1,0:T(4,128)S(1)}, f32[3,256]{1,0:T(4,128)}, u32[]{:S(2)}) copy-start(f32[3,256]{1,0:T(4,128)} %param.5) | copy-start | bytes 9220
  0.6 11.6 %copy-start.2 = (bf16[128,128]{1,0:T(8,128)(2,1)S(1)}, bf16[128,128]{1,0:T(8,128)(2,1)}, u32[]{:S(2)}) copy-start(bf16[128,128]{1,0:T(8,128)(2,1)} %param.7) | copy-start | bytes 98308
  0.7 6.6 %collective-permute-start = (bf16[1,128,128]{2,1,0:T(8,128)(2,1)}, bf16[1,128,128]{2,1,0:T(8,128)(2,1)S(1)}, u32[]{:S(2)}, u32[]{:S(2)}) collective-permute-start(bf16[1,128,128]{2,1,0:T(8,128)(2,1)} %bitcast.4), channel_id=1, source_target_pairs={{0,16},{2,18},{4,20},{6,22},{8,24},{10,26},{12,28},{14,30},{16,0},... | collective-permute-start | bytes 98312 | tf_op jit(solution)/shard_map/ppermute | solution.py:268
  8.0 4.3 %collective-permute-start.1 = (bf16[2,128,128]{2,1,0:T(8,128)(2,1)S(1)}, bf16[2,128,128]{2,1,0:T(8,128)(2,1)S(1)}, u32[]{:S(2)}, u32[]{:S(2)}) collective-permute-start(bf16[2,128,128]{2,1,0:T(8,128)(2,1)S(1)} %pad_maximum_fusion.2), channel_id=1, source_target_pairs={{0,8},{2,10},{4,12},{6,14},{8,0},{10,2},{12,4},{14,6},{16,24},{18,... | collective-permute-start | bytes 196616 | tf_op jit(solution)/shard_map/ppermute | solution.py:268
  12.3 5.0 %collective-permute-start.2 = (bf16[4,128,128]{2,1,0:T(8,128)(2,1)S(1)}, bf16[4,128,128]{2,1,0:T(8,128)(2,1)S(1)}, u32[]{:S(2)}, u32[]{:S(2)}) collective-permute-start(bf16[4,128,128]{2,1,0:T(8,128)(2,1)S(1)} %pad_maximum_fusion.1), channel_id=1, source_target_pairs={{0,4},{2,6},{4,0},{6,2},{8,12},{10,14},{12,8},{14,10},{16,20},{18,... | collective-permute-start | bytes 393224 | tf_op jit(solution)/shard_map/ppermute | solution.py:268
  17.4 18.1 %copy-start.1 = (bf16[8,128,128]{2,1,0:T(8,128)(2,1)}, bf16[8,128,128]{2,1,0:T(8,128)(2,1)S(1)}, u32[]{:S(2)}) copy-start(bf16[8,128,128]{2,1,0:T(8,128)(2,1)S(1)} %pad_maximum_fusion.refs_3_) | copy-start | bytes 786436
  17.4 1.8 %copy-start.9 = (bf16[3,128]{1,0:T(4,128)(2,1)S(1)}, bf16[3,128]{1,0:T(4,128)(2,1)}, u32[]{:S(2)}) copy-start(bf16[3,128]{1,0:T(4,128)(2,1)} %param.6) | copy-start | bytes 2308
  17.4 7.6 %collective-permute-start.3 = (bf16[8,128,128]{2,1,0:T(8,128)(2,1)S(1)}, bf16[8,128,128]{2,1,0:T(8,128)(2,1)S(1)}, u32[]{:S(2)}, u32[]{:S(2)}) collective-permute-start(bf16[8,128,128]{2,1,0:T(8,128)(2,1)S(1)} %pad_maximum_fusion.refs_3_), channel_id=1, source_target_pairs={{0,1},{1,0},{2,3},{3,2},{4,5},{5,4},{6,7},{7,6},{8,9},{9,8},{10,11... | collective-permute-start | bytes 786440 | tf_op jit(solution)/shard_map/ppermute | solution.py:268
  19.2 4.5 %collective-permute-start.6 = (bf16[1,3,128]{2,1,0:T(4,128)(2,1)S(1)}, bf16[1,3,128]{2,1,0:T(4,128)(2,1)S(1)}, u32[]{:S(2)}, u32[]{:S(2)}) collective-permute-start(bf16[1,3,128]{2,1,0:T(4,128)(2,1)S(1)} %bitcast.9), channel_id=1, source_target_pairs={{0,16},{2,18},{4,20},{6,22},{8,24},{10,26},{12,28},{14,30},{16,0},... | collective-permute-start | bytes 2312 | tf_op jit(solution)/shard_map/ppermute | solution.py:268
  23.7 3.6 %collective-permute-start.7 = (bf16[2,3,128]{2,1,0:T(4,128)(2,1)S(1)}, bf16[2,3,128]{2,1,0:T(4,128)(2,1)S(1)}, u32[]{:S(2)}, u32[]{:S(2)}) collective-permute-start(bf16[2,3,128]{2,1,0:T(4,128)(2,1)S(1)} %pad_maximum_fusion.5), channel_id=1, source_target_pairs={{0,8},{2,10},{4,12},{6,14},{8,0},{10,2},{12,4},{14,6},{16,24},{18,... | collective-permute-start | bytes 4616 | tf_op jit(solution)/shard_map/ppermute | solution.py:268
  25.0 13.5 %collective-permute-start.4 = (bf16[8,128,128]{2,1,0:T(8,128)(2,1)S(1)}, bf16[8,128,128]{2,1,0:T(8,128)(2,1)S(1)}, u32[]{:S(2)}, u32[]{:S(2)}) collective-permute-start(bf16[8,128,128]{2,1,0:T(8,128)(2,1)S(1)} %pad_maximum_fusion.refs_3_), channel_id=1, source_target_pairs={{0,2},{2,0},{4,6},{6,4},{8,10},{10,8},{12,14},{14,12},{16,18},{18,... | collective-permute-start | bytes 786440 | tf_op jit(solution)/shard_map/ppermute | solution.py:268
  25.0 10.4 %copy-start.3 = (bf16[8,128,128]{2,1,0:T(8,128)(2,1)}, bf16[8,128,128]{2,1,0:T(8,128)(2,1)S(1)}, u32[]{:S(2)}) copy-start(bf16[8,128,128]{2,1,0:T(8,128)(2,1)S(1)} %collective-permute-done.3.refs_4_) | copy-start | bytes 786436
  25.0 13.5 %collective-permute-start.5 = (bf16[8,128,128]{2,1,0:T(8,128)(2,1)S(1)}, bf16[8,128,128]{2,1,0:T(8,128)(2,1)S(1)}, u32[]{:S(2)}, u32[]{:S(2)}) collective-permute-start(bf16[8,128,128]{2,1,0:T(8,128)(2,1)S(1)} %collective-permute-done.3.refs_4_), channel_id=1, source_target_pairs={{0,2},{2,0},{4,6},{6,4},{8,10},{10,8},{12,14},{14,12},{16,18},{18,... | collective-permute-start | bytes 786440 | tf_op jit(solution)/shard_map/ppermute | solution.py:268
  27.3 3.7 %collective-permute-start.8 = (bf16[4,3,128]{2,1,0:T(4,128)(2,1)S(1)}, bf16[4,3,128]{2,1,0:T(4,128)(2,1)S(1)}, u32[]{:S(2)}, u32[]{:S(2)}) collective-permute-start(bf16[4,3,128]{2,1,0:T(4,128)(2,1)S(1)} %pad_maximum_fusion.4), channel_id=1, source_target_pairs={{0,4},{2,6},{4,0},{6,2},{8,12},{10,14},{12,8},{14,10},{16,20},{18,... | collective-permute-start | bytes 9224 | tf_op jit(solution)/shard_map/ppermute | solution.py:268
  30.9 2.0 %copy-start.8 = (bf16[8,3,128]{2,1,0:T(4,128)(2,1)}, bf16[8,3,128]{2,1,0:T(4,128)(2,1)S(1)}, u32[]{:S(2)}) copy-start(bf16[8,3,128]{2,1,0:T(4,128)(2,1)S(1)} %pad_maximum_fusion.3.refs_1_) | copy-start | bytes 18436
  31.0 4.5 %collective-permute-start.9 = (bf16[8,3,128]{2,1,0:T(4,128)(2,1)S(1)}, bf16[8,3,128]{2,1,0:T(4,128)(2,1)S(1)}, u32[]{:S(2)}, u32[]{:S(2)}) collective-permute-start(bf16[8,3,128]{2,1,0:T(4,128)(2,1)S(1)} %pad_maximum_fusion.3.refs_1_), channel_id=1, source_target_pairs={{0,2},{2,0},{4,6},{6,4},{8,10},{10,8},{12,14},{14,12},{16,18},{18,... | collective-permute-start | bytes 18440 | tf_op jit(solution)/shard_map/ppermute | solution.py:268
  35.5 0.6 copy-start.10
  38.5 0.7 copy-start.4
  38.6 0.8 %copy-start.5 = (bf16[8,128,128]{2,1,0:T(8,128)(2,1)}, bf16[8,128,128]{2,1,0:T(8,128)(2,1)S(1)}, u32[]{:S(2)}) copy-start(bf16[8,128,128]{2,1,0:T(8,128)(2,1)S(1)} %collective-permute-done.5.refs_6_) | copy-start | bytes 786436
  50.7 1.8 %collective-permute-start.10 = (f32[256,256]{1,0:T(8,128)}, f32[256,256]{1,0:T(8,128)S(1)}, u32[]{:S(2)}, u32[]{:S(2)}) collective-permute-start(f32[256,256]{1,0:T(8,128)} %get-tuple-element.9.own_ref), channel_id=1, source_target_pairs={{0,2},{2,0},{4,6},{6,4},{8,10},{10,8},{12,14},{14,12},{16,18},{18,... | collective-permute-start | bytes 786440 | tf_op jit(solution)/shard_map/ppermute | solution.py:268
  52.5 0.7 copy-start.6
  62.9 6.1 %collective-permute-start.11 = (f32[264,128]{1,0:T(8,128)}, f32[264,128]{1,0:T(8,128)S(1)}, u32[]{:S(2)}, u32[]{:S(2)}) collective-permute-start(f32[264,128]{1,0:T(8,128)} %get-tuple-element.11), channel_id=1, source_target_pairs={{0,4},{2,6},{4,0},{6,2},{8,12},{10,14},{12,8},{14,10},{16,20},{18,... | collective-permute-start | bytes 405512 | tf_op jit(solution)/shard_map/ppermute | solution.py:268
  69.0 0.7 copy-start.7

commit v2 on v1

--- a/solution.py
+++ b/solution.py
@@ -6,6 +6,7 @@
 from jax.experimental import pallas as pl
 from jax.experimental.pallas import tpu as pltpu
 from jax.sharding import PartitionSpec as P
+
 
 wavenumber = 30.0
 softening = 0.02
@@ -163,44 +164,51 @@
     return full_ref[...] + jnp.concatenate([top, bottom], axis=0)
 
 
-def kernel_body(col_total, targets_ref, sources_ref, out_ref):
-    pieces, _, width = sources_ref.shape
+def kernel_body(col_total, high, targets_ref, *refs):
     m = targets_ref.shape[1]
+    width = refs[0].shape[2]
     turned = jnp.concatenate([targets_ref[...], jnp.zeros((m - 8, m), F32)], axis=0).T
     points = [jnp.broadcast_to(turned[:, c : c + 1], (m, width)) for c in range(3)]
+    count = len(refs) // 2
+    for piece_ref, out_ref in zip(refs[:count], refs[count:]):
+        for i in range(piece_ref.shape[0]):
+            source = piece_ref[i, high : high + 3, :].astype(F32)
+            first, second = kernel_values(source, points, col_total)
+            out_ref[i, 0:m, :] = first
+            out_ref[i, m : 2 * m, :] = second
+
+
+def kernel_values(source, points, col_total):
     size = 1.0 / math.sqrt(col_total)
     turns = wavenumber * 2.0 / math.pi
     h = math.pi / 2
-    for i in range(pieces):
-        source = sources_ref[i].astype(F32)
-        square = softening * softening
-        for c in range(3):
-            diff = source[c : c + 1, :] - points[c]
-            square = square + diff * diff
-        near = lax.rsqrt(square)
-        amplitude = near * size
-        quarter = (square * near) * turns
-        whole = jnp.round(quarter)
-        rest = quarter - whole
-        r2 = rest * rest
-        sine = rest * (h + r2 * (-(h**3) / 6 + r2 * (h**5 / 120 + r2 * (-(h**7) / 5040))))
-        cosine = 1.0 + r2 * (-(h**2) / 2 + r2 * (h**4 / 24 + r2 * (-(h**6) / 720 + r2 * (h**8 / 40320))))
-        count = whole.astype(jnp.int32)
-        odd = (count & 1) == 1
-        first = jnp.where(odd, sine, cosine)
-        second = jnp.where(odd, cosine, sine)
-        first = jnp.where(((count + 1) & 2) == 0, first, -first)
-        second = jnp.where((count & 2) == 0, second, -second)
-        out_ref[i, 0:m, :] = (amplitude * first).astype(BF16)
-        out_ref[i, m : 2 * m, :] = (amplitude * second).astype(BF16)
-
-
-def accumulate(probe_ref, kernel_ref, total):
+    square = softening * softening
+    for c in range(3):
+        diff = source[c : c + 1, :] - points[c]
+        square = square + diff * diff
+    near = lax.rsqrt(square)
+    amplitude = near * size
+    quarter = (square * near) * turns
+    whole = jnp.round(quarter)
+    rest = quarter - whole
+    r2 = rest * rest
+    sine = rest * (h + r2 * (-(h**3) / 6 + r2 * (h**5 / 120 + r2 * (-(h**7) / 5040))))
+    cosine = 1.0 + r2 * (-(h**2) / 2 + r2 * (h**4 / 24 + r2 * (-(h**6) / 720 + r2 * (h**8 / 40320))))
+    count = whole.astype(jnp.int32)
+    odd = (count & 1) == 1
+    first = jnp.where(odd, sine, cosine)
+    second = jnp.where(odd, cosine, sine)
+    first = jnp.where(((count + 1) & 2) == 0, first, -first)
+    second = jnp.where((count & 2) == 0, second, -second)
+    return (amplitude * first).astype(BF16), (amplitude * second).astype(BF16)
+
+
+def accumulate(probe_ref, kernel_ref, high, total):
     pieces = probe_ref.shape[0]
     both = 2 if pieces % 2 == 0 else 1
 
     def one(i, total):
-        left = jnp.concatenate([probe_ref[both * i + k] for k in range(both)], axis=1)
+        left = jnp.concatenate([probe_ref[both * i + k, 0:high, :] for k in range(both)], axis=1)
         right = jnp.concatenate([kernel_ref[both * i + k] for k in range(both)], axis=1)
         return total + mxu(left, right, NT)
 
@@ -208,16 +216,17 @@
     return lax.fori_loop(0, count, one, total, unroll=count <= 8)
 
 
-def leaf_body(blocks, place_ref, sizes_ref, ranks_ref, *refs):
-    near, far = refs[:blocks], refs[blocks : 2 * blocks]
-    near_kernel, far_kernel, h_ref, w_ref, m_ref, t_ref = refs[2 * blocks :]
+def leaf_body(groups, blocks, place_ref, sizes_ref, ranks_ref, *refs):
+    probe_refs = refs[: groups * blocks]
+    kernel_refs = refs[groups * blocks : groups * (blocks + 1)]
+    h_ref, w_ref, m_ref, t_ref = refs[groups * (blocks + 1) :]
     n = h_ref.shape[0]
     rows, cols = grids(n)
     high = n // blocks
     for o in range(blocks):
         total = jnp.zeros((high, n), F32)
-        total = accumulate(near[o], near_kernel, total)
-        total = accumulate(far[o], far_kernel, total)
+        for g in range(groups):
+            total = accumulate(probe_refs[groups * o + g], kernel_refs[g], high, total)
         at = pl.multiple_of((place_ref[0] ^ o) * high, high)
         m_ref[pl.ds(at, high), :] = total
     used = sizes_ref[0]
@@ -250,76 +259,88 @@
     z_ref[...] = (value * jnp.sqrt(shift)).T
 
 
-def call(body, name, outs, operands, specs=None, scratch=(), flops=0):
+def call(body, outs, operands, specs=None, scratch=(), flops=0):
     bytes_used = sum(x.size * x.dtype.itemsize for x in (*outs, *operands))
     return pl.pallas_call(
         body,
-        name=name,
         out_shape=list(outs),
         in_specs=list(specs or [VMEM] * len(operands)),
         out_specs=[VMEM] * len(outs),
         scratch_shapes=list(scratch),
         cost_estimate=pl.CostEstimate(flops=flops, bytes_accessed=bytes_used, transcendentals=0),
+        compiler_params=pltpu.CompilerParams(vmem_limit_bytes=2 * bytes_used + (6 << 20)),
     )(*operands)
 
 
-def flip(value, axis, mask):
-    pairs = [(source, source ^ mask) for source in range(lax.axis_size(axis))]
-    return lax.ppermute(value, axis, pairs)
+def flip(value, rows_mask, probe_mask=0):
+    probe_size = lax.axis_size("probe")
+    if probe_mask == 0:
+        pairs = [(i, i ^ rows_mask) for i in range(lax.axis_size("rows"))]
+        return lax.ppermute(value, "rows", pairs)
+    if rows_mask == 0:
+        pairs = [(i, i ^ probe_mask) for i in range(probe_size)]
+        return lax.ppermute(value, "probe", pairs)
+    pairs = [
+        (i * probe_size + j, (i ^ rows_mask) * probe_size + (j ^ probe_mask))
+        for i in range(lax.axis_size("rows"))
+        for j in range(probe_size)
+    ]
+    return lax.ppermute(value, ("rows", "probe"), pairs)
 
 
 def per_device(targets, sources, probes, cluster_sizes, leaf_ranks):
     rows_size = lax.axis_size("rows")
     probe_size = lax.axis_size("probe")
     col_total = sources.shape[1] * rows_size
-    n = probes.shape[0] * probe_size
+    high = probes.shape[0]
+    n = high * probe_size
     leaf_rows = targets.shape[1] // probe_size
     place = lax.axis_index("probe")
 
     points = lax.dynamic_slice_in_dim(targets, place * leaf_rows, leaf_rows, 1)
     points = jnp.pad(points, ((0, 8 - points.shape[0]), (0, 0)))
 
-    def evaluate(pieces):
-        out = jax.ShapeDtypeStruct((pieces.shape[0], 2 * leaf_rows, pieces.shape[2]), BF16)
+    def evaluate(arrays):
+        outs = [jax.ShapeDtypeStruct((x.shape[0], 2 * leaf_rows, x.shape[2]), BF16) for x in arrays]
         return call(
-            lambda *refs: kernel_body(col_total, *refs), "kernel_values", [out], [points, pieces],
-            flops=100 * out.size,
-        )[0]
-
+            lambda *refs: kernel_body(col_total, high, *refs), outs, [points, *arrays],
+            flops=2000 * sum(x.size for x in outs),
+        )
+
+    pieces = jnp.concatenate([probes, jnp.pad(sources, ((0, 16 - sources.shape[0]), (0, 0)))], axis=0)[None]
     mask = rows_size // 2
-    held, held_sources = probes[None], sources[None]
+    while mask > 2:
+        low = mask // 2 if mask // 2 > 2 else 0
+        received = [flip(pieces, m) for m in ([low, mask, mask + low] if low else [mask])]
+        pieces = jnp.concatenate([pieces, *received], axis=0)
+        mask //= 4 if low else 2
+    masks = [0, 2] if rows_size > 2 else [0]
     values = []
-    done = 0
-    while mask > 1:
-        more_sources = flip(held_sources, "rows", mask)
-        more = flip(held, "rows", mask)
-        held = jnp.concatenate([held, more], axis=0)
-        held_sources = jnp.concatenate([held_sources, more_sources], axis=0)
-        mask //= 2
-    near = [held]
-    far_sources = flip(held_sources, "rows", 1)
-    bit = 1
-    while bit < probe_size:
-        near += [flip(x, "probe", bit) for x in near]
-        bit *= 2
-    far = [flip(x, "rows", 1) for x in near]
-    near_kernel = evaluate(held_sources)
-    far_kernel = evaluate(far_sources)
+    groups = []
+    for o in range(probe_size):
+        both = []
+        for m in masks:
+            near = pieces if (m, o) == (0, 0) else flip(pieces, m, o)
+            far = flip(near, 1)
+            both += [near, far]
+            if o == 0:
+                values += evaluate([near, far])
+        groups.append(both)
 
     square = jax.ShapeDtypeStruct((n, n), F32)
     scratch = [pltpu.VMEM((n, n), F32)]
-    blocks = len(near)
+    flat = [x for both in groups for x in both]
     h, w, m = call(
-        lambda *refs: leaf_body(blocks, *refs), "leaf", [square] * 3,
-        [place[None], cluster_sizes, leaf_ranks, *near, *far, near_kernel, far_kernel],
-        specs=[SMEM] * 3 + [VMEM] * (2 * blocks + 2), scratch=scratch, flops=n**3,
+        lambda *refs: leaf_body(len(values), probe_size, *refs), [square] * 3,
+        [place[None], cluster_sizes, leaf_ranks, *flat, *values],
+        specs=[SMEM] * 3 + [VMEM] * (len(flat) + len(values)), scratch=scratch, flops=n**3,
     )
-    other = flip(h, "rows", 1)
-    basis = call(basis_body, "basis", [square], [w, m], flops=6 * n**3)[0]
+    other = flip(h, 1)
+    basis = call(basis_body, [square], [w, m], flops=60 * n**3)[0]
     packed = jax.ShapeDtypeStruct((n + 8, n // 2), F32)
-    h, sent = call(node_body, "node", [square, packed], [h, other], scratch=scratch, flops=n**3)
-    other = flip(sent, "rows", 2)
-    top = call(top_body, "top", [square], [h, other], scratch=scratch, flops=n**3)[0]
+    h, sent = call(node_body, [square, packed], [h, other], scratch=scratch, flops=n**3)
+    other = flip(sent, 2)
+    top = call(top_body, [square], [h, other], scratch=scratch, flops=n**3)[0]
     return (basis.reshape(n, 2, leaf_rows), top[None])
 
 

time: 79.4 us -> 56.6 us (0.71)
  Pallas kernels: 37.3 us -> 27.6 us
  starting transfers between devices: 17.1 us -> 11.2 us
  local copies, waits for them, and re-layouts: 5.16 us -> 0.85 us
  waiting for transfers between devices: 16.5 us -> 13.9 us
    pallas_call x6, Pallas kernels: 37.3 us -> 27.6 us  [call(): pl.pallas_call(body, out_shape=list(outs), in_specs=list(specs or [VMEM]...]
    ppermute x12, starting transfers between devices: 17.1 us -> 11.2 us  [the longest x10 8.22 us: flip(): return lax.ppermute(value, 'rows', pairs)]
    unnamed x22 -> x2, local copies, waits for them, and re-layouts: 2.77 us -> 0.01 us
    ppermute x12, waiting for transfers between devices: 16.5 us -> 13.9 us  [the longest x10 8.96 us: flip(): return lax.ppermute(value, 'rows', pairs)]
    reshape x1, local copies, waits for them, and re-layouts: 1.78 us -> 0.83 us  [per_device(): return (basis.reshape(n, 2, leaf_rows), top[None])]
    concatenate x6 -> x1, other arithmetic: 0.84 us -> 0.02 us  [per_device(): pieces = jnp.concatenate([pieces, *received], axis=0)]
  transfers between devices with their start and end apart: 12 -> 12, of which waited for: 8 -> 6; matrix products, arithmetic and copies ran while one was open for 3% -> 1% of each run, Pallas kernels for 9% -> 4%
where the time goes in v2:
time: 56.6 us; the launch traced here: 56.4 us
  Pallas kernels  27.6 us (49%)
  waiting for transfers between devices  13.9 us (25%)
  starting transfers between devices  11.2 us (20%)
  between operations  2.02 us (4%)
  local copies, waits for them, and re-layouts  0.85 us (2%)
  other arithmetic  0.81 us (1%)
    pallas_call x6, Pallas kernels, call(): pl.pallas_call(body, out_shape=list(outs), in_specs=list(specs or [VMEM]...  27.6 us
    ppermute x10, waiting for transfers between devices, flip(): return lax.ppermute(value, 'rows', pairs)  8.96 us
    ppermute x10, starting transfers between devices, flip(): return lax.ppermute(value, 'rows', pairs)  8.22 us
    ppermute x1, waiting for transfers between devices, flip(): return lax.ppermute(value, ('rows', 'probe'), pairs)  4.12 us
    ppermute x1, starting transfers between devices, flip(): return lax.ppermute(value, ('rows', 'probe'), pairs)  2.51 us
  transfers between devices with their start and end apart: 12, of which 6 were waited for; matrix products, arithmetic and copies ran while one was open for 1% of the time, Pallas kernels for 4%

profile of v2, /device:TPU:0, one launch (start us, length us, event | category | flops | bytes accessed | tf_op | source)
XLA Modules:
  0.0 56.4 jit_solution(3254115641724481738)
XLA Ops:
  0.6 0.0 copy-start
  0.6 0.8 %fusion.2 = bf16[1,144,128]{2,1,0:T(8,128)(2,1)S(1)} fusion(bf16[3,128]{1,0:T(4,128)(2,1)} %param.6, bf16[128,128]{1,0:T(8,128)(2,1)} %param.7), kind=kLoop, calls=%fused_computation.4 | loop fusion | flops 110592 | bytes 70400 | tf_op jit(solution)/shard_map/broadcast_in_dim | solution.py:310
  1.4 5.1 %collective-permute-start.2 = (bf16[1,144,128]{2,1,0:T(8,128)(2,1)S(1)}, bf16[1,144,128]{2,1,0:T(8,128)(2,1)S(1)}, u32[]{:S(2)}, u32[]{:S(2)}) collective-permute-start(bf16[1,144,128]{2,1,0:T(8,128)(2,1)S(1)} %fusion.2), channel_id=1, source_target_pairs={{0,24},{2,26},{4,28},{6,30},{8,16},{10,18},{12,20},{14,22},{16,8},... | collective-permute-start | bytes 110600 | tf_op jit(solution)/shard_map/ppermute | solution.py:279
  6.5 0.0 collective-permute-start.1
  6.5 0.6 %collective-permute-start = (bf16[1,144,128]{2,1,0:T(8,128)(2,1)S(1)}, bf16[1,144,128]{2,1,0:T(8,128)(2,1)S(1)}, u32[]{:S(2)}, u32[]{:S(2)}) collective-permute-start(bf16[1,144,128]{2,1,0:T(8,128)(2,1)S(1)} %fusion.2), channel_id=1, source_target_pairs={{0,8},{2,10},{4,12},{6,14},{8,0},{10,2},{12,4},{14,6},{16,24},{18,... | collective-permute-start | bytes 110600 | tf_op jit(solution)/shard_map/ppermute | solution.py:279
  7.1 1.3 %collective-permute-done.2 = bf16[1,144,128]{2,1,0:T(8,128)(2,1)S(1)} collective-permute-done((bf16[1,144,128]{2,1,0:T(8,128)(2,1)S(1)}, bf16[1,144,128]{2,1,0:T(8,128)(2,1)S(1)}, u32[]{:S(2)}, u32[]{:S(2)}) %collective-permute-start.2) | collective-permute-done | bytes 36896 | tf_op jit(solution)/shard_map/ppermute | solution.py:279
  8.4 2.9 %collective-permute-done.1 = bf16[1,144,128]{2,1,0:T(8,128)(2,1)S(1)} collective-permute-done((bf16[1,144,128]{2,1,0:T(8,128)(2,1)S(1)}, bf16[1,144,128]{2,1,0:T(8,128)(2,1)S(1)}, u32[]{:S(2)}, u32[]{:S(2)}) %collective-permute-start.1) | collective-permute-done | bytes 36896 | tf_op jit(solution)/shard_map/ppermute | solution.py:279
  11.4 0.0 collective-permute-done
  11.4 2.5 %collective-permute-start.8 = (bf16[4,144,128]{2,1,0:T(8,128)(2,1)S(1)}, bf16[4,144,128]{2,1,0:T(8,128)(2,1)S(1)}, u32[]{:S(2)}, u32[]{:S(2)}) collective-permute-start(bf16[4,144,128]{2,1,0:T(8,128)(2,1)S(1)} %pad_maximum_fusion.refs_1_.refs_3_), channel_id=1, source_target_pairs={{0,5},{1,4},{2,7},{3,6},{4,1},{5,0},{6,3},{7,2},{8,13},{9,12},{10,... | collective-permute-start | bytes 442376 | tf_op jit(solution)/shard_map/ppermute | solution.py:288
  13.9 0.5 collective-permute-start.6
  14.4 0.5 collective-permute-start.4
  15.0 0.0 collective-permute-start.3
  15.0 4.1 %collective-permute-done.8.refs_9_ = bf16[4,144,128]{2,1,0:T(8,128)(2,1)S(1)} collective-permute-done((bf16[4,144,128]{2,1,0:T(8,128)(2,1)S(1)}, bf16[4,144,128]{2,1,0:T(8,128)(2,1)S(1)}, u32[]{:S(2)}, u32[]{:S(2)}) %collective-permute-start.8) | collective-permute-done | bytes 147488 | tf_op jit(solution)/shard_map/ppermute | solution.py:288
  19.1 0.0 collective-permute-start.9
  19.1 0.8 %collective-permute-done.6.refs_7_ = bf16[4,144,128]{2,1,0:T(8,128)(2,1)S(1)} collective-permute-done((bf16[4,144,128]{2,1,0:T(8,128)(2,1)S(1)}, bf16[4,144,128]{2,1,0:T(8,128)(2,1)S(1)}, u32[]{:S(2)}, u32[]{:S(2)}) %collective-permute-start.6) | collective-permute-done | bytes 147488 | tf_op jit(solution)/shard_map/ppermute | solution.py:282
  19.9 0.0 collective-permute-start.7
  19.9 0.0 collective-permute-done.4.refs_1_.refs_5_
  19.9 0.5 collective-permute-start.5
  21.7 0.0 collective-permute-done.3.refs_2_.refs_4_
  21.7 1.0 %shard_map.68 = (bf16[4,256,128]{2,1,0:T(8,128)(2,1)S(1)}, bf16[4,256,128]{2,1,0:T(8,128)(2,1)S(1)}) custom-call(f32[8,128]{1,0:T(8,128)S(1)} %pad.9.refs_0_, bf16[4,144,128]{2,1,0:T(8,128)(2,1)S(1)} %pad_maximum_fusion.refs_1_.refs_3_, bf16[4,144,128]{2,1,0:T(8,128)(2,1)S(1)} %collective-permute-done.3.refs_2_.refs_4_), custom_call_target="tpu_custom_call" | custom-call | flops 524288000 | bytes 823296 | tf_op jit(solution)/shard_map/pallas_call | solution.py:264
  22.7 0.0 collective-permute-done.5.refs_2_.refs_6_
  22.7 1.0 %shard_map.69 = (bf16[4,256,128]{2,1,0:T(8,128)(2,1)S(1)}, bf16[4,256,128]{2,1,0:T(8,128)(2,1)S(1)}) custom-call(f32[8,128]{1,0:T(8,128)S(1)} %pad.9.refs_0_, bf16[4,144,128]{2,1,0:T(8,128)(2,1)S(1)} %collective-permute-done.4.refs_1_.refs_5_, bf16[4,144,128]{2,1,0:T(8,128)(2,1)S(1)} %collective-permute-done.5.refs_2_.refs_6_), custom_call_target="tpu_custom_call" | custom-call | flops 524288000 | bytes 823296 | tf_op jit(solution)/shard_map/pallas_call | solution.py:264
  23.7 0.0 collective-permute-done.7.refs_8_
  23.7 9.1 %shard_map.70 = (f32[256,256]{1,0:T(8,128)S(1)}, f32[256,256]{1,0:T(8,128)S(1)}, f32[256,256]{1,0:T(8,128)S(1)}) custom-call(s32[1]{0:T(128)} %bitcast.refs_0_, s32[1]{0:T(128)S(6)} %copy.7.refs_1_, s32[1]{0:T(128)S(6)} %copy.8.refs_2_, bf16[4,144,128]{2,1,0:T(8,128)(2,1)S(1)} %pad_maximum_fusion.refs_1_.refs_3_, ...), custom_call_target="tpu_custom_call" | custom-call | flops 16777216 | bytes 3014668 | tf_op jit(solution)/shard_map/pallas_call | solution.py:264
  32.8 0.1 collective-permute-start.10
  32.8 1.5 %collective-permute-done.10.other_ref = f32[256,256]{1,0:T(8,128)S(1)} collective-permute-done((f32[256,256]{1,0:T(8,128)S(1)}, f32[256,256]{1,0:T(8,128)S(1)}, u32[]{:S(2)}, u32[]{:S(2)}) %collective-permute-start.10) | collective-permute-done | bytes 262176 | tf_op jit(solution)/shard_map/ppermute | solution.py:279
  34.4 7.9 %shard_map.72 = (f32[256,256]{1,0:T(8,128)S(1)}, f32[264,128]{1,0:T(8,128)S(1)}) custom-call(f32[256,256]{1,0:T(8,128)S(1)} %get-tuple-element.17.own_ref, f32[256,256]{1,0:T(8,128)S(1)} %collective-permute-done.10.other_ref), custom_call_target="tpu_custom_call" | custom-call | flops 16777216 | bytes 921600 | tf_op jit(solution)/shard_map/pallas_call | solution.py:264
  42.3 1.4 %collective-permute-start.11 = (f32[264,128]{1,0:T(8,128)S(1)}, f32[264,128]{1,0:T(8,128)S(1)}, u32[]{:S(2)}, u32[]{:S(2)}) collective-permute-start(f32[264,128]{1,0:T(8,128)S(1)} %get-tuple-element.19), channel_id=1, source_target_pairs={{0,4},{2,6},{4,0},{6,2},{8,12},{10,14},{12,8},{14,10},{16,20},{18,... | collective-permute-start | bytes 405512 | tf_op jit(solution)/shard_map/ppermute | solution.py:279
  43.7 0.3 shard_map.71
  44.0 0.8 %reshape.7 = f32[256,2,128]{2,1,0:T(2,128)} reshape(f32[256,256]{1,0:T(8,128)S(1)} %shard_map.71) | data formatting | bytes 524288 | tf_op jit(solution)/shard_map/reshape | solution.py:344
  44.8 3.2 %collective-permute-done.11.other_ref = f32[264,128]{1,0:T(8,128)S(1)} collective-permute-done((f32[264,128]{1,0:T(8,128)S(1)}, f32[264,128]{1,0:T(8,128)S(1)}, u32[]{:S(2)}, u32[]{:S(2)}) %collective-permute-start.11) | collective-permute-done | bytes 135200 | tf_op jit(solution)/shard_map/ppermute | solution.py:279
  48.0 8.4 %shard_map.73 = f32[256,256]{1,0:T(8,128)} custom-call(f32[256,256]{1,0:T(8,128)S(1)} %get-tuple-element.18.own_ref, f32[264,128]{1,0:T(8,128)S(1)} %collective-permute-done.11.other_ref), custom_call_target="tpu_custom_call" | custom-call | flops 16777216 | bytes 659456 | tf_op jit(solution)/shard_map/pallas_call | solution.py:264
  (5 shorter events, 0.0 us)
Async XLA Ops:
  0.6 19.7 %copy-start = (f32[3,256]{1,0:T(4,128)S(1)}, f32[3,256]{1,0:T(4,128)}, u32[]{:S(2)}) copy-start(f32[3,256]{1,0:T(4,128)} %param.5) | copy-start | bytes 9220
  1.4 7.0 %collective-permute-start.2 = (bf16[1,144,128]{2,1,0:T(8,128)(2,1)S(1)}, bf16[1,144,128]{2,1,0:T(8,128)(2,1)S(1)}, u32[]{:S(2)}, u32[]{:S(2)}) collective-permute-start(bf16[1,144,128]{2,1,0:T(8,128)(2,1)S(1)} %fusion.2), channel_id=1, source_target_pairs={{0,24},{2,26},{4,28},{6,30},{8,16},{10,18},{12,20},{14,22},{16,8},... | collective-permute-start | bytes 110600 | tf_op jit(solution)/shard_map/ppermute | solution.py:279
  6.5 4.9 %collective-permute-start.1 = (bf16[1,144,128]{2,1,0:T(8,128)(2,1)S(1)}, bf16[1,144,128]{2,1,0:T(8,128)(2,1)S(1)}, u32[]{:S(2)}, u32[]{:S(2)}) collective-permute-start(bf16[1,144,128]{2,1,0:T(8,128)(2,1)S(1)} %fusion.2), channel_id=1, source_target_pairs={{0,16},{2,18},{4,20},{6,22},{8,24},{10,26},{12,28},{14,30},{16,0},... | collective-permute-start | bytes 110600 | tf_op jit(solution)/shard_map/ppermute | solution.py:279
  6.5 4.9 %collective-permute-start = (bf16[1,144,128]{2,1,0:T(8,128)(2,1)S(1)}, bf16[1,144,128]{2,1,0:T(8,128)(2,1)S(1)}, u32[]{:S(2)}, u32[]{:S(2)}) collective-permute-start(bf16[1,144,128]{2,1,0:T(8,128)(2,1)S(1)} %fusion.2), channel_id=1, source_target_pairs={{0,8},{2,10},{4,12},{6,14},{8,0},{10,2},{12,4},{14,6},{16,24},{18,... | collective-permute-start | bytes 110600 | tf_op jit(solution)/shard_map/ppermute | solution.py:279
  11.4 7.7 %collective-permute-start.8 = (bf16[4,144,128]{2,1,0:T(8,128)(2,1)S(1)}, bf16[4,144,128]{2,1,0:T(8,128)(2,1)S(1)}, u32[]{:S(2)}, u32[]{:S(2)}) collective-permute-start(bf16[4,144,128]{2,1,0:T(8,128)(2,1)S(1)} %pad_maximum_fusion.refs_1_.refs_3_), channel_id=1, source_target_pairs={{0,5},{1,4},{2,7},{3,6},{4,1},{5,0},{6,3},{7,2},{8,13},{9,12},{10,... | collective-permute-start | bytes 442376 | tf_op jit(solution)/shard_map/ppermute | solution.py:288
  13.9 6.0 %collective-permute-start.6 = (bf16[4,144,128]{2,1,0:T(8,128)(2,1)S(1)}, bf16[4,144,128]{2,1,0:T(8,128)(2,1)S(1)}, u32[]{:S(2)}, u32[]{:S(2)}) collective-permute-start(bf16[4,144,128]{2,1,0:T(8,128)(2,1)S(1)} %pad_maximum_fusion.refs_1_.refs_3_), channel_id=1, source_target_pairs={{0,1},{1,0},{2,3},{3,2},{4,5},{5,4},{6,7},{7,6},{8,9},{9,8},{10,11... | collective-permute-start | bytes 442376 | tf_op jit(solution)/shard_map/ppermute | solution.py:282
  14.4 5.4 %collective-permute-start.4 = (bf16[4,144,128]{2,1,0:T(8,128)(2,1)S(1)}, bf16[4,144,128]{2,1,0:T(8,128)(2,1)S(1)}, u32[]{:S(2)}, u32[]{:S(2)}) collective-permute-start(bf16[4,144,128]{2,1,0:T(8,128)(2,1)S(1)} %pad_maximum_fusion.refs_1_.refs_3_), channel_id=1, source_target_pairs={{0,4},{2,6},{4,0},{6,2},{8,12},{10,14},{12,8},{14,10},{16,20},{18,... | collective-permute-start | bytes 442376 | tf_op jit(solution)/shard_map/ppermute | solution.py:279
  15.0 6.7 %collective-permute-start.3 = (bf16[4,144,128]{2,1,0:T(8,128)(2,1)S(1)}, bf16[4,144,128]{2,1,0:T(8,128)(2,1)S(1)}, u32[]{:S(2)}, u32[]{:S(2)}) collective-permute-start(bf16[4,144,128]{2,1,0:T(8,128)(2,1)S(1)} %pad_maximum_fusion.refs_1_.refs_3_), channel_id=1, source_target_pairs={{0,2},{2,0},{4,6},{6,4},{8,10},{10,8},{12,14},{14,12},{16,18},{18,... | collective-permute-start | bytes 442376 | tf_op jit(solution)/shard_map/ppermute | solution.py:279
  19.1 4.6 %collective-permute-start.9 = (bf16[4,144,128]{2,1,0:T(8,128)(2,1)S(1)}, bf16[4,144,128]{2,1,0:T(8,128)(2,1)S(1)}, u32[]{:S(2)}, u32[]{:S(2)}) collective-permute-start(bf16[4,144,128]{2,1,0:T(8,128)(2,1)S(1)} %collective-permute-done.8.refs_9_), channel_id=1, source_target_pairs={{0,2},{2,0},{4,6},{6,4},{8,10},{10,8},{12,14},{14,12},{16,18},{18,... | collective-permute-start | bytes 442376 | tf_op jit(solution)/shard_map/ppermute | solution.py:279
  19.9 3.8 %collective-permute-start.7 = (bf16[4,144,128]{2,1,0:T(8,128)(2,1)S(1)}, bf16[4,144,128]{2,1,0:T(8,128)(2,1)S(1)}, u32[]{:S(2)}, u32[]{:S(2)}) collective-permute-start(bf16[4,144,128]{2,1,0:T(8,128)(2,1)S(1)} %collective-permute-done.6.refs_7_), channel_id=1, source_target_pairs={{0,2},{2,0},{4,6},{6,4},{8,10},{10,8},{12,14},{14,12},{16,18},{18,... | collective-permute-start | bytes 442376 | tf_op jit(solution)/shard_map/ppermute | solution.py:279
  19.9 2.8 %collective-permute-start.5 = (bf16[4,144,128]{2,1,0:T(8,128)(2,1)S(1)}, bf16[4,144,128]{2,1,0:T(8,128)(2,1)S(1)}, u32[]{:S(2)}, u32[]{:S(2)}) collective-permute-start(bf16[4,144,128]{2,1,0:T(8,128)(2,1)S(1)} %collective-permute-done.4.refs_1_.refs_5_), channel_id=1, source_target_pairs={{0,2},{2,0},{4,6},{6,4},{8,10},{10,8},{12,14},{14,12},{16,18},{18,... | collective-permute-start | bytes 442376 | tf_op jit(solution)/shard_map/ppermute | solution.py:279
  32.8 1.6 %collective-permute-start.10 = (f32[256,256]{1,0:T(8,128)S(1)}, f32[256,256]{1,0:T(8,128)S(1)}, u32[]{:S(2)}, u32[]{:S(2)}) collective-permute-start(f32[256,256]{1,0:T(8,128)S(1)} %get-tuple-element.17.own_ref), channel_id=1, source_target_pairs={{0,2},{2,0},{4,6},{6,4},{8,10},{10,8},{12,14},{14,12},{16,18},{18,... | collective-permute-start | bytes 786440 | tf_op jit(solution)/shard_map/ppermute | solution.py:279
  42.3 5.7 %collective-permute-start.11 = (f32[264,128]{1,0:T(8,128)S(1)}, f32[264,128]{1,0:T(8,128)S(1)}, u32[]{:S(2)}, u32[]{:S(2)}) collective-permute-start(f32[264,128]{1,0:T(8,128)S(1)} %get-tuple-element.19), channel_id=1, source_target_pairs={{0,4},{2,6},{4,0},{6,2},{8,12},{10,14},{12,8},{14,10},{16,20},{18,... | collective-permute-start | bytes 405512 | tf_op jit(solution)/shard_map/ppermute | solution.py:279

commit v3 on v2

--- a/solution.py
+++ b/solution.py
@@ -22,6 +22,7 @@
 LANES = 128
 PANEL = 32
 GROUP = 8
+CHUNK = 256
 
 
 def split_bf16(value):
@@ -66,22 +67,19 @@
         for first in range(0, PANEL, GROUP):
             i0 = first // 8
             cols = [[pick_lane(block[i][at], low + first + a) for i in range(i0, steps)] for a in range(GROUP)]
-            rows = [[pick_row(block[i0][t], a) for t in range(tiles)] for a in range(GROUP)]
             for a in range(GROUP):
                 here = lane == low + first + a
                 pivot = pick_row(cols[a][0], a)
                 inverse = 1.0 / pivot
                 along_lanes[at] = jnp.where(here, pivot, along_lanes[at])
                 pivots[i0] = jnp.where(row == a, pivot, pivots[i0])
-                swept = list(rows[a])
-                swept[at] = jnp.where(here, 2.0 * swept[at], swept[at])
                 factors = [c * inverse for c in cols[a]]
                 factors[0] = jnp.where(row > a, factors[0], 0.0)
                 for b in range(a + 1, GROUP):
                     entry = pick_row(cols[b][0], a)
-                    factor = pick_row(factors[0], b)
                     cols[b] = [c - f * entry for c, f in zip(cols[b], factors)]
-                    rows[b] = [r - factor * s for r, s in zip(rows[b], swept)]
+                swept = [pick_row(block[i0][t], a) for t in range(tiles)]
+                swept[at] = jnp.where(here, 2.0 * swept[at], swept[at])
                 for x, i in enumerate(range(i0, steps)):
                     for t in range(tiles):
                         block[i][t] = block[i][t] - factors[x] * swept[t]
@@ -91,16 +89,28 @@
         along_rows += pivots
         end = start + PANEL
         if end < n:
-            whole = t_ref[start:end, :]
             rowi = lax.broadcasted_iota(jnp.int32, (PANEL, n), 0)
             coli = lax.broadcasted_iota(jnp.int32, (PANEL, n), 1)
+            whole = jnp.concatenate([jnp.concatenate(x, axis=1) for x in block], axis=0)
             kept = jnp.where((coli < end) & (coli - start > rowi), 0.0, whole)
             scale = 1.0 / jnp.concatenate(pivots, axis=0)
-            factors = (whole * jnp.concatenate([scale] * tiles, axis=1)).T
-            colr = lax.broadcasted_iota(jnp.int32, (n - end, n), 1)
-            rest = t_ref[end:n, :]
-            rest = jnp.where((colr >= start) & (colr < end), 0.0, rest)
-            t_ref[end:n, :] = rest - dot3(factors[end:n, :], kept, NN)
+            base = end // LANES * LANES
+            factors = whole[:, base:] * jnp.concatenate([scale] * ((n - base) // LANES), axis=1)
+            fh, fl = split_bf16(factors)
+            kh, kl = split_bf16(kept)
+            left = jnp.concatenate([fh, fh, fl], axis=0)
+            left = left.T
+            right = jnp.concatenate([kh, kl, kh], axis=0)
+            for to in range(end, n, CHUNK):
+                high = min(CHUNK, n - to)
+                change = mxu(left[to - base : to - base + high, :], right, NN)
+                colr = lax.broadcasted_iota(jnp.int32, (high, LANES), 1)
+                for t in range(tiles):
+                    at_t = slice(LANES * t, LANES * (t + 1))
+                    rest = t_ref[to : to + high, at_t]
+                    if t == at:
+                        rest = jnp.where((colr >= low) & (colr < low + PANEL), 0.0, rest)
+                    t_ref[to : to + high, at_t] = rest - change[:, at_t]
     return along_lanes, along_rows
 
 
@@ -324,7 +334,8 @@
             far = flip(near, 1)
             both += [near, far]
             if o == 0:
-                values += evaluate([near, far])
+                for x in (near, far):
+                    values += evaluate([x])
         groups.append(both)
 
     square = jax.ShapeDtypeStruct((n, n), F32)

time: 56.6 us -> 54.8 us (0.968)
  Pallas kernels: 27.6 us -> 25.8 us
    pallas_call x6 -> x8, Pallas kernels: 27.6 us -> 25.8 us  [call(): pl.pallas_call(body, out_shape=list(outs), in_specs=list(specs or [VMEM]...]
  transfers between devices with their start and end apart: 12 -> 12, of which waited for: 6 -> 6; matrix products, arithmetic and copies ran while one was open for 1% -> 2% of each run, Pallas kernels for 4% -> 5%
where the time goes in v3:
time: 54.8 us; the launch traced here: 54.6 us
  Pallas kernels  25.8 us (47%)
  waiting for transfers between devices  13.9 us (25%)
  starting transfers between devices  11.2 us (20%)
  between operations  2.05 us (4%)
  local copies, waits for them, and re-layouts  0.85 us (2%)
  other arithmetic  0.81 us (1%)
    pallas_call x8, Pallas kernels, call(): pl.pallas_call(body, out_shape=list(outs), in_specs=list(specs or [VMEM]...  25.8 us
    ppermute x10, waiting for transfers between devices, flip(): return lax.ppermute(value, 'rows', pairs)  8.96 us
    ppermute x10, starting transfers between devices, flip(): return lax.ppermute(value, 'rows', pairs)  8.21 us
    ppermute x1, waiting for transfers between devices, flip(): return lax.ppermute(value, ('rows', 'probe'), pairs)  4.12 us
    ppermute x1, starting transfers between devices, flip(): return lax.ppermute(value, ('rows', 'probe'), pairs)  2.51 us
  transfers between devices with their start and end apart: 12, of which 6 were waited for; matrix products, arithmetic and copies ran while one was open for 2% of the time, Pallas kernels for 5%

profile of v3, /device:TPU:0, one launch (start us, length us, event | category | flops | bytes accessed | tf_op | source)
XLA Modules:
  0.0 54.6 jit_solution(11262023464655364486)
XLA Ops:
  0.6 0.0 copy-start
  0.6 0.8 %fusion.2 = bf16[1,144,128]{2,1,0:T(8,128)(2,1)S(1)} fusion(bf16[3,128]{1,0:T(4,128)(2,1)} %param.6, bf16[128,128]{1,0:T(8,128)(2,1)} %param.7), kind=kLoop, calls=%fused_computation.4 | loop fusion | flops 110592 | bytes 70400 | tf_op jit(solution)/shard_map/broadcast_in_dim | solution.py:320
  1.4 5.1 %collective-permute-start.2 = (bf16[1,144,128]{2,1,0:T(8,128)(2,1)S(1)}, bf16[1,144,128]{2,1,0:T(8,128)(2,1)S(1)}, u32[]{:S(2)}, u32[]{:S(2)}) collective-permute-start(bf16[1,144,128]{2,1,0:T(8,128)(2,1)S(1)} %fusion.2), channel_id=1, source_target_pairs={{0,24},{2,26},{4,28},{6,30},{8,16},{10,18},{12,20},{14,22},{16,8},... | collective-permute-start | bytes 110600 | tf_op jit(solution)/shard_map/ppermute | solution.py:289
  6.5 0.0 collective-permute-start.1
  6.5 0.6 %collective-permute-start = (bf16[1,144,128]{2,1,0:T(8,128)(2,1)S(1)}, bf16[1,144,128]{2,1,0:T(8,128)(2,1)S(1)}, u32[]{:S(2)}, u32[]{:S(2)}) collective-permute-start(bf16[1,144,128]{2,1,0:T(8,128)(2,1)S(1)} %fusion.2), channel_id=1, source_target_pairs={{0,8},{2,10},{4,12},{6,14},{8,0},{10,2},{12,4},{14,6},{16,24},{18,... | collective-permute-start | bytes 110600 | tf_op jit(solution)/shard_map/ppermute | solution.py:289
  7.1 1.3 %collective-permute-done.2 = bf16[1,144,128]{2,1,0:T(8,128)(2,1)S(1)} collective-permute-done((bf16[1,144,128]{2,1,0:T(8,128)(2,1)S(1)}, bf16[1,144,128]{2,1,0:T(8,128)(2,1)S(1)}, u32[]{:S(2)}, u32[]{:S(2)}) %collective-permute-start.2) | collective-permute-done | bytes 36896 | tf_op jit(solution)/shard_map/ppermute | solution.py:289
  8.4 2.9 %collective-permute-done.1 = bf16[1,144,128]{2,1,0:T(8,128)(2,1)S(1)} collective-permute-done((bf16[1,144,128]{2,1,0:T(8,128)(2,1)S(1)}, bf16[1,144,128]{2,1,0:T(8,128)(2,1)S(1)}, u32[]{:S(2)}, u32[]{:S(2)}) %collective-permute-start.1) | collective-permute-done | bytes 36896 | tf_op jit(solution)/shard_map/ppermute | solution.py:289
  11.4 0.0 collective-permute-done
  11.4 2.5 %collective-permute-start.8 = (bf16[4,144,128]{2,1,0:T(8,128)(2,1)S(1)}, bf16[4,144,128]{2,1,0:T(8,128)(2,1)S(1)}, u32[]{:S(2)}, u32[]{:S(2)}) collective-permute-start(bf16[4,144,128]{2,1,0:T(8,128)(2,1)S(1)} %pad_maximum_fusion.refs_1_.refs_3_), channel_id=1, source_target_pairs={{0,5},{1,4},{2,7},{3,6},{4,1},{5,0},{6,3},{7,2},{8,13},{9,12},{10,... | collective-permute-start | bytes 442376 | tf_op jit(solution)/shard_map/ppermute | solution.py:298
  13.9 0.5 collective-permute-start.6
  14.4 0.5 collective-permute-start.4
  15.0 0.0 collective-permute-start.3
  15.0 4.1 %collective-permute-done.8.refs_9_ = bf16[4,144,128]{2,1,0:T(8,128)(2,1)S(1)} collective-permute-done((bf16[4,144,128]{2,1,0:T(8,128)(2,1)S(1)}, bf16[4,144,128]{2,1,0:T(8,128)(2,1)S(1)}, u32[]{:S(2)}, u32[]{:S(2)}) %collective-permute-start.8) | collective-permute-done | bytes 147488 | tf_op jit(solution)/shard_map/ppermute | solution.py:298
  19.1 0.0 collective-permute-start.9
  19.1 0.8 %collective-permute-done.6.refs_7_ = bf16[4,144,128]{2,1,0:T(8,128)(2,1)S(1)} collective-permute-done((bf16[4,144,128]{2,1,0:T(8,128)(2,1)S(1)}, bf16[4,144,128]{2,1,0:T(8,128)(2,1)S(1)}, u32[]{:S(2)}, u32[]{:S(2)}) %collective-permute-start.6) | collective-permute-done | bytes 147488 | tf_op jit(solution)/shard_map/ppermute | solution.py:292
  19.9 0.0 collective-permute-start.7
  19.9 0.5 collective-permute-start.5
  21.7 0.6 %shard_map.68.refs_11_ = bf16[4,256,128]{2,1,0:T(8,128)(2,1)S(1)} custom-call(f32[8,128]{1,0:T(8,128)S(1)} %pad.9.refs_0_, bf16[4,144,128]{2,1,0:T(8,128)(2,1)S(1)} %pad_maximum_fusion.refs_1_.refs_3_), custom_call_target="tpu_custom_call" | custom-call | flops 262144000 | bytes 413696 | tf_op jit(solution)/shard_map/pallas_call | solution.py:274
  22.3 0.6 %shard_map.70.refs_13_ = bf16[4,256,128]{2,1,0:T(8,128)(2,1)S(1)} custom-call(f32[8,128]{1,0:T(8,128)S(1)} %pad.9.refs_0_, bf16[4,144,128]{2,1,0:T(8,128)(2,1)S(1)} %collective-permute-done.4.refs_1_.refs_5_), custom_call_target="tpu_custom_call" | custom-call | flops 262144000 | bytes 413696 | tf_op jit(solution)/shard_map/pallas_call | solution.py:274
  22.8 0.6 %shard_map.69.refs_12_ = bf16[4,256,128]{2,1,0:T(8,128)(2,1)S(1)} custom-call(f32[8,128]{1,0:T(8,128)S(1)} %pad.9.refs_0_, bf16[4,144,128]{2,1,0:T(8,128)(2,1)S(1)} %collective-permute-done.3.refs_1_.refs_4_), custom_call_target="tpu_custom_call" | custom-call | flops 262144000 | bytes 413696 | tf_op jit(solution)/shard_map/pallas_call | solution.py:274
  23.4 0.0 collective-permute-done.5.refs_1_.refs_6_
  23.4 0.6 %shard_map.71.refs_14_ = bf16[4,256,128]{2,1,0:T(8,128)(2,1)S(1)} custom-call(f32[8,128]{1,0:T(8,128)S(1)} %pad.9.refs_0_, bf16[4,144,128]{2,1,0:T(8,128)(2,1)S(1)} %collective-permute-done.5.refs_1_.refs_6_), custom_call_target="tpu_custom_call" | custom-call | flops 262144000 | bytes 413696 | tf_op jit(solution)/shard_map/pallas_call | solution.py:274
  24.0 0.0 collective-permute-done.9.refs_10_
  24.0 8.4 %shard_map.72 = (f32[256,256]{1,0:T(8,128)S(1)}, f32[256,256]{1,0:T(8,128)S(1)}, f32[256,256]{1,0:T(8,128)S(1)}) custom-call(s32[1]{0:T(128)} %bitcast.refs_0_, s32[1]{0:T(128)S(6)} %copy.7.refs_1_, s32[1]{0:T(128)S(6)} %copy.8.refs_2_, bf16[4,144,128]{2,1,0:T(8,128)(2,1)S(1)} %pad_maximum_fusion.refs_1_.refs_3_, ...), custom_call_target="tpu_custom_call" | custom-call | flops 16777216 | bytes 3014668 | tf_op jit(solution)/shard_map/pallas_call | solution.py:274
  32.4 0.1 collective-permute-start.10
  32.4 1.5 %collective-permute-done.10.other_ref = f32[256,256]{1,0:T(8,128)S(1)} collective-permute-done((f32[256,256]{1,0:T(8,128)S(1)}, f32[256,256]{1,0:T(8,128)S(1)}, u32[]{:S(2)}, u32[]{:S(2)}) %collective-permute-start.10) | collective-permute-done | bytes 262176 | tf_op jit(solution)/shard_map/ppermute | solution.py:289
  34.0 7.1 %shard_map.74 = (f32[256,256]{1,0:T(8,128)S(1)}, f32[264,128]{1,0:T(8,128)S(1)}) custom-call(f32[256,256]{1,0:T(8,128)S(1)} %get-tuple-element.9.own_ref, f32[256,256]{1,0:T(8,128)S(1)} %collective-permute-done.10.other_ref), custom_call_target="tpu_custom_call" | custom-call | flops 16777216 | bytes 921600 | tf_op jit(solution)/shard_map/pallas_call | solution.py:274
  41.0 1.4 %collective-permute-start.11 = (f32[264,128]{1,0:T(8,128)S(1)}, f32[264,128]{1,0:T(8,128)S(1)}, u32[]{:S(2)}, u32[]{:S(2)}) collective-permute-start(f32[264,128]{1,0:T(8,128)S(1)} %get-tuple-element.11), channel_id=1, source_target_pairs={{0,4},{2,6},{4,0},{6,2},{8,12},{10,14},{12,8},{14,10},{16,20},{18,... | collective-permute-start | bytes 405512 | tf_op jit(solution)/shard_map/ppermute | solution.py:289
  42.4 0.3 shard_map.73
  42.7 0.8 %reshape.7 = f32[256,2,128]{2,1,0:T(2,128)} reshape(f32[256,256]{1,0:T(8,128)S(1)} %shard_map.73) | data formatting | bytes 524288 | tf_op jit(solution)/shard_map/reshape | solution.py:355
  43.5 3.2 %collective-permute-done.11.other_ref = f32[264,128]{1,0:T(8,128)S(1)} collective-permute-done((f32[264,128]{1,0:T(8,128)S(1)}, f32[264,128]{1,0:T(8,128)S(1)}, u32[]{:S(2)}, u32[]{:S(2)}) %collective-permute-start.11) | collective-permute-done | bytes 135200 | tf_op jit(solution)/shard_map/ppermute | solution.py:289
  46.7 7.9 %shard_map.75 = f32[256,256]{1,0:T(8,128)} custom-call(f32[256,256]{1,0:T(8,128)S(1)} %get-tuple-element.10.own_ref, f32[264,128]{1,0:T(8,128)S(1)} %collective-permute-done.11.other_ref), custom_call_target="tpu_custom_call" | custom-call | flops 16777216 | bytes 659456 | tf_op jit(solution)/shard_map/pallas_call | solution.py:274
  (7 shorter events, 0.0 us)
Async XLA Ops:
  0.6 19.7 %copy-start = (f32[3,256]{1,0:T(4,128)S(1)}, f32[3,256]{1,0:T(4,128)}, u32[]{:S(2)}) copy-start(f32[3,256]{1,0:T(4,128)} %param.5) | copy-start | bytes 9220
  1.4 7.0 %collective-permute-start.2 = (bf16[1,144,128]{2,1,0:T(8,128)(2,1)S(1)}, bf16[1,144,128]{2,1,0:T(8,128)(2,1)S(1)}, u32[]{:S(2)}, u32[]{:S(2)}) collective-permute-start(bf16[1,144,128]{2,1,0:T(8,128)(2,1)S(1)} %fusion.2), channel_id=1, source_target_pairs={{0,24},{2,26},{4,28},{6,30},{8,16},{10,18},{12,20},{14,22},{16,8},... | collective-permute-start | bytes 110600 | tf_op jit(solution)/shard_map/ppermute | solution.py:289
  6.5 4.9 %collective-permute-start.1 = (bf16[1,144,128]{2,1,0:T(8,128)(2,1)S(1)}, bf16[1,144,128]{2,1,0:T(8,128)(2,1)S(1)}, u32[]{:S(2)}, u32[]{:S(2)}) collective-permute-start(bf16[1,144,128]{2,1,0:T(8,128)(2,1)S(1)} %fusion.2), channel_id=1, source_target_pairs={{0,16},{2,18},{4,20},{6,22},{8,24},{10,26},{12,28},{14,30},{16,0},... | collective-permute-start | bytes 110600 | tf_op jit(solution)/shard_map/ppermute | solution.py:289
  6.5 4.9 %collective-permute-start = (bf16[1,144,128]{2,1,0:T(8,128)(2,1)S(1)}, bf16[1,144,128]{2,1,0:T(8,128)(2,1)S(1)}, u32[]{:S(2)}, u32[]{:S(2)}) collective-permute-start(bf16[1,144,128]{2,1,0:T(8,128)(2,1)S(1)} %fusion.2), channel_id=1, source_target_pairs={{0,8},{2,10},{4,12},{6,14},{8,0},{10,2},{12,4},{14,6},{16,24},{18,... | collective-permute-start | bytes 110600 | tf_op jit(solution)/shard_map/ppermute | solution.py:289
  11.4 7.7 %collective-permute-start.8 = (bf16[4,144,128]{2,1,0:T(8,128)(2,1)S(1)}, bf16[4,144,128]{2,1,0:T(8,128)(2,1)S(1)}, u32[]{:S(2)}, u32[]{:S(2)}) collective-permute-start(bf16[4,144,128]{2,1,0:T(8,128)(2,1)S(1)} %pad_maximum_fusion.refs_1_.refs_3_), channel_id=1, source_target_pairs={{0,5},{1,4},{2,7},{3,6},{4,1},{5,0},{6,3},{7,2},{8,13},{9,12},{10,... | collective-permute-start | bytes 442376 | tf_op jit(solution)/shard_map/ppermute | solution.py:298
  13.9 6.0 %collective-permute-start.6 = (bf16[4,144,128]{2,1,0:T(8,128)(2,1)S(1)}, bf16[4,144,128]{2,1,0:T(8,128)(2,1)S(1)}, u32[]{:S(2)}, u32[]{:S(2)}) collective-permute-start(bf16[4,144,128]{2,1,0:T(8,128)(2,1)S(1)} %pad_maximum_fusion.refs_1_.refs_3_), channel_id=1, source_target_pairs={{0,1},{1,0},{2,3},{3,2},{4,5},{5,4},{6,7},{7,6},{8,9},{9,8},{10,11... | collective-permute-start | bytes 442376 | tf_op jit(solution)/shard_map/ppermute | solution.py:292
  14.4 5.4 %collective-permute-start.4 = (bf16[4,144,128]{2,1,0:T(8,128)(2,1)S(1)}, bf16[4,144,128]{2,1,0:T(8,128)(2,1)S(1)}, u32[]{:S(2)}, u32[]{:S(2)}) collective-permute-start(bf16[4,144,128]{2,1,0:T(8,128)(2,1)S(1)} %pad_maximum_fusion.refs_1_.refs_3_), channel_id=1, source_target_pairs={{0,4},{2,6},{4,0},{6,2},{8,12},{10,14},{12,8},{14,10},{16,20},{18,... | collective-permute-start | bytes 442376 | tf_op jit(solution)/shard_map/ppermute | solution.py:289
  15.0 7.9 %collective-permute-start.3 = (bf16[4,144,128]{2,1,0:T(8,128)(2,1)S(1)}, bf16[4,144,128]{2,1,0:T(8,128)(2,1)S(1)}, u32[]{:S(2)}, u32[]{:S(2)}) collective-permute-start(bf16[4,144,128]{2,1,0:T(8,128)(2,1)S(1)} %pad_maximum_fusion.refs_1_.refs_3_), channel_id=1, source_target_pairs={{0,2},{2,0},{4,6},{6,4},{8,10},{10,8},{12,14},{14,12},{16,18},{18,... | collective-permute-start | bytes 442376 | tf_op jit(solution)/shard_map/ppermute | solution.py:289
  19.1 4.9 %collective-permute-start.9 = (bf16[4,144,128]{2,1,0:T(8,128)(2,1)S(1)}, bf16[4,144,128]{2,1,0:T(8,128)(2,1)S(1)}, u32[]{:S(2)}, u32[]{:S(2)}) collective-permute-start(bf16[4,144,128]{2,1,0:T(8,128)(2,1)S(1)} %collective-permute-done.8.refs_9_), channel_id=1, source_target_pairs={{0,2},{2,0},{4,6},{6,4},{8,10},{10,8},{12,14},{14,12},{16,18},{18,... | collective-permute-start | bytes 442376 | tf_op jit(solution)/shard_map/ppermute | solution.py:289
  19.9 4.1 %collective-permute-start.7 = (bf16[4,144,128]{2,1,0:T(8,128)(2,1)S(1)}, bf16[4,144,128]{2,1,0:T(8,128)(2,1)S(1)}, u32[]{:S(2)}, u32[]{:S(2)}) collective-permute-start(bf16[4,144,128]{2,1,0:T(8,128)(2,1)S(1)} %collective-permute-done.6.refs_7_), channel_id=1, source_target_pairs={{0,2},{2,0},{4,6},{6,4},{8,10},{10,8},{12,14},{14,12},{16,18},{18,... | collective-permute-start | bytes 442376 | tf_op jit(solution)/shard_map/ppermute | solution.py:289
  19.9 3.5 %collective-permute-start.5 = (bf16[4,144,128]{2,1,0:T(8,128)(2,1)S(1)}, bf16[4,144,128]{2,1,0:T(8,128)(2,1)S(1)}, u32[]{:S(2)}, u32[]{:S(2)}) collective-permute-start(bf16[4,144,128]{2,1,0:T(8,128)(2,1)S(1)} %collective-permute-done.4.refs_1_.refs_5_), channel_id=1, source_target_pairs={{0,2},{2,0},{4,6},{6,4},{8,10},{10,8},{12,14},{14,12},{16,18},{18,... | collective-permute-start | bytes 442376 | tf_op jit(solution)/shard_map/ppermute | solution.py:289
  32.4 1.6 %collective-permute-start.10 = (f32[256,256]{1,0:T(8,128)S(1)}, f32[256,256]{1,0:T(8,128)S(1)}, u32[]{:S(2)}, u32[]{:S(2)}) collective-permute-start(f32[256,256]{1,0:T(8,128)S(1)} %get-tuple-element.9.own_ref), channel_id=1, source_target_pairs={{0,2},{2,0},{4,6},{6,4},{8,10},{10,8},{12,14},{14,12},{16,18},{18,... | collective-permute-start | bytes 786440 | tf_op jit(solution)/shard_map/ppermute | solution.py:289
  41.0 5.7 %collective-permute-start.11 = (f32[264,128]{1,0:T(8,128)S(1)}, f32[264,128]{1,0:T(8,128)S(1)}, u32[]{:S(2)}, u32[]{:S(2)}) collective-permute-start(f32[264,128]{1,0:T(8,128)S(1)} %get-tuple-element.11), channel_id=1, source_target_pairs={{0,4},{2,6},{4,0},{6,2},{8,12},{10,14},{12,8},{14,10},{16,20},{18,... | collective-permute-start | bytes 405512 | tf_op jit(solution)/shard_map/ppermute | solution.py:289

commit v4 on v3

--- a/solution.py
+++ b/solution.py
@@ -20,8 +20,7 @@
 TN = ((0,), (0,))
 
 LANES = 128
-PANEL = 32
-GROUP = 8
+PANEL = 64
 CHUNK = 256
 
 
@@ -55,7 +54,7 @@
     steps = PANEL // 8
     lane = lax.broadcasted_iota(jnp.int32, (8, LANES), 1)
     row = lax.broadcasted_iota(jnp.int32, (8, LANES), 0)
-    along_lanes = [jnp.ones((8, LANES), F32) for _ in range(tiles)]
+    along_lanes = [jnp.zeros((8, LANES), F32) for _ in range(tiles)]
     along_rows = []
     for start in range(0, n, PANEL):
         at, low = divmod(start, LANES)
@@ -64,25 +63,40 @@
             for i in range(steps)
         ]
         pivots = [jnp.zeros((8, LANES), F32) for _ in range(steps)]
-        for first in range(0, PANEL, GROUP):
-            i0 = first // 8
-            cols = [[pick_lane(block[i][at], low + first + a) for i in range(i0, steps)] for a in range(GROUP)]
-            for a in range(GROUP):
-                here = lane == low + first + a
-                pivot = pick_row(cols[a][0], a)
+        ahead = None
+        for i0 in range(steps):
+            first = low + 8 * i0
+
+            def columns(i, base):
+                return [pick_lane(block[i][at], base + a) for a in range(8)]
+
+            cols = ahead or columns(i0, first)
+            below = {i: columns(i, first) for i in range(i0 + 1, steps)}
+            after = columns(i0 + 1, first + 8) if i0 + 1 < steps else None
+            sums = [jnp.zeros((8, LANES), F32)] * 8
+            for a in range(8):
+                here = lane == first + a
+                pivot = pick_row(cols[a], a)
                 inverse = 1.0 / pivot
-                along_lanes[at] = jnp.where(here, pivot, along_lanes[at])
                 pivots[i0] = jnp.where(row == a, pivot, pivots[i0])
-                factors = [c * inverse for c in cols[a]]
-                factors[0] = jnp.where(row > a, factors[0], 0.0)
-                for b in range(a + 1, GROUP):
-                    entry = pick_row(cols[b][0], a)
-                    cols[b] = [c - f * entry for c, f in zip(cols[b], factors)]
+                factor = jnp.where(row > a, cols[a] * inverse, 0.0)
+                entries = {b: pick_row(cols[b], a) for b in range(a + 1, 8)}
+                for b in entries:
+                    cols[b] = cols[b] - factor * entries[b]
                 swept = [pick_row(block[i0][t], a) for t in range(tiles)]
                 swept[at] = jnp.where(here, 2.0 * swept[at], swept[at])
-                for x, i in enumerate(range(i0, steps)):
+                for t in range(tiles):
+                    block[i0][t] = block[i0][t] - factor * swept[t]
+                for i, mine in below.items():
+                    factor = mine[a] * inverse
+                    for b in entries:
+                        mine[b] = mine[b] - factor * entries[b]
                     for t in range(tiles):
-                        block[i][t] = block[i][t] - factors[x] * swept[t]
+                        block[i][t] = block[i][t] - factor * swept[t]
+                    if after and i == i0 + 1:
+                        sums = [x + factor * pick_row(mine[a], b) for b, x in enumerate(sums)]
+            along_lanes[at] = along_lanes[at] + jnp.where(lane == first + row, block[i0][at], 0.0)
+            ahead = after and [x - y for x, y in zip(after, sums)]
         for i in range(steps):
             for t in range(tiles):
                 t_ref[start + 8 * i : start + 8 * i + 8, LANES * t : LANES * (t + 1)] = block[i][t]
@@ -98,8 +112,7 @@
             factors = whole[:, base:] * jnp.concatenate([scale] * ((n - base) // LANES), axis=1)
             fh, fl = split_bf16(factors)
             kh, kl = split_bf16(kept)
-            left = jnp.concatenate([fh, fh, fl], axis=0)
-            left = left.T
+            left = jnp.concatenate([fh, fh, fl], axis=0).T
             right = jnp.concatenate([kh, kl, kh], axis=0)
             for to in range(end, n, CHUNK):
                 high = min(CHUNK, n - to)
@@ -127,7 +140,8 @@
     shift = jnp.sum(jnp.sum(diagonal, axis=0, keepdims=True), axis=1, keepdims=True) / n
     t_ref[...] = gram / shift + jnp.where(rows == cols, 1.0, 0.0)
     along_lanes, along_rows = sweep(t_ref)
-    by_col = jnp.concatenate([jnp.broadcast_to(x[0:1, :], (n, LANES)) for x in along_lanes], axis=1)
+    sums = [jnp.sum(x, axis=0, keepdims=True) for x in along_lanes]
+    by_col = jnp.concatenate([jnp.broadcast_to(x, (n, LANES)) for x in sums], axis=1)
     by_row = jnp.concatenate([jnp.concatenate([x] * (n // LANES), axis=1) for x in along_rows], axis=0)
     return shift, by_row, by_col
 

time: 54.8 us -> 48.8 us (0.89)
  Pallas kernels: 25.8 us -> 19.8 us
    pallas_call x8, Pallas kernels: 25.8 us -> 19.8 us  [call(): pl.pallas_call(body, out_shape=list(outs), in_specs=list(specs or [VMEM]...]
where the time goes in v4:
time: 48.8 us; the launch traced here: 48.6 us
  Pallas kernels  19.8 us (41%)
  waiting for transfers between devices  13.9 us (28%)
  starting transfers between devices  11.2 us (23%)
  between operations  2.04 us (4%)
  local copies, waits for them, and re-layouts  0.85 us (2%)
  other arithmetic  0.81 us (2%)
    pallas_call x8, Pallas kernels, call(): pl.pallas_call(body, out_shape=list(outs), in_specs=list(specs or [VMEM]...  19.8 us
    ppermute x10, waiting for transfers between devices, flip(): return lax.ppermute(value, 'rows', pairs)  8.96 us
    ppermute x10, starting transfers between devices, flip(): return lax.ppermute(value, 'rows', pairs)  8.22 us
    ppermute x1, waiting for transfers between devices, flip(): return lax.ppermute(value, ('rows', 'probe'), pairs)  4.12 us
    ppermute x1, starting transfers between devices, flip(): return lax.ppermute(value, ('rows', 'probe'), pairs)  2.51 us
  transfers between devices with their start and end apart: 12, of which 6 were waited for; matrix products, arithmetic and copies ran while one was open for 2% of the time, Pallas kernels for 5%

profile of v4, /device:TPU:0, one launch (start us, length us, event | category | flops | bytes accessed | tf_op | source)
XLA Modules:
  0.0 48.6 jit_solution(9739178231722809221)
XLA Ops:
  0.6 0.0 copy-start
  0.6 0.8 %fusion.2 = bf16[1,144,128]{2,1,0:T(8,128)(2,1)S(1)} fusion(bf16[3,128]{1,0:T(4,128)(2,1)} %param.6, bf16[128,128]{1,0:T(8,128)(2,1)} %param.7), kind=kLoop, calls=%fused_computation.4 | loop fusion | flops 110592 | bytes 70400 | tf_op jit(solution)/shard_map/broadcast_in_dim | solution.py:334
  1.4 5.1 %collective-permute-start.2 = (bf16[1,144,128]{2,1,0:T(8,128)(2,1)S(1)}, bf16[1,144,128]{2,1,0:T(8,128)(2,1)S(1)}, u32[]{:S(2)}, u32[]{:S(2)}) collective-permute-start(bf16[1,144,128]{2,1,0:T(8,128)(2,1)S(1)} %fusion.2), channel_id=1, source_target_pairs={{0,24},{2,26},{4,28},{6,30},{8,16},{10,18},{12,20},{14,22},{16,8},... | collective-permute-start | bytes 110600 | tf_op jit(solution)/shard_map/ppermute | solution.py:303
  6.5 0.0 collective-permute-start.1
  6.5 0.6 %collective-permute-start = (bf16[1,144,128]{2,1,0:T(8,128)(2,1)S(1)}, bf16[1,144,128]{2,1,0:T(8,128)(2,1)S(1)}, u32[]{:S(2)}, u32[]{:S(2)}) collective-permute-start(bf16[1,144,128]{2,1,0:T(8,128)(2,1)S(1)} %fusion.2), channel_id=1, source_target_pairs={{0,8},{2,10},{4,12},{6,14},{8,0},{10,2},{12,4},{14,6},{16,24},{18,... | collective-permute-start | bytes 110600 | tf_op jit(solution)/shard_map/ppermute | solution.py:303
  7.1 1.3 %collective-permute-done.2 = bf16[1,144,128]{2,1,0:T(8,128)(2,1)S(1)} collective-permute-done((bf16[1,144,128]{2,1,0:T(8,128)(2,1)S(1)}, bf16[1,144,128]{2,1,0:T(8,128)(2,1)S(1)}, u32[]{:S(2)}, u32[]{:S(2)}) %collective-permute-start.2) | collective-permute-done | bytes 36896 | tf_op jit(solution)/shard_map/ppermute | solution.py:303
  8.4 2.9 %collective-permute-done.1 = bf16[1,144,128]{2,1,0:T(8,128)(2,1)S(1)} collective-permute-done((bf16[1,144,128]{2,1,0:T(8,128)(2,1)S(1)}, bf16[1,144,128]{2,1,0:T(8,128)(2,1)S(1)}, u32[]{:S(2)}, u32[]{:S(2)}) %collective-permute-start.1) | collective-permute-done | bytes 36896 | tf_op jit(solution)/shard_map/ppermute | solution.py:303
  11.4 0.0 collective-permute-done
  11.4 2.5 %collective-permute-start.8 = (bf16[4,144,128]{2,1,0:T(8,128)(2,1)S(1)}, bf16[4,144,128]{2,1,0:T(8,128)(2,1)S(1)}, u32[]{:S(2)}, u32[]{:S(2)}) collective-permute-start(bf16[4,144,128]{2,1,0:T(8,128)(2,1)S(1)} %pad_maximum_fusion.refs_1_.refs_3_), channel_id=1, source_target_pairs={{0,5},{1,4},{2,7},{3,6},{4,1},{5,0},{6,3},{7,2},{8,13},{9,12},{10,... | collective-permute-start | bytes 442376 | tf_op jit(solution)/shard_map/ppermute | solution.py:312
  13.9 0.5 %collective-permute-start.6 = (bf16[4,144,128]{2,1,0:T(8,128)(2,1)S(1)}, bf16[4,144,128]{2,1,0:T(8,128)(2,1)S(1)}, u32[]{:S(2)}, u32[]{:S(2)}) collective-permute-start(bf16[4,144,128]{2,1,0:T(8,128)(2,1)S(1)} %pad_maximum_fusion.refs_1_.refs_3_), channel_id=1, source_target_pairs={{0,1},{1,0},{2,3},{3,2},{4,5},{5,4},{6,7},{7,6},{8,9},{9,8},{10,11... | collective-permute-start | bytes 442376 | tf_op jit(solution)/shard_map/ppermute | solution.py:306
  14.4 0.5 %collective-permute-start.4 = (bf16[4,144,128]{2,1,0:T(8,128)(2,1)S(1)}, bf16[4,144,128]{2,1,0:T(8,128)(2,1)S(1)}, u32[]{:S(2)}, u32[]{:S(2)}) collective-permute-start(bf16[4,144,128]{2,1,0:T(8,128)(2,1)S(1)} %pad_maximum_fusion.refs_1_.refs_3_), channel_id=1, source_target_pairs={{0,4},{2,6},{4,0},{6,2},{8,12},{10,14},{12,8},{14,10},{16,20},{18,... | collective-permute-start | bytes 442376 | tf_op jit(solution)/shard_map/ppermute | solution.py:303
  15.0 0.0 collective-permute-start.3
  15.0 4.1 %collective-permute-done.8.refs_9_ = bf16[4,144,128]{2,1,0:T(8,128)(2,1)S(1)} collective-permute-done((bf16[4,144,128]{2,1,0:T(8,128)(2,1)S(1)}, bf16[4,144,128]{2,1,0:T(8,128)(2,1)S(1)}, u32[]{:S(2)}, u32[]{:S(2)}) %collective-permute-start.8) | collective-permute-done | bytes 147488 | tf_op jit(solution)/shard_map/ppermute | solution.py:312
  19.1 0.0 collective-permute-start.9
  19.1 0.8 %collective-permute-done.6.refs_7_ = bf16[4,144,128]{2,1,0:T(8,128)(2,1)S(1)} collective-permute-done((bf16[4,144,128]{2,1,0:T(8,128)(2,1)S(1)}, bf16[4,144,128]{2,1,0:T(8,128)(2,1)S(1)}, u32[]{:S(2)}, u32[]{:S(2)}) %collective-permute-start.6) | collective-permute-done | bytes 147488 | tf_op jit(solution)/shard_map/ppermute | solution.py:306
  19.9 0.0 collective-permute-start.7
  19.9 0.5 %collective-permute-start.5 = (bf16[4,144,128]{2,1,0:T(8,128)(2,1)S(1)}, bf16[4,144,128]{2,1,0:T(8,128)(2,1)S(1)}, u32[]{:S(2)}, u32[]{:S(2)}) collective-permute-start(bf16[4,144,128]{2,1,0:T(8,128)(2,1)S(1)} %collective-permute-done.4.refs_1_.refs_5_), channel_id=1, source_target_pairs={{0,2},{2,0},{4,6},{6,4},{8,10},{10,8},{12,14},{14,12},{16,18},{18,... | collective-permute-start | bytes 442376 | tf_op jit(solution)/shard_map/ppermute | solution.py:303
  21.7 0.6 %shard_map.68.refs_11_ = bf16[4,256,128]{2,1,0:T(8,128)(2,1)S(1)} custom-call(f32[8,128]{1,0:T(8,128)S(1)} %pad.9.refs_0_, bf16[4,144,128]{2,1,0:T(8,128)(2,1)S(1)} %pad_maximum_fusion.refs_1_.refs_3_), custom_call_target="tpu_custom_call" | custom-call | flops 262144000 | bytes 413696 | tf_op jit(solution)/shard_map/pallas_call | solution.py:288
  22.3 0.6 %shard_map.70.refs_13_ = bf16[4,256,128]{2,1,0:T(8,128)(2,1)S(1)} custom-call(f32[8,128]{1,0:T(8,128)S(1)} %pad.9.refs_0_, bf16[4,144,128]{2,1,0:T(8,128)(2,1)S(1)} %collective-permute-done.4.refs_1_.refs_5_), custom_call_target="tpu_custom_call" | custom-call | flops 262144000 | bytes 413696 | tf_op jit(solution)/shard_map/pallas_call | solution.py:288
  22.8 0.6 %shard_map.69.refs_12_ = bf16[4,256,128]{2,1,0:T(8,128)(2,1)S(1)} custom-call(f32[8,128]{1,0:T(8,128)S(1)} %pad.9.refs_0_, bf16[4,144,128]{2,1,0:T(8,128)(2,1)S(1)} %collective-permute-done.3.refs_1_.refs_4_), custom_call_target="tpu_custom_call" | custom-call | flops 262144000 | bytes 413696 | tf_op jit(solution)/shard_map/pallas_call | solution.py:288
  23.4 0.0 collective-permute-done.5.refs_1_.refs_6_
  23.4 0.6 %shard_map.71.refs_14_ = bf16[4,256,128]{2,1,0:T(8,128)(2,1)S(1)} custom-call(f32[8,128]{1,0:T(8,128)S(1)} %pad.9.refs_0_, bf16[4,144,128]{2,1,0:T(8,128)(2,1)S(1)} %collective-permute-done.5.refs_1_.refs_6_), custom_call_target="tpu_custom_call" | custom-call | flops 262144000 | bytes 413696 | tf_op jit(solution)/shard_map/pallas_call | solution.py:288
  24.0 0.0 collective-permute-done.9.refs_10_
  24.0 6.4 %shard_map.72 = (f32[256,256]{1,0:T(8,128)S(1)}, f32[256,256]{1,0:T(8,128)S(1)}, f32[256,256]{1,0:T(8,128)S(1)}) custom-call(s32[1]{0:T(128)} %bitcast.refs_0_, s32[1]{0:T(128)S(6)} %copy.7.refs_1_, s32[1]{0:T(128)S(6)} %copy.8.refs_2_, bf16[4,144,128]{2,1,0:T(8,128)(2,1)S(1)} %pad_maximum_fusion.refs_1_.refs_3_, ...), custom_call_target="tpu_custom_call" | custom-call | flops 16777216 | bytes 3014668 | tf_op jit(solution)/shard_map/pallas_call | solution.py:288
  30.3 0.1 collective-permute-start.10
  30.4 1.5 %collective-permute-done.10.other_ref = f32[256,256]{1,0:T(8,128)S(1)} collective-permute-done((f32[256,256]{1,0:T(8,128)S(1)}, f32[256,256]{1,0:T(8,128)S(1)}, u32[]{:S(2)}, u32[]{:S(2)}) %collective-permute-start.10) | collective-permute-done | bytes 262176 | tf_op jit(solution)/shard_map/ppermute | solution.py:303
  31.9 5.3 %shard_map.74 = (f32[256,256]{1,0:T(8,128)S(1)}, f32[264,128]{1,0:T(8,128)S(1)}) custom-call(f32[256,256]{1,0:T(8,128)S(1)} %get-tuple-element.9.own_ref, f32[256,256]{1,0:T(8,128)S(1)} %collective-permute-done.10.other_ref), custom_call_target="tpu_custom_call" | custom-call | flops 16777216 | bytes 921600 | tf_op jit(solution)/shard_map/pallas_call | solution.py:288
  37.2 1.4 %collective-permute-start.11 = (f32[264,128]{1,0:T(8,128)S(1)}, f32[264,128]{1,0:T(8,128)S(1)}, u32[]{:S(2)}, u32[]{:S(2)}) collective-permute-start(f32[264,128]{1,0:T(8,128)S(1)} %get-tuple-element.11), channel_id=1, source_target_pairs={{0,4},{2,6},{4,0},{6,2},{8,12},{10,14},{12,8},{14,10},{16,20},{18,... | collective-permute-start | bytes 405512 | tf_op jit(solution)/shard_map/ppermute | solution.py:303
  38.6 0.3 shard_map.73
  38.9 0.8 %reshape.7 = f32[256,2,128]{2,1,0:T(2,128)} reshape(f32[256,256]{1,0:T(8,128)S(1)} %shard_map.73) | data formatting | bytes 524288 | tf_op jit(solution)/shard_map/reshape | solution.py:369
  39.7 3.2 %collective-permute-done.11.other_ref = f32[264,128]{1,0:T(8,128)S(1)} collective-permute-done((f32[264,128]{1,0:T(8,128)S(1)}, f32[264,128]{1,0:T(8,128)S(1)}, u32[]{:S(2)}, u32[]{:S(2)}) %collective-permute-start.11) | collective-permute-done | bytes 135200 | tf_op jit(solution)/shard_map/ppermute | solution.py:303
  42.9 5.7 %shard_map.75 = f32[256,256]{1,0:T(8,128)} custom-call(f32[256,256]{1,0:T(8,128)S(1)} %get-tuple-element.10.own_ref, f32[264,128]{1,0:T(8,128)S(1)} %collective-permute-done.11.other_ref), custom_call_target="tpu_custom_call" | custom-call | flops 16777216 | bytes 659456 | tf_op jit(solution)/shard_map/pallas_call | solution.py:288
  (7 shorter events, 0.0 us)
Async XLA Ops:
  0.6 19.7 %copy-start = (f32[3,256]{1,0:T(4,128)S(1)}, f32[3,256]{1,0:T(4,128)}, u32[]{:S(2)}) copy-start(f32[3,256]{1,0:T(4,128)} %param.5) | copy-start | bytes 9220
  1.4 7.0 %collective-permute-start.2 = (bf16[1,144,128]{2,1,0:T(8,128)(2,1)S(1)}, bf16[1,144,128]{2,1,0:T(8,128)(2,1)S(1)}, u32[]{:S(2)}, u32[]{:S(2)}) collective-permute-start(bf16[1,144,128]{2,1,0:T(8,128)(2,1)S(1)} %fusion.2), channel_id=1, source_target_pairs={{0,24},{2,26},{4,28},{6,30},{8,16},{10,18},{12,20},{14,22},{16,8},... | collective-permute-start | bytes 110600 | tf_op jit(solution)/shard_map/ppermute | solution.py:303
  6.5 4.9 %collective-permute-start.1 = (bf16[1,144,128]{2,1,0:T(8,128)(2,1)S(1)}, bf16[1,144,128]{2,1,0:T(8,128)(2,1)S(1)}, u32[]{:S(2)}, u32[]{:S(2)}) collective-permute-start(bf16[1,144,128]{2,1,0:T(8,128)(2,1)S(1)} %fusion.2), channel_id=1, source_target_pairs={{0,16},{2,18},{4,20},{6,22},{8,24},{10,26},{12,28},{14,30},{16,0},... | collective-permute-start | bytes 110600 | tf_op jit(solution)/shard_map/ppermute | solution.py:303
  6.5 4.9 %collective-permute-start = (bf16[1,144,128]{2,1,0:T(8,128)(2,1)S(1)}, bf16[1,144,128]{2,1,0:T(8,128)(2,1)S(1)}, u32[]{:S(2)}, u32[]{:S(2)}) collective-permute-start(bf16[1,144,128]{2,1,0:T(8,128)(2,1)S(1)} %fusion.2), channel_id=1, source_target_pairs={{0,8},{2,10},{4,12},{6,14},{8,0},{10,2},{12,4},{14,6},{16,24},{18,... | collective-permute-start | bytes 110600 | tf_op jit(solution)/shard_map/ppermute | solution.py:303
  11.4 7.7 %collective-permute-start.8 = (bf16[4,144,128]{2,1,0:T(8,128)(2,1)S(1)}, bf16[4,144,128]{2,1,0:T(8,128)(2,1)S(1)}, u32[]{:S(2)}, u32[]{:S(2)}) collective-permute-start(bf16[4,144,128]{2,1,0:T(8,128)(2,1)S(1)} %pad_maximum_fusion.refs_1_.refs_3_), channel_id=1, source_target_pairs={{0,5},{1,4},{2,7},{3,6},{4,1},{5,0},{6,3},{7,2},{8,13},{9,12},{10,... | collective-permute-start | bytes 442376 | tf_op jit(solution)/shard_map/ppermute | solution.py:312
  13.9 6.0 %collective-permute-start.6 = (bf16[4,144,128]{2,1,0:T(8,128)(2,1)S(1)}, bf16[4,144,128]{2,1,0:T(8,128)(2,1)S(1)}, u32[]{:S(2)}, u32[]{:S(2)}) collective-permute-start(bf16[4,144,128]{2,1,0:T(8,128)(2,1)S(1)} %pad_maximum_fusion.refs_1_.refs_3_), channel_id=1, source_target_pairs={{0,1},{1,0},{2,3},{3,2},{4,5},{5,4},{6,7},{7,6},{8,9},{9,8},{10,11... | collective-permute-start | bytes 442376 | tf_op jit(solution)/shard_map/ppermute | solution.py:306
  14.4 5.4 %collective-permute-start.4 = (bf16[4,144,128]{2,1,0:T(8,128)(2,1)S(1)}, bf16[4,144,128]{2,1,0:T(8,128)(2,1)S(1)}, u32[]{:S(2)}, u32[]{:S(2)}) collective-permute-start(bf16[4,144,128]{2,1,0:T(8,128)(2,1)S(1)} %pad_maximum_fusion.refs_1_.refs_3_), channel_id=1, source_target_pairs={{0,4},{2,6},{4,0},{6,2},{8,12},{10,14},{12,8},{14,10},{16,20},{18,... | collective-permute-start | bytes 442376 | tf_op jit(solution)/shard_map/ppermute | solution.py:303
  15.0 7.9 %collective-permute-start.3 = (bf16[4,144,128]{2,1,0:T(8,128)(2,1)S(1)}, bf16[4,144,128]{2,1,0:T(8,128)(2,1)S(1)}, u32[]{:S(2)}, u32[]{:S(2)}) collective-permute-start(bf16[4,144,128]{2,1,0:T(8,128)(2,1)S(1)} %pad_maximum_fusion.refs_1_.refs_3_), channel_id=1, source_target_pairs={{0,2},{2,0},{4,6},{6,4},{8,10},{10,8},{12,14},{14,12},{16,18},{18,... | collective-permute-start | bytes 442376 | tf_op jit(solution)/shard_map/ppermute | solution.py:303
  19.1 4.9 %collective-permute-start.9 = (bf16[4,144,128]{2,1,0:T(8,128)(2,1)S(1)}, bf16[4,144,128]{2,1,0:T(8,128)(2,1)S(1)}, u32[]{:S(2)}, u32[]{:S(2)}) collective-permute-start(bf16[4,144,128]{2,1,0:T(8,128)(2,1)S(1)} %collective-permute-done.8.refs_9_), channel_id=1, source_target_pairs={{0,2},{2,0},{4,6},{6,4},{8,10},{10,8},{12,14},{14,12},{16,18},{18,... | collective-permute-start | bytes 442376 | tf_op jit(solution)/shard_map/ppermute | solution.py:303
  19.9 4.1 %collective-permute-start.7 = (bf16[4,144,128]{2,1,0:T(8,128)(2,1)S(1)}, bf16[4,144,128]{2,1,0:T(8,128)(2,1)S(1)}, u32[]{:S(2)}, u32[]{:S(2)}) collective-permute-start(bf16[4,144,128]{2,1,0:T(8,128)(2,1)S(1)} %collective-permute-done.6.refs_7_), channel_id=1, source_target_pairs={{0,2},{2,0},{4,6},{6,4},{8,10},{10,8},{12,14},{14,12},{16,18},{18,... | collective-permute-start | bytes 442376 | tf_op jit(solution)/shard_map/ppermute | solution.py:303
  19.9 3.5 %collective-permute-start.5 = (bf16[4,144,128]{2,1,0:T(8,128)(2,1)S(1)}, bf16[4,144,128]{2,1,0:T(8,128)(2,1)S(1)}, u32[]{:S(2)}, u32[]{:S(2)}) collective-permute-start(bf16[4,144,128]{2,1,0:T(8,128)(2,1)S(1)} %collective-permute-done.4.refs_1_.refs_5_), channel_id=1, source_target_pairs={{0,2},{2,0},{4,6},{6,4},{8,10},{10,8},{12,14},{14,12},{16,18},{18,... | collective-permute-start | bytes 442376 | tf_op jit(solution)/shard_map/ppermute | solution.py:303
  30.3 1.6 %collective-permute-start.10 = (f32[256,256]{1,0:T(8,128)S(1)}, f32[256,256]{1,0:T(8,128)S(1)}, u32[]{:S(2)}, u32[]{:S(2)}) collective-permute-start(f32[256,256]{1,0:T(8,128)S(1)} %get-tuple-element.9.own_ref), channel_id=1, source_target_pairs={{0,2},{2,0},{4,6},{6,4},{8,10},{10,8},{12,14},{14,12},{16,18},{18,... | collective-permute-start | bytes 786440 | tf_op jit(solution)/shard_map/ppermute | solution.py:303
  37.2 5.7 %collective-permute-start.11 = (f32[264,128]{1,0:T(8,128)S(1)}, f32[264,128]{1,0:T(8,128)S(1)}, u32[]{:S(2)}, u32[]{:S(2)}) collective-permute-start(f32[264,128]{1,0:T(8,128)S(1)} %get-tuple-element.11), channel_id=1, source_target_pairs={{0,4},{2,6},{4,0},{6,2},{8,12},{10,14},{12,8},{14,10},{16,20},{18,... | collective-permute-start | bytes 405512 | tf_op jit(solution)/shard_map/ppermute | solution.py:303

commit v5 on v4

--- a/solution.py
+++ b/solution.py
@@ -17,7 +17,6 @@
 SMEM = pl.BlockSpec(memory_space=pltpu.SMEM)
 NN = ((1,), (0,))
 NT = ((1,), (1,))
-TN = ((0,), (0,))
 
 LANES = 128
 PANEL = 64
@@ -37,6 +36,14 @@
     lh, ll = split_bf16(left)
     rh, rl = split_bf16(right)
     return mxu(lh, rh, dims) + (mxu(lh, rl, dims) + mxu(ll, rh, dims))
+
+
+def rows_gram(value):
+    n = value.shape[1]
+    high, low = split_bf16(value)
+    turned = jnp.concatenate([high, low], axis=1).T
+    first = mxu(turned, high, NN)
+    return first[:n] + (first[n:] + mxu(turned[:n], low, NN))
 
 
 def pick_lane(tile, lane):
@@ -154,12 +161,6 @@
     )
 
 
-def inverse_factor(t_ref, by_row, by_col):
-    rows, cols = grids(t_ref.shape[0])
-    held = t_ref[...]
-    return lax.rsqrt(by_row) * jnp.where(rows > cols, held / by_col, jnp.where(rows == cols, 1.0, 0.0))
-
-
 def fold(full_ref, packed_ref):
     n = full_ref.shape[0]
     half = n // 2
@@ -240,17 +241,24 @@
     return lax.fori_loop(0, count, one, total, unroll=count <= 8)
 
 
-def leaf_body(groups, blocks, place_ref, sizes_ref, ranks_ref, *refs):
-    probe_refs = refs[: groups * blocks]
-    kernel_refs = refs[groups * blocks : groups * (blocks + 1)]
-    h_ref, w_ref, m_ref, t_ref = refs[groups * (blocks + 1) :]
+def sample_body(groups, *refs):
+    out_ref = refs[-1]
+    high, n = out_ref.shape
+    total = jnp.zeros((high, n), F32)
+    for g in range(groups):
+        total = accumulate(refs[g], refs[groups + g], high, total)
+    out_ref[...] = total
+
+
+def leaf_body(blocks, place_ref, sizes_ref, ranks_ref, probe_ref, kernel_ref, *refs):
+    h_ref, m_ref, t_ref = refs[blocks:]
     n = h_ref.shape[0]
     rows, cols = grids(n)
     high = n // blocks
     for o in range(blocks):
-        total = jnp.zeros((high, n), F32)
-        for g in range(groups):
-            total = accumulate(probe_refs[groups * o + g], kernel_refs[g], high, total)
+        total = refs[o][...]
+        if o == blocks - 1:
+            total = accumulate(probe_ref, kernel_ref, high, total)
         at = pl.multiple_of((place_ref[0] ^ o) * high, high)
         m_ref[pl.ds(at, high), :] = total
     used = sizes_ref[0]
@@ -258,22 +266,30 @@
     inside = cols - jnp.where(cols >= half, half, 0) < used
     matrix = jnp.where(inside, m_ref[...], 0.0)
     m_ref[...] = matrix
-    gram = dot3(matrix, matrix, NT)
-    shift, by_row, by_col = factorize(gram, t_ref)
+    shift, by_row, by_col = factorize(dot3(matrix, matrix, NT), t_ref)
     in_rank = rows < ranks_ref[0]
     value = jnp.where(in_rank, projected_rows(t_ref, by_row, by_col), 0.0)
-    h_ref[...] = dot3(value, value, TN) * shift
-    w_ref[...] = jnp.where(in_rank, inverse_factor(t_ref, by_row, by_col) * lax.rsqrt(shift), 0.0)
-
-
-def basis_body(w_ref, m_ref, b_ref):
-    b_ref[...] = dot3(w_ref[...], m_ref[...], NN)
+    h_ref[...] = rows_gram(value) * shift
+
+
+def basis_body(ranks_ref, t_ref, m_ref, b_ref):
+    n = t_ref.shape[0]
+    rows, cols = grids(n)
+    held = t_ref[...]
+    matrix = m_ref[...]
+    shift = jnp.sum(jnp.sum(matrix * matrix, axis=0, keepdims=True), axis=1, keepdims=True) / n
+    diagonal = jnp.where(rows == cols, held, 0.0)
+    by_row = jnp.sum(diagonal, axis=1, keepdims=True)
+    by_col = jnp.sum(diagonal, axis=0, keepdims=True)
+    inverse = jnp.where(rows > cols, held / by_col, jnp.where(rows == cols, 1.0, 0.0))
+    scale = jnp.where(rows < ranks_ref[0], lax.rsqrt(by_row * shift), 0.0)
+    b_ref[...] = dot3(inverse * scale, matrix, NN)
 
 
 def node_body(own_ref, other_ref, h_ref, packed_ref, t_ref):
     shift, by_row, by_col = factorize(own_ref[...] + other_ref[...], t_ref)
     value = projected_rows(t_ref, by_row, by_col)
-    h_ref[...] = dot3(value, value, TN) * shift
+    h_ref[...] = rows_gram(value) * shift
     fold(h_ref, packed_ref)
 
 
@@ -339,29 +355,33 @@
         pieces = jnp.concatenate([pieces, *received], axis=0)
         mask //= 4 if low else 2
     masks = [0, 2] if rows_size > 2 else [0]
+    probes_only = pieces[:, :high]
+    square = jax.ShapeDtypeStruct((n, n), F32)
+    block = jax.ShapeDtypeStruct((high, n), F32)
     values = []
-    groups = []
+    samples = []
     for o in range(probe_size):
-        both = []
+        held = []
         for m in masks:
-            near = pieces if (m, o) == (0, 0) else flip(pieces, m, o)
+            near = pieces if (m, o) == (0, 0) else flip(probes_only if o else pieces, m, o)
             far = flip(near, 1)
-            both += [near, far]
+            held += [near, far]
             if o == 0:
                 for x in (near, far):
                     values += evaluate([x])
-        groups.append(both)
-
-    square = jax.ShapeDtypeStruct((n, n), F32)
+        count = len(held) - (o == probe_size - 1)
+        samples += call(
+            lambda *refs, count=count: sample_body(count, *refs), [block],
+            [*held[:count], *values[:count]], flops=200 * high * n * n,
+        )
     scratch = [pltpu.VMEM((n, n), F32)]
-    flat = [x for both in groups for x in both]
-    h, w, m = call(
-        lambda *refs: leaf_body(len(values), probe_size, *refs), [square] * 3,
-        [place[None], cluster_sizes, leaf_ranks, *flat, *values],
-        specs=[SMEM] * 3 + [VMEM] * (len(flat) + len(values)), scratch=scratch, flops=n**3,
+    h, m, t = call(
+        lambda *refs: leaf_body(probe_size, *refs), [square] * 3,
+        [place[None], cluster_sizes, leaf_ranks, held[-1], values[-1], *samples],
+        specs=[SMEM] * 3 + [VMEM] * (2 + len(samples)), flops=n**3,
     )
     other = flip(h, 1)
-    basis = call(basis_body, [square], [w, m], flops=60 * n**3)[0]
+    basis = call(basis_body, [square], [leaf_ranks, t, m], specs=[SMEM, VMEM, VMEM], flops=60 * n**3)[0]
     packed = jax.ShapeDtypeStruct((n + 8, n // 2), F32)
     h, sent = call(node_body, [square, packed], [h, other], scratch=scratch, flops=n**3)
     other = flip(sent, 2)

time: 48.8 us -> 51.6 us (1.057)
  waiting for transfers between devices: 13.9 us -> 16.7 us
  starting transfers between devices: 11.2 us -> 10.6 us
  Pallas kernels: 19.8 us -> 20.4 us
    ppermute x10, waiting for transfers between devices: 8.96 us -> 11.1 us  [flip(): return lax.ppermute(value, 'rows', pairs)]
    ppermute x1, starting transfers between devices: 2.51 us -> 0.54 us  [flip(): return lax.ppermute(value, ('rows', 'probe'), pairs)]
    ppermute x1, waiting for transfers between devices: 4.12 us -> 5.52 us  [flip(): return lax.ppermute(value, ('rows', 'probe'), pairs)]
    ppermute x1, starting transfers between devices: 0.51 us -> 1.58 us  [flip(): return lax.ppermute(value, 'probe', pairs)]
    ppermute x1, waiting for transfers between devices: 0.78 us -> 0.04 us  [flip(): return lax.ppermute(value, 'probe', pairs)]
    pallas_call x8 -> x10, Pallas kernels: 19.8 us -> 20.4 us  [call(): pl.pallas_call(body, out_shape=list(outs), in_specs=list(specs or [VMEM]...]
  transfers between devices with their start and end apart: 12 -> 12, of which waited for: 6 -> 5; matrix products, arithmetic and copies ran while one was open for 2% -> 2% of each run, Pallas kernels for 5% -> 7%
where the time goes in v5:
time: 51.6 us; the launch traced here: 51.4 us
  Pallas kernels  20.4 us (40%)
  waiting for transfers between devices  16.7 us (32%)
  starting transfers between devices  10.6 us (21%)
  between operations  2.07 us (4%)
  local copies, waits for them, and re-layouts  0.86 us (2%)
  other arithmetic  0.81 us (2%)
    pallas_call x10, Pallas kernels, call(): pl.pallas_call(body, out_shape=list(outs), in_specs=list(specs or [VMEM]...  20.4 us
    ppermute x10, waiting for transfers between devices, flip(): return lax.ppermute(value, 'rows', pairs)  11.1 us
    ppermute x10, starting transfers between devices, flip(): return lax.ppermute(value, 'rows', pairs)  8.49 us
    ppermute x1, waiting for transfers between devices, flip(): return lax.ppermute(value, ('rows', 'probe'), pairs)  5.52 us
    ppermute x1, starting transfers between devices, flip(): return lax.ppermute(value, 'probe', pairs)  1.58 us
  transfers between devices with their start and end apart: 12, of which 5 were waited for; matrix products, arithmetic and copies ran while one was open for 2% of the time, Pallas kernels for 7%

profile of v5, /device:TPU:0, one launch (start us, length us, event | category | flops | bytes accessed | tf_op | source)
XLA Modules:
  0.0 51.4 jit_solution(9568430996723479226)
XLA Ops:
  0.6 0.0 copy-start
  0.6 0.8 %fusion.2 = bf16[1,144,128]{2,1,0:T(8,128)(2,1)S(1)} fusion(bf16[3,128]{1,0:T(4,128)(2,1)} %param.6, bf16[128,128]{1,0:T(8,128)(2,1)} %param.7), kind=kLoop, calls=%fused_computation.4 | loop fusion | flops 110592 | bytes 70400 | tf_op jit(solution)/shard_map/broadcast_in_dim | solution.py:350
  1.4 3.1 %collective-permute-start = (bf16[1,144,128]{2,1,0:T(8,128)(2,1)S(1)}, bf16[1,144,128]{2,1,0:T(8,128)(2,1)S(1)}, u32[]{:S(2)}, u32[]{:S(2)}) collective-permute-start(bf16[1,144,128]{2,1,0:T(8,128)(2,1)S(1)} %fusion.2), channel_id=1, source_target_pairs={{0,8},{2,10},{4,12},{6,14},{8,0},{10,2},{12,4},{14,6},{16,24},{18,... | collective-permute-start | bytes 110600 | tf_op jit(solution)/shard_map/ppermute | solution.py:319
  4.5 2.6 %collective-permute-start.1 = (bf16[1,144,128]{2,1,0:T(8,128)(2,1)S(1)}, bf16[1,144,128]{2,1,0:T(8,128)(2,1)S(1)}, u32[]{:S(2)}, u32[]{:S(2)}) collective-permute-start(bf16[1,144,128]{2,1,0:T(8,128)(2,1)S(1)} %fusion.2), channel_id=1, source_target_pairs={{0,16},{2,18},{4,20},{6,22},{8,24},{10,26},{12,28},{14,30},{16,0},... | collective-permute-start | bytes 110600 | tf_op jit(solution)/shard_map/ppermute | solution.py:319
  7.1 0.0 collective-permute-start.2
  7.1 0.0 collective-permute-done
  7.1 2.9 %collective-permute-done.1 = bf16[1,144,128]{2,1,0:T(8,128)(2,1)S(1)} collective-permute-done((bf16[1,144,128]{2,1,0:T(8,128)(2,1)S(1)}, bf16[1,144,128]{2,1,0:T(8,128)(2,1)S(1)}, u32[]{:S(2)}, u32[]{:S(2)}) %collective-permute-start.1) | collective-permute-done | bytes 36896 | tf_op jit(solution)/shard_map/ppermute | solution.py:319
  10.0 2.8 %collective-permute-done.2 = bf16[1,144,128]{2,1,0:T(8,128)(2,1)S(1)} collective-permute-done((bf16[1,144,128]{2,1,0:T(8,128)(2,1)S(1)}, bf16[1,144,128]{2,1,0:T(8,128)(2,1)S(1)}, u32[]{:S(2)}, u32[]{:S(2)}) %collective-permute-start.2) | collective-permute-done | bytes 36896 | tf_op jit(solution)/shard_map/ppermute | solution.py:319
  12.9 1.6 %collective-permute-start.8 = (bf16[4,128,128]{2,1,0:T(8,128)(2,1)S(1)}, bf16[4,128,128]{2,1,0:T(8,128)(2,1)S(1)}, u32[]{:S(2)}, u32[]{:S(2)}) collective-permute-start(bf16[4,128,128]{2,1,0:T(8,128)(2,1)S(1)} %slice.4), channel_id=1, source_target_pairs={{0,1},{1,0},{2,3},{3,2},{4,5},{5,4},{6,7},{7,6},{8,9},{9,8},{10,11... | collective-permute-start | bytes 393224 | tf_op jit(solution)/shard_map/ppermute | solution.py:322
  14.5 1.5 %collective-permute-start.5 = (bf16[4,144,128]{2,1,0:T(8,128)(2,1)S(1)}, bf16[4,144,128]{2,1,0:T(8,128)(2,1)S(1)}, u32[]{:S(2)}, u32[]{:S(2)}) collective-permute-start(bf16[4,144,128]{2,1,0:T(8,128)(2,1)S(1)} %pad_maximum_fusion.refs_1_.refs_0_), channel_id=1, source_target_pairs={{0,4},{2,6},{4,0},{6,2},{8,12},{10,14},{12,8},{14,10},{16,20},{18,... | collective-permute-start | bytes 442376 | tf_op jit(solution)/shard_map/ppermute | solution.py:319
  17.2 0.1 collective-permute-start.7
  17.3 0.5 %collective-permute-start.3 = (bf16[4,128,128]{2,1,0:T(8,128)(2,1)S(1)}, bf16[4,128,128]{2,1,0:T(8,128)(2,1)S(1)}, u32[]{:S(2)}, u32[]{:S(2)}) collective-permute-start(bf16[4,128,128]{2,1,0:T(8,128)(2,1)S(1)} %slice.4), channel_id=1, source_target_pairs={{0,5},{1,4},{2,7},{3,6},{4,1},{5,0},{6,3},{7,2},{8,13},{9,12},{10,... | collective-permute-start | bytes 393224 | tf_op jit(solution)/shard_map/ppermute | solution.py:328
  17.9 0.0 collective-permute-done.8.refs_0_
  17.9 0.1 collective-permute-start.9
  18.0 0.6 %shard_map.69.refs_4_.refs_3_ = bf16[4,256,128]{2,1,0:T(8,128)(2,1)S(1)} custom-call(f32[8,128]{1,0:T(8,128)S(1)} %pad.9.refs_0_, bf16[4,144,128]{2,1,0:T(8,128)(2,1)S(1)} %pad_maximum_fusion.refs_1_.refs_0_), custom_call_target="tpu_custom_call" | custom-call | flops 262144000 | bytes 413696 | tf_op jit(solution)/shard_map/pallas_call | solution.py:304
  18.6 5.5 %collective-permute-done.3.refs_2_ = bf16[4,128,128]{2,1,0:T(8,128)(2,1)S(1)} collective-permute-done((bf16[4,128,128]{2,1,0:T(8,128)(2,1)S(1)}, bf16[4,128,128]{2,1,0:T(8,128)(2,1)S(1)}, u32[]{:S(2)}, u32[]{:S(2)}) %collective-permute-start.3) | collective-permute-done | bytes 131104 | tf_op jit(solution)/shard_map/ppermute | solution.py:328
  24.1 0.0 collective-permute-start.4
  24.1 0.5 collective-permute-start.6
  24.6 0.6 %shard_map.71.refs_6_.refs_5_ = bf16[4,256,128]{2,1,0:T(8,128)(2,1)S(1)} custom-call(f32[8,128]{1,0:T(8,128)S(1)} %pad.9.refs_0_, bf16[4,144,128]{2,1,0:T(8,128)(2,1)S(1)} %collective-permute-done.5.refs_1_.refs_2_), custom_call_target="tpu_custom_call" | custom-call | flops 262144000 | bytes 413696 | tf_op jit(solution)/shard_map/pallas_call | solution.py:304
  25.2 0.6 %shard_map.70.refs_5_.refs_4_ = bf16[4,256,128]{2,1,0:T(8,128)(2,1)S(1)} custom-call(f32[8,128]{1,0:T(8,128)S(1)} %pad.9.refs_0_, bf16[4,144,128]{2,1,0:T(8,128)(2,1)S(1)} %collective-permute-done.7.refs_1_), custom_call_target="tpu_custom_call" | custom-call | flops 262144000 | bytes 413696 | tf_op jit(solution)/shard_map/pallas_call | solution.py:304
  25.8 0.4 shard_map.73.refs_6_
  26.2 0.6 %shard_map.68.refs_7_.refs_4_ = bf16[4,256,128]{2,1,0:T(8,128)(2,1)S(1)} custom-call(f32[8,128]{1,0:T(8,128)S(1)} %pad.9.refs_0_, bf16[4,144,128]{2,1,0:T(8,128)(2,1)S(1)} %collective-permute-done.6.refs_1_.refs_3_), custom_call_target="tpu_custom_call" | custom-call | flops 262144000 | bytes 413696 | tf_op jit(solution)/shard_map/pallas_call | solution.py:304
  26.8 0.5 shard_map.72.refs_5_
  27.3 5.8 %shard_map.74 = (f32[256,256]{1,0:T(8,128)S(1)}, f32[256,256]{1,0:T(8,128)S(1)}, f32[256,256]{1,0:T(8,128)S(1)}) custom-call(s32[1]{0:T(128)} %bitcast.refs_0_, s32[1]{0:T(128)S(6)} %copy.7.refs_1_, s32[1]{0:T(128)S(6)} %copy.8.refs_2_.ranks_ref, bf16[4,128,128]{2,1,0:T(8,128)(2,1)S(1)} %collective-permute-done.4.refs_3_, ...), custom_call_target="tpu_custom_call" | custom-call | flops 16777216 | bytes 1441804 | tf_op jit(solution)/shard_map/pallas_call | solution.py:304
  33.1 0.1 collective-permute-start.10
  33.2 1.5 %collective-permute-done.10.other_ref = f32[256,256]{1,0:T(8,128)S(1)} collective-permute-done((f32[256,256]{1,0:T(8,128)S(1)}, f32[256,256]{1,0:T(8,128)S(1)}, u32[]{:S(2)}, u32[]{:S(2)}) %collective-permute-start.10) | collective-permute-done | bytes 262176 | tf_op jit(solution)/shard_map/ppermute | solution.py:319
  34.7 5.3 %shard_map.76 = (f32[256,256]{1,0:T(8,128)S(1)}, f32[264,128]{1,0:T(8,128)S(1)}) custom-call(f32[256,256]{1,0:T(8,128)S(1)} %get-tuple-element.9.own_ref, f32[256,256]{1,0:T(8,128)S(1)} %collective-permute-done.10.other_ref), custom_call_target="tpu_custom_call" | custom-call | flops 16777216 | bytes 921600 | tf_op jit(solution)/shard_map/pallas_call | solution.py:304
  40.0 0.6 %collective-permute-start.11 = (f32[264,128]{1,0:T(8,128)S(1)}, f32[264,128]{1,0:T(8,128)S(1)}, u32[]{:S(2)}, u32[]{:S(2)}) collective-permute-start(f32[264,128]{1,0:T(8,128)S(1)} %get-tuple-element.11), channel_id=1, source_target_pairs={{0,4},{2,6},{4,0},{6,2},{8,12},{10,14},{12,8},{14,10},{16,20},{18,... | collective-permute-start | bytes 405512 | tf_op jit(solution)/shard_map/ppermute | solution.py:319
  40.6 0.4 shard_map.75
  41.0 0.8 %reshape.7 = f32[256,2,128]{2,1,0:T(2,128)} reshape(f32[256,256]{1,0:T(8,128)S(1)} %shard_map.75) | data formatting | bytes 524288 | tf_op jit(solution)/shard_map/reshape | solution.py:389
  41.8 3.8 %collective-permute-done.11.other_ref = f32[264,128]{1,0:T(8,128)S(1)} collective-permute-done((f32[264,128]{1,0:T(8,128)S(1)}, f32[264,128]{1,0:T(8,128)S(1)}, u32[]{:S(2)}, u32[]{:S(2)}) %collective-permute-start.11) | collective-permute-done | bytes 135200 | tf_op jit(solution)/shard_map/ppermute | solution.py:319
  45.7 5.7 %shard_map.77 = f32[256,256]{1,0:T(8,128)} custom-call(f32[256,256]{1,0:T(8,128)S(1)} %get-tuple-element.10.own_ref, f32[264,128]{1,0:T(8,128)S(1)} %collective-permute-done.11.other_ref), custom_call_target="tpu_custom_call" | custom-call | flops 16777216 | bytes 659456 | tf_op jit(solution)/shard_map/pallas_call | solution.py:304
  (10 shorter events, 0.1 us)
Async XLA Ops:
  0.6 17.4 %copy-start = (f32[3,256]{1,0:T(4,128)S(1)}, f32[3,256]{1,0:T(4,128)}, u32[]{:S(2)}) copy-start(f32[3,256]{1,0:T(4,128)} %param.5) | copy-start | bytes 9220
  1.4 5.6 %collective-permute-start = (bf16[1,144,128]{2,1,0:T(8,128)(2,1)S(1)}, bf16[1,144,128]{2,1,0:T(8,128)(2,1)S(1)}, u32[]{:S(2)}, u32[]{:S(2)}) collective-permute-start(bf16[1,144,128]{2,1,0:T(8,128)(2,1)S(1)} %fusion.2), channel_id=1, source_target_pairs={{0,8},{2,10},{4,12},{6,14},{8,0},{10,2},{12,4},{14,6},{16,24},{18,... | collective-permute-start | bytes 110600 | tf_op jit(solution)/shard_map/ppermute | solution.py:319
  4.5 5.5 %collective-permute-start.1 = (bf16[1,144,128]{2,1,0:T(8,128)(2,1)S(1)}, bf16[1,144,128]{2,1,0:T(8,128)(2,1)S(1)}, u32[]{:S(2)}, u32[]{:S(2)}) collective-permute-start(bf16[1,144,128]{2,1,0:T(8,128)(2,1)S(1)} %fusion.2), channel_id=1, source_target_pairs={{0,16},{2,18},{4,20},{6,22},{8,24},{10,26},{12,28},{14,30},{16,0},... | collective-permute-start | bytes 110600 | tf_op jit(solution)/shard_map/ppermute | solution.py:319
  7.1 5.8 %collective-permute-start.2 = (bf16[1,144,128]{2,1,0:T(8,128)(2,1)S(1)}, bf16[1,144,128]{2,1,0:T(8,128)(2,1)S(1)}, u32[]{:S(2)}, u32[]{:S(2)}) collective-permute-start(bf16[1,144,128]{2,1,0:T(8,128)(2,1)S(1)} %fusion.2), channel_id=1, source_target_pairs={{0,24},{2,26},{4,28},{6,30},{8,16},{10,18},{12,20},{14,22},{16,8},... | collective-permute-start | bytes 110600 | tf_op jit(solution)/shard_map/ppermute | solution.py:319
  12.9 5.0 %collective-permute-start.8 = (bf16[4,128,128]{2,1,0:T(8,128)(2,1)S(1)}, bf16[4,128,128]{2,1,0:T(8,128)(2,1)S(1)}, u32[]{:S(2)}, u32[]{:S(2)}) collective-permute-start(bf16[4,128,128]{2,1,0:T(8,128)(2,1)S(1)} %slice.4), channel_id=1, source_target_pairs={{0,1},{1,0},{2,3},{3,2},{4,5},{5,4},{6,7},{7,6},{8,9},{9,8},{10,11... | collective-permute-start | bytes 393224 | tf_op jit(solution)/shard_map/ppermute | solution.py:322
  14.5 9.7 %collective-permute-start.5 = (bf16[4,144,128]{2,1,0:T(8,128)(2,1)S(1)}, bf16[4,144,128]{2,1,0:T(8,128)(2,1)S(1)}, u32[]{:S(2)}, u32[]{:S(2)}) collective-permute-start(bf16[4,144,128]{2,1,0:T(8,128)(2,1)S(1)} %pad_maximum_fusion.refs_1_.refs_0_), channel_id=1, source_target_pairs={{0,4},{2,6},{4,0},{6,2},{8,12},{10,14},{12,8},{14,10},{16,20},{18,... | collective-permute-start | bytes 442376 | tf_op jit(solution)/shard_map/ppermute | solution.py:319
  17.2 8.0 %collective-permute-start.7 = (bf16[4,144,128]{2,1,0:T(8,128)(2,1)S(1)}, bf16[4,144,128]{2,1,0:T(8,128)(2,1)S(1)}, u32[]{:S(2)}, u32[]{:S(2)}) collective-permute-start(bf16[4,144,128]{2,1,0:T(8,128)(2,1)S(1)} %pad_maximum_fusion.refs_1_.refs_0_), channel_id=1, source_target_pairs={{0,2},{2,0},{4,6},{6,4},{8,10},{10,8},{12,14},{14,12},{16,18},{18,... | collective-permute-start | bytes 442376 | tf_op jit(solution)/shard_map/ppermute | solution.py:319
  17.3 6.8 %collective-permute-start.3 = (bf16[4,128,128]{2,1,0:T(8,128)(2,1)S(1)}, bf16[4,128,128]{2,1,0:T(8,128)(2,1)S(1)}, u32[]{:S(2)}, u32[]{:S(2)}) collective-permute-start(bf16[4,128,128]{2,1,0:T(8,128)(2,1)S(1)} %slice.4), channel_id=1, source_target_pairs={{0,5},{1,4},{2,7},{3,6},{4,1},{5,0},{6,3},{7,2},{8,13},{9,12},{10,... | collective-permute-start | bytes 393224 | tf_op jit(solution)/shard_map/ppermute | solution.py:328
  17.9 7.9 %collective-permute-start.9 = (bf16[4,128,128]{2,1,0:T(8,128)(2,1)S(1)}, bf16[4,128,128]{2,1,0:T(8,128)(2,1)S(1)}, u32[]{:S(2)}, u32[]{:S(2)}) collective-permute-start(bf16[4,128,128]{2,1,0:T(8,128)(2,1)S(1)} %collective-permute-done.8.refs_0_), channel_id=1, source_target_pairs={{0,2},{2,0},{4,6},{6,4},{8,10},{10,8},{12,14},{14,12},{16,18},{18,... | collective-permute-start | bytes 393224 | tf_op jit(solution)/shard_map/ppermute | solution.py:319
  24.1 3.1 %collective-permute-start.4 = (bf16[4,128,128]{2,1,0:T(8,128)(2,1)S(1)}, bf16[4,128,128]{2,1,0:T(8,128)(2,1)S(1)}, u32[]{:S(2)}, u32[]{:S(2)}) collective-permute-start(bf16[4,128,128]{2,1,0:T(8,128)(2,1)S(1)} %collective-permute-done.3.refs_2_), channel_id=1, source_target_pairs={{0,2},{2,0},{4,6},{6,4},{8,10},{10,8},{12,14},{14,12},{16,18},{18,... | collective-permute-start | bytes 393224 | tf_op jit(solution)/shard_map/ppermute | solution.py:319
  24.1 2.1 %collective-permute-start.6 = (bf16[4,144,128]{2,1,0:T(8,128)(2,1)S(1)}, bf16[4,144,128]{2,1,0:T(8,128)(2,1)S(1)}, u32[]{:S(2)}, u32[]{:S(2)}) collective-permute-start(bf16[4,144,128]{2,1,0:T(8,128)(2,1)S(1)} %collective-permute-done.5.refs_1_.refs_2_), channel_id=1, source_target_pairs={{0,2},{2,0},{4,6},{6,4},{8,10},{10,8},{12,14},{14,12},{16,18},{18,... | collective-permute-start | bytes 442376 | tf_op jit(solution)/shard_map/ppermute | solution.py:319
  33.1 1.6 %collective-permute-start.10 = (f32[256,256]{1,0:T(8,128)S(1)}, f32[256,256]{1,0:T(8,128)S(1)}, u32[]{:S(2)}, u32[]{:S(2)}) collective-permute-start(f32[256,256]{1,0:T(8,128)S(1)} %get-tuple-element.9.own_ref), channel_id=1, source_target_pairs={{0,2},{2,0},{4,6},{6,4},{8,10},{10,8},{12,14},{14,12},{16,18},{18,... | collective-permute-start | bytes 786440 | tf_op jit(solution)/shard_map/ppermute | solution.py:319
  40.0 5.7 %collective-permute-start.11 = (f32[264,128]{1,0:T(8,128)S(1)}, f32[264,128]{1,0:T(8,128)S(1)}, u32[]{:S(2)}, u32[]{:S(2)}) collective-permute-start(f32[264,128]{1,0:T(8,128)S(1)} %get-tuple-element.11), channel_id=1, source_target_pairs={{0,4},{2,6},{4,0},{6,2},{8,12},{10,14},{12,8},{14,10},{16,20},{18,... | collective-permute-start | bytes 405512 | tf_op jit(solution)/shard_map/ppermute | solution.py:319

commit v6 on v5

--- a/solution.py
+++ b/solution.py
@@ -250,7 +250,7 @@
     out_ref[...] = total
 
 
-def leaf_body(blocks, place_ref, sizes_ref, ranks_ref, probe_ref, kernel_ref, *refs):
+def leaf_body(blocks, place_ref, points_ref, probe_ref, kernel_ref, *refs):
     h_ref, m_ref, t_ref = refs[blocks:]
     n = h_ref.shape[0]
     rows, cols = grids(n)
@@ -261,18 +261,17 @@
             total = accumulate(probe_ref, kernel_ref, high, total)
         at = pl.multiple_of((place_ref[0] ^ o) * high, high)
         m_ref[pl.ds(at, high), :] = total
-    used = sizes_ref[0]
     half = n // 2
-    inside = cols - jnp.where(cols >= half, half, 0) < used
+    inside = (cols - jnp.where(cols >= half, half, 0)).astype(F32) < points_ref[3:4, 0:1]
     matrix = jnp.where(inside, m_ref[...], 0.0)
     m_ref[...] = matrix
     shift, by_row, by_col = factorize(dot3(matrix, matrix, NT), t_ref)
-    in_rank = rows < ranks_ref[0]
+    in_rank = rows.astype(F32) < points_ref[4:5, 0:1]
     value = jnp.where(in_rank, projected_rows(t_ref, by_row, by_col), 0.0)
     h_ref[...] = rows_gram(value) * shift
 
 
-def basis_body(ranks_ref, t_ref, m_ref, b_ref):
+def basis_body(points_ref, t_ref, m_ref, b_ref):
     n = t_ref.shape[0]
     rows, cols = grids(n)
     held = t_ref[...]
@@ -282,7 +281,7 @@
     by_row = jnp.sum(diagonal, axis=1, keepdims=True)
     by_col = jnp.sum(diagonal, axis=0, keepdims=True)
     inverse = jnp.where(rows > cols, held / by_col, jnp.where(rows == cols, 1.0, 0.0))
-    scale = jnp.where(rows < ranks_ref[0], lax.rsqrt(by_row * shift), 0.0)
+    scale = jnp.where(rows.astype(F32) < points_ref[4:5, 0:1], lax.rsqrt(by_row * shift), 0.0)
     b_ref[...] = dot3(inverse * scale, matrix, NN)
 
 
@@ -338,7 +337,8 @@
     place = lax.axis_index("probe")
 
     points = lax.dynamic_slice_in_dim(targets, place * leaf_rows, leaf_rows, 1)
-    points = jnp.pad(points, ((0, 8 - points.shape[0]), (0, 0)))
+    limits = [jnp.full((1, leaf_rows), x[0]).astype(F32) for x in (cluster_sizes, leaf_ranks)]
+    points = jnp.concatenate([points, *limits, jnp.zeros((3, leaf_rows), F32)], axis=0)
 
     def evaluate(arrays):
         outs = [jax.ShapeDtypeStruct((x.shape[0], 2 * leaf_rows, x.shape[2]), BF16) for x in arrays]
@@ -351,7 +351,9 @@
     mask = rows_size // 2
     while mask > 2:
         low = mask // 2 if mask // 2 > 2 else 0
-        received = [flip(pieces, m) for m in ([low, mask, mask + low] if low else [mask])]
+        received = []
+        for m in [low, mask, mask + low] if low else [mask]:
+            received.append(flip(pieces, m))
         pieces = jnp.concatenate([pieces, *received], axis=0)
         mask //= 4 if low else 2
     masks = [0, 2] if rows_size > 2 else [0]
@@ -377,11 +379,11 @@
     scratch = [pltpu.VMEM((n, n), F32)]
     h, m, t = call(
         lambda *refs: leaf_body(probe_size, *refs), [square] * 3,
-        [place[None], cluster_sizes, leaf_ranks, held[-1], values[-1], *samples],
-        specs=[SMEM] * 3 + [VMEM] * (2 + len(samples)), flops=n**3,
+        [place[None], points, held[-1], values[-1], *samples],
+        specs=[SMEM] + [VMEM] * (3 + len(samples)), flops=n**3,
     )
     other = flip(h, 1)
-    basis = call(basis_body, [square], [leaf_ranks, t, m], specs=[SMEM, VMEM, VMEM], flops=60 * n**3)[0]
+    basis = call(basis_body, [square], [points, t, m], flops=60 * n**3)[0]
     packed = jax.ShapeDtypeStruct((n + 8, n // 2), F32)
     h, sent = call(node_body, [square, packed], [h, other], scratch=scratch, flops=n**3)
     other = flip(sent, 2)

time: 51.6 us -> 51.8 us (level)
  waiting for transfers between devices: 16.7 us -> 16 us
  starting transfers between devices: 10.6 us -> 11.2 us
    ppermute x10, starting transfers between devices: 8.49 us -> 9.12 us  [flip(): return lax.ppermute(value, 'rows', pairs)]
    ppermute x10, waiting for transfers between devices: 11.1 us -> 10.6 us  [flip(): return lax.ppermute(value, 'rows', pairs)]
where the time goes in v6:
time: 51.8 us; the launch traced here: 51.6 us
  Pallas kernels  20.4 us (39%)
  waiting for transfers between devices  16 us (31%)
  starting transfers between devices  11.2 us (22%)
  between operations  2.06 us (4%)
  local copies, waits for them, and re-layouts  1.08 us (2%)
  other arithmetic  0.88 us (2%)
    pallas_call x10, Pallas kernels, call(): pl.pallas_call(body, out_shape=list(outs), in_specs=list(specs or [VMEM]...  20.4 us
    ppermute x10, waiting for transfers between devices, flip(): return lax.ppermute(value, 'rows', pairs)  10.6 us
    ppermute x10, starting transfers between devices, flip(): return lax.ppermute(value, 'rows', pairs)  9.12 us
    ppermute x1, waiting for transfers between devices, flip(): return lax.ppermute(value, ('rows', 'probe'), pairs)  5.46 us
    ppermute x1, starting transfers between devices, flip(): return lax.ppermute(value, 'probe', pairs)  1.58 us
  transfers between devices with their start and end apart: 12, of which 5 were waited for; matrix products, arithmetic and copies ran while one was open for 2% of the time, Pallas kernels for 7%

profile of v6, /device:TPU:0, one launch (start us, length us, event | category | flops | bytes accessed | tf_op | source)
XLA Modules:
  0.0 51.6 jit_solution(9682003683149165577)
XLA Ops:
  0.6 0.0 copy-start
  0.6 0.8 %fusion.2 = bf16[1,144,128]{2,1,0:T(8,128)(2,1)S(1)} fusion(bf16[3,128]{1,0:T(4,128)(2,1)} %param.6, bf16[128,128]{1,0:T(8,128)(2,1)} %param.7), kind=kLoop, calls=%fused_computation.4 | loop fusion | flops 110592 | bytes 70400 | tf_op jit(solution)/shard_map/broadcast_in_dim | solution.py:350
  1.4 3.1 %collective-permute-start = (bf16[1,144,128]{2,1,0:T(8,128)(2,1)S(1)}, bf16[1,144,128]{2,1,0:T(8,128)(2,1)S(1)}, u32[]{:S(2)}, u32[]{:S(2)}) collective-permute-start(bf16[1,144,128]{2,1,0:T(8,128)(2,1)S(1)} %fusion.2), channel_id=1, source_target_pairs={{0,8},{2,10},{4,12},{6,14},{8,0},{10,2},{12,4},{14,6},{16,24},{18,... | collective-permute-start | bytes 110600 | tf_op jit(solution)/shard_map/ppermute | solution.py:318
  4.5 2.6 %collective-permute-start.1 = (bf16[1,144,128]{2,1,0:T(8,128)(2,1)S(1)}, bf16[1,144,128]{2,1,0:T(8,128)(2,1)S(1)}, u32[]{:S(2)}, u32[]{:S(2)}) collective-permute-start(bf16[1,144,128]{2,1,0:T(8,128)(2,1)S(1)} %fusion.2), channel_id=1, source_target_pairs={{0,16},{2,18},{4,20},{6,22},{8,24},{10,26},{12,28},{14,30},{16,0},... | collective-permute-start | bytes 110600 | tf_op jit(solution)/shard_map/ppermute | solution.py:318
  7.1 0.0 collective-permute-start.2
  7.1 2.9 %collective-permute-done.1 = bf16[1,144,128]{2,1,0:T(8,128)(2,1)S(1)} collective-permute-done((bf16[1,144,128]{2,1,0:T(8,128)(2,1)S(1)}, bf16[1,144,128]{2,1,0:T(8,128)(2,1)S(1)}, u32[]{:S(2)}, u32[]{:S(2)}) %collective-permute-start.1) | collective-permute-done | bytes 36896 | tf_op jit(solution)/shard_map/ppermute | solution.py:318
  10.0 2.8 %collective-permute-done.2 = bf16[1,144,128]{2,1,0:T(8,128)(2,1)S(1)} collective-permute-done((bf16[1,144,128]{2,1,0:T(8,128)(2,1)S(1)}, bf16[1,144,128]{2,1,0:T(8,128)(2,1)S(1)}, u32[]{:S(2)}, u32[]{:S(2)}) %collective-permute-start.2) | collective-permute-done | bytes 36896 | tf_op jit(solution)/shard_map/ppermute | solution.py:318
  12.9 1.6 %collective-permute-start.8 = (bf16[4,128,128]{2,1,0:T(8,128)(2,1)S(1)}, bf16[4,128,128]{2,1,0:T(8,128)(2,1)S(1)}, u32[]{:S(2)}, u32[]{:S(2)}) collective-permute-start(bf16[4,128,128]{2,1,0:T(8,128)(2,1)S(1)} %slice.4), channel_id=1, source_target_pairs={{0,1},{1,0},{2,3},{3,2},{4,5},{5,4},{6,7},{7,6},{8,9},{9,8},{10,11... | collective-permute-start | bytes 393224 | tf_op jit(solution)/shard_map/ppermute | solution.py:321
  15.8 0.1 pad.12.clone
  15.8 0.1 pad.13.clone
  15.9 0.1 pad.14.clone
  16.0 1.5 %collective-permute-start.5 = (bf16[4,144,128]{2,1,0:T(8,128)(2,1)S(1)}, bf16[4,144,128]{2,1,0:T(8,128)(2,1)S(1)}, u32[]{:S(2)}, u32[]{:S(2)}) collective-permute-start(bf16[4,144,128]{2,1,0:T(8,128)(2,1)S(1)} %pad_maximum_fusion.refs_1_.refs_0_), channel_id=1, source_target_pairs={{0,4},{2,6},{4,0},{6,2},{8,12},{10,14},{12,8},{14,10},{16,20},{18,... | collective-permute-start | bytes 442376 | tf_op jit(solution)/shard_map/ppermute | solution.py:318
  17.5 0.5 collective-permute-start.3
  18.0 0.2 collective-permute-start.9
  18.2 0.1 maximum_maximum_fusion.refs_0_.refs_1_.points_ref
  18.3 0.6 %shard_map.69.refs_4_.refs_3_ = bf16[4,256,128]{2,1,0:T(8,128)(2,1)S(1)} custom-call(f32[8,128]{1,0:T(8,128)S(1)} %maximum_maximum_fusion.refs_0_.refs_1_.points_ref, bf16[4,144,128]{2,1,0:T(8,128)(2,1)S(1)} %pad_maximum_fusion.refs_1_.refs_0_), custom_call_target="tpu_custom_call" | custom-call | flops 262144000 | bytes 413696 | tf_op jit(solution)/shard_map/pallas_call | solution.py:303
  18.9 5.5 %collective-permute-done.3.refs_2_ = bf16[4,128,128]{2,1,0:T(8,128)(2,1)S(1)} collective-permute-done((bf16[4,128,128]{2,1,0:T(8,128)(2,1)S(1)}, bf16[4,128,128]{2,1,0:T(8,128)(2,1)S(1)}, u32[]{:S(2)}, u32[]{:S(2)}) %collective-permute-start.3) | collective-permute-done | bytes 131104 | tf_op jit(solution)/shard_map/ppermute | solution.py:327
  24.3 0.5 collective-permute-start.6
  24.8 0.6 %shard_map.71.refs_6_.refs_5_ = bf16[4,256,128]{2,1,0:T(8,128)(2,1)S(1)} custom-call(f32[8,128]{1,0:T(8,128)S(1)} %maximum_maximum_fusion.refs_0_.refs_1_.points_ref, bf16[4,144,128]{2,1,0:T(8,128)(2,1)S(1)} %collective-permute-done.5.refs_1_.refs_2_), custom_call_target="tpu_custom_call" | custom-call | flops 262144000 | bytes 413696 | tf_op jit(solution)/shard_map/pallas_call | solution.py:303
  25.4 0.6 %shard_map.70.refs_5_.refs_4_ = bf16[4,256,128]{2,1,0:T(8,128)(2,1)S(1)} custom-call(f32[8,128]{1,0:T(8,128)S(1)} %maximum_maximum_fusion.refs_0_.refs_1_.points_ref, bf16[4,144,128]{2,1,0:T(8,128)(2,1)S(1)} %collective-permute-done.7.refs_1_), custom_call_target="tpu_custom_call" | custom-call | flops 262144000 | bytes 413696 | tf_op jit(solution)/shard_map/pallas_call | solution.py:303
  26.0 0.4 shard_map.73.refs_5_
  26.4 0.6 %shard_map.68.refs_7_.refs_3_ = bf16[4,256,128]{2,1,0:T(8,128)(2,1)S(1)} custom-call(f32[8,128]{1,0:T(8,128)S(1)} %maximum_maximum_fusion.refs_0_.refs_1_.points_ref, bf16[4,144,128]{2,1,0:T(8,128)(2,1)S(1)} %collective-permute-done.6.refs_1_.refs_3_), custom_call_target="tpu_custom_call" | custom-call | flops 262144000 | bytes 413696 | tf_op jit(solution)/shard_map/pallas_call | solution.py:303
  26.9 0.5 shard_map.72.refs_4_
  27.4 5.8 %shard_map.74 = (f32[256,256]{1,0:T(8,128)S(1)}, f32[256,256]{1,0:T(8,128)S(1)}, f32[256,256]{1,0:T(8,128)S(1)}) custom-call(s32[1]{0:T(128)} %bitcast.2.refs_0_, f32[8,128]{1,0:T(8,128)S(1)} %maximum_maximum_fusion.refs_0_.refs_1_.points_ref, bf16[4,128,128]{2,1,0:T(8,128)(2,1)S(1)} %collective-permute-done.4.refs_2_, ...), custom_call_target="tpu_custom_call" | custom-call | flops 16777216 | bytes 1445892 | tf_op jit(solution)/shard_map/pallas_call | solution.py:303
  33.3 0.1 collective-permute-start.10
  33.4 1.5 %collective-permute-done.10.other_ref = f32[256,256]{1,0:T(8,128)S(1)} collective-permute-done((f32[256,256]{1,0:T(8,128)S(1)}, f32[256,256]{1,0:T(8,128)S(1)}, u32[]{:S(2)}, u32[]{:S(2)}) %collective-permute-start.10) | collective-permute-done | bytes 262176 | tf_op jit(solution)/shard_map/ppermute | solution.py:318
  34.9 5.3 %shard_map.76 = (f32[256,256]{1,0:T(8,128)S(1)}, f32[264,128]{1,0:T(8,128)S(1)}) custom-call(f32[256,256]{1,0:T(8,128)S(1)} %get-tuple-element.9.own_ref, f32[256,256]{1,0:T(8,128)S(1)} %collective-permute-done.10.other_ref), custom_call_target="tpu_custom_call" | custom-call | flops 16777216 | bytes 921600 | tf_op jit(solution)/shard_map/pallas_call | solution.py:303
  40.2 1.1 %collective-permute-start.11 = (f32[264,128]{1,0:T(8,128)S(1)}, f32[264,128]{1,0:T(8,128)S(1)}, u32[]{:S(2)}, u32[]{:S(2)}) collective-permute-start(f32[264,128]{1,0:T(8,128)S(1)} %get-tuple-element.11), channel_id=1, source_target_pairs={{0,4},{2,6},{4,0},{6,2},{8,12},{10,14},{12,8},{14,10},{16,20},{18,... | collective-permute-start | bytes 405512 | tf_op jit(solution)/shard_map/ppermute | solution.py:318
  41.3 0.4 shard_map.75
  41.8 0.8 %reshape.9 = f32[256,2,128]{2,1,0:T(2,128)} reshape(f32[256,256]{1,0:T(8,128)S(1)} %shard_map.75) | data formatting | bytes 524288 | tf_op jit(solution)/shard_map/reshape | solution.py:391
  42.6 3.3 %collective-permute-done.11.other_ref = f32[264,128]{1,0:T(8,128)S(1)} collective-permute-done((f32[264,128]{1,0:T(8,128)S(1)}, f32[264,128]{1,0:T(8,128)S(1)}, u32[]{:S(2)}, u32[]{:S(2)}) %collective-permute-start.11) | collective-permute-done | bytes 135200 | tf_op jit(solution)/shard_map/ppermute | solution.py:318
  45.9 5.7 %shard_map.77 = f32[256,256]{1,0:T(8,128)} custom-call(f32[256,256]{1,0:T(8,128)S(1)} %get-tuple-element.10.own_ref, f32[264,128]{1,0:T(8,128)S(1)} %collective-permute-done.11.other_ref), custom_call_target="tpu_custom_call" | custom-call | flops 16777216 | bytes 659456 | tf_op jit(solution)/shard_map/pallas_call | solution.py:303
  (14 shorter events, 0.1 us)
Async XLA Ops:
  0.6 15.4 %copy-start = (f32[3,256]{1,0:T(4,128)S(1)}, f32[3,256]{1,0:T(4,128)}, u32[]{:S(2)}) copy-start(f32[3,256]{1,0:T(4,128)} %param.5) | copy-start | bytes 9220
  1.4 5.6 %collective-permute-start = (bf16[1,144,128]{2,1,0:T(8,128)(2,1)S(1)}, bf16[1,144,128]{2,1,0:T(8,128)(2,1)S(1)}, u32[]{:S(2)}, u32[]{:S(2)}) collective-permute-start(bf16[1,144,128]{2,1,0:T(8,128)(2,1)S(1)} %fusion.2), channel_id=1, source_target_pairs={{0,8},{2,10},{4,12},{6,14},{8,0},{10,2},{12,4},{14,6},{16,24},{18,... | collective-permute-start | bytes 110600 | tf_op jit(solution)/shard_map/ppermute | solution.py:318
  4.5 5.5 %collective-permute-start.1 = (bf16[1,144,128]{2,1,0:T(8,128)(2,1)S(1)}, bf16[1,144,128]{2,1,0:T(8,128)(2,1)S(1)}, u32[]{:S(2)}, u32[]{:S(2)}) collective-permute-start(bf16[1,144,128]{2,1,0:T(8,128)(2,1)S(1)} %fusion.2), channel_id=1, source_target_pairs={{0,16},{2,18},{4,20},{6,22},{8,24},{10,26},{12,28},{14,30},{16,0},... | collective-permute-start | bytes 110600 | tf_op jit(solution)/shard_map/ppermute | solution.py:318
  7.1 5.8 %collective-permute-start.2 = (bf16[1,144,128]{2,1,0:T(8,128)(2,1)S(1)}, bf16[1,144,128]{2,1,0:T(8,128)(2,1)S(1)}, u32[]{:S(2)}, u32[]{:S(2)}) collective-permute-start(bf16[1,144,128]{2,1,0:T(8,128)(2,1)S(1)} %fusion.2), channel_id=1, source_target_pairs={{0,24},{2,26},{4,28},{6,30},{8,16},{10,18},{12,20},{14,22},{16,8},... | collective-permute-start | bytes 110600 | tf_op jit(solution)/shard_map/ppermute | solution.py:318
  12.9 5.1 %collective-permute-start.8 = (bf16[4,128,128]{2,1,0:T(8,128)(2,1)S(1)}, bf16[4,128,128]{2,1,0:T(8,128)(2,1)S(1)}, u32[]{:S(2)}, u32[]{:S(2)}) collective-permute-start(bf16[4,128,128]{2,1,0:T(8,128)(2,1)S(1)} %slice.4), channel_id=1, source_target_pairs={{0,1},{1,0},{2,3},{3,2},{4,5},{5,4},{6,7},{7,6},{8,9},{9,8},{10,11... | collective-permute-start | bytes 393224 | tf_op jit(solution)/shard_map/ppermute | solution.py:321
  16.0 8.3 %collective-permute-start.5 = (bf16[4,144,128]{2,1,0:T(8,128)(2,1)S(1)}, bf16[4,144,128]{2,1,0:T(8,128)(2,1)S(1)}, u32[]{:S(2)}, u32[]{:S(2)}) collective-permute-start(bf16[4,144,128]{2,1,0:T(8,128)(2,1)S(1)} %pad_maximum_fusion.refs_1_.refs_0_), channel_id=1, source_target_pairs={{0,4},{2,6},{4,0},{6,2},{8,12},{10,14},{12,8},{14,10},{16,20},{18,... | collective-permute-start | bytes 442376 | tf_op jit(solution)/shard_map/ppermute | solution.py:318
  17.5 7.9 %collective-permute-start.7 = (bf16[4,144,128]{2,1,0:T(8,128)(2,1)S(1)}, bf16[4,144,128]{2,1,0:T(8,128)(2,1)S(1)}, u32[]{:S(2)}, u32[]{:S(2)}) collective-permute-start(bf16[4,144,128]{2,1,0:T(8,128)(2,1)S(1)} %pad_maximum_fusion.refs_1_.refs_0_), channel_id=1, source_target_pairs={{0,2},{2,0},{4,6},{6,4},{8,10},{10,8},{12,14},{14,12},{16,18},{18,... | collective-permute-start | bytes 442376 | tf_op jit(solution)/shard_map/ppermute | solution.py:318
  17.5 6.8 %collective-permute-start.3 = (bf16[4,128,128]{2,1,0:T(8,128)(2,1)S(1)}, bf16[4,128,128]{2,1,0:T(8,128)(2,1)S(1)}, u32[]{:S(2)}, u32[]{:S(2)}) collective-permute-start(bf16[4,128,128]{2,1,0:T(8,128)(2,1)S(1)} %slice.4), channel_id=1, source_target_pairs={{0,5},{1,4},{2,7},{3,6},{4,1},{5,0},{6,3},{7,2},{8,13},{9,12},{10,... | collective-permute-start | bytes 393224 | tf_op jit(solution)/shard_map/ppermute | solution.py:327
  18.0 8.0 %collective-permute-start.9 = (bf16[4,128,128]{2,1,0:T(8,128)(2,1)S(1)}, bf16[4,128,128]{2,1,0:T(8,128)(2,1)S(1)}, u32[]{:S(2)}, u32[]{:S(2)}) collective-permute-start(bf16[4,128,128]{2,1,0:T(8,128)(2,1)S(1)} %collective-permute-done.8.refs_0_), channel_id=1, source_target_pairs={{0,2},{2,0},{4,6},{6,4},{8,10},{10,8},{12,14},{14,12},{16,18},{18,... | collective-permute-start | bytes 393224 | tf_op jit(solution)/shard_map/ppermute | solution.py:318
  24.3 3.1 %collective-permute-start.4 = (bf16[4,128,128]{2,1,0:T(8,128)(2,1)S(1)}, bf16[4,128,128]{2,1,0:T(8,128)(2,1)S(1)}, u32[]{:S(2)}, u32[]{:S(2)}) collective-permute-start(bf16[4,128,128]{2,1,0:T(8,128)(2,1)S(1)} %collective-permute-done.3.refs_2_), channel_id=1, source_target_pairs={{0,2},{2,0},{4,6},{6,4},{8,10},{10,8},{12,14},{14,12},{16,18},{18,... | collective-permute-start | bytes 393224 | tf_op jit(solution)/shard_map/ppermute | solution.py:318
  24.3 2.0 %collective-permute-start.6 = (bf16[4,144,128]{2,1,0:T(8,128)(2,1)S(1)}, bf16[4,144,128]{2,1,0:T(8,128)(2,1)S(1)}, u32[]{:S(2)}, u32[]{:S(2)}) collective-permute-start(bf16[4,144,128]{2,1,0:T(8,128)(2,1)S(1)} %collective-permute-done.5.refs_1_.refs_2_), channel_id=1, source_target_pairs={{0,2},{2,0},{4,6},{6,4},{8,10},{10,8},{12,14},{14,12},{16,18},{18,... | collective-permute-start | bytes 442376 | tf_op jit(solution)/shard_map/ppermute | solution.py:318
  33.3 1.6 %collective-permute-start.10 = (f32[256,256]{1,0:T(8,128)S(1)}, f32[256,256]{1,0:T(8,128)S(1)}, u32[]{:S(2)}, u32[]{:S(2)}) collective-permute-start(f32[256,256]{1,0:T(8,128)S(1)} %get-tuple-element.9.own_ref), channel_id=1, source_target_pairs={{0,2},{2,0},{4,6},{6,4},{8,10},{10,8},{12,14},{14,12},{16,18},{18,... | collective-permute-start | bytes 786440 | tf_op jit(solution)/shard_map/ppermute | solution.py:318
  40.2 5.7 %collective-permute-start.11 = (f32[264,128]{1,0:T(8,128)S(1)}, f32[264,128]{1,0:T(8,128)S(1)}, u32[]{:S(2)}, u32[]{:S(2)}) collective-permute-start(f32[264,128]{1,0:T(8,128)S(1)} %get-tuple-element.11), channel_id=1, source_target_pairs={{0,4},{2,6},{4,0},{6,2},{8,12},{10,14},{12,8},{14,10},{16,20},{18,... | collective-permute-start | bytes 405512 | tf_op jit(solution)/shard_map/ppermute | solution.py:318

commit v7 on v6

--- a/solution.py
+++ b/solution.py
@@ -18,9 +18,13 @@
 NN = ((1,), (0,))
 NT = ((1,), (1,))
 
+SINE = (3.1415927410125732, -5.167710304260254, 2.550077438354492, -0.598291277885437, 0.07765766233205795)
+COSINE = (0.9999999403953552, -4.934792995452881, 4.058411121368408, -1.331876516342163, 0.21968960762023926)
+
 LANES = 128
 PANEL = 64
 CHUNK = 256
+COARSE = 0.2
 
 
 def split_bf16(value):
@@ -140,11 +144,16 @@
     return rows, cols
 
 
+def trace(matrix):
+    rows, cols = grids(matrix.shape[0])
+    diagonal = jnp.where(rows == cols, matrix, 0.0)
+    return jnp.sum(jnp.sum(diagonal, axis=0, keepdims=True), axis=1, keepdims=True)
+
+
 def factorize(gram, t_ref):
     n = gram.shape[0]
     rows, cols = grids(n)
-    diagonal = jnp.where(rows == cols, gram, 0.0)
-    shift = jnp.sum(jnp.sum(diagonal, axis=0, keepdims=True), axis=1, keepdims=True) / n
+    shift = trace(gram) / n
     t_ref[...] = gram / shift + jnp.where(rows == cols, 1.0, 0.0)
     along_lanes, along_rows = sweep(t_ref)
     sums = [jnp.sum(x, axis=0, keepdims=True) for x in along_lanes]
@@ -205,27 +214,28 @@
 
 def kernel_values(source, points, col_total):
     size = 1.0 / math.sqrt(col_total)
-    turns = wavenumber * 2.0 / math.pi
-    h = math.pi / 2
     square = softening * softening
     for c in range(3):
         diff = source[c : c + 1, :] - points[c]
         square = square + diff * diff
     near = lax.rsqrt(square)
     amplitude = near * size
-    quarter = (square * near) * turns
-    whole = jnp.round(quarter)
-    rest = quarter - whole
+    turns = (square * near) * (wavenumber / math.pi)
+    whole = jnp.round(turns)
+    rest = turns - whole
     r2 = rest * rest
-    sine = rest * (h + r2 * (-(h**3) / 6 + r2 * (h**5 / 120 + r2 * (-(h**7) / 5040))))
-    cosine = 1.0 + r2 * (-(h**2) / 2 + r2 * (h**4 / 24 + r2 * (-(h**6) / 720 + r2 * (h**8 / 40320))))
-    count = whole.astype(jnp.int32)
-    odd = (count & 1) == 1
-    first = jnp.where(odd, sine, cosine)
-    second = jnp.where(odd, cosine, sine)
-    first = jnp.where(((count + 1) & 2) == 0, first, -first)
-    second = jnp.where((count & 2) == 0, second, -second)
-    return (amplitude * first).astype(BF16), (amplitude * second).astype(BF16)
+    sine = rest * power_series(SINE, r2)
+    cosine = power_series(COSINE, r2)
+    odd = (whole.astype(jnp.int32) & 1) == 1
+    amplitude = jnp.where(odd, -amplitude, amplitude)
+    return (amplitude * cosine).astype(BF16), (amplitude * sine).astype(BF16)
+
+
+def power_series(terms, x):
+    value = terms[-1]
+    for term in terms[-2::-1]:
+        value = value * x + term
+    return value
 
 
 def accumulate(probe_ref, kernel_ref, high, total):
@@ -285,10 +295,39 @@
     b_ref[...] = dot3(inverse * scale, matrix, NN)
 
 
-def node_body(own_ref, other_ref, h_ref, packed_ref, t_ref):
-    shift, by_row, by_col = factorize(own_ref[...] + other_ref[...], t_ref)
-    value = projected_rows(t_ref, by_row, by_col)
-    h_ref[...] = rows_gram(value) * shift
+def inverse(matrix):
+    n = matrix.shape[0]
+    rows, cols = grids(n)
+    high, low = split_bf16(matrix)
+    least, most = 1.0, 1.001 * (n + 1.0)
+    scale = 2.0 / (least + most)
+    guess = jnp.where(rows == cols, 2.0 * scale, 0.0) - scale * scale * matrix
+    spread = (most - least) / (most + least)
+    while spread > 1e-3:
+        least = 1.0 - spread * spread
+        scale = 2.0 / (1.0 + least)
+        spread = (1.0 - least) / (1.0 + least)
+        if spread > COARSE:
+            rough = guess.astype(BF16)
+            product = mxu(high, rough, NN).astype(BF16)
+            change = mxu(rough, product, NN)
+        else:
+            gh, gl = split_bf16(guess)
+            product = mxu(high, gh, NN) + (mxu(high, gl, NN) + mxu(low, gh, NN))
+            ph, pl_ = split_bf16(product)
+            change = mxu(gh, ph, NN) + (mxu(gh, pl_, NN) + mxu(gl, ph, NN))
+        guess = (2.0 * scale) * guess - (scale * scale) * change
+    return guess
+
+
+def node_body(own_ref, other_ref, h_ref, packed_ref):
+    gram = own_ref[...] + other_ref[...]
+    n = gram.shape[0]
+    rows, cols = grids(n)
+    shift = trace(gram) / n
+    scaled = gram / shift
+    start = scaled + jnp.where(rows == cols, 1.0, 0.0)
+    h_ref[...] = (scaled - jnp.where(rows == cols, 1.0, 0.0) + inverse(start)) * shift
     fold(h_ref, packed_ref)
 
 
@@ -385,7 +424,7 @@
     other = flip(h, 1)
     basis = call(basis_body, [square], [points, t, m], flops=60 * n**3)[0]
     packed = jax.ShapeDtypeStruct((n + 8, n // 2), F32)
-    h, sent = call(node_body, [square, packed], [h, other], scratch=scratch, flops=n**3)
+    h, sent = call(node_body, [square, packed], [h, other], flops=n**3)
     other = flip(sent, 2)
     top = call(top_body, [square], [h, other], scratch=scratch, flops=n**3)[0]
     return (basis.reshape(n, 2, leaf_rows), top[None])

time: 51.8 us -> 49.3 us (0.952)
  Pallas kernels: 20.4 us -> 17.8 us
    pallas_call x10, Pallas kernels: 20.4 us -> 17.8 us  [call(): pl.pallas_call(body, out_shape=list(outs), in_specs=list(specs or [VMEM]...]
where the time goes in v7:
time: 49.3 us; the launch traced here: 49.1 us
  Pallas kernels  17.8 us (36%)
  waiting for transfers between devices  16.1 us (33%)
  starting transfers between devices  11.2 us (23%)
  between operations  2.05 us (4%)
  local copies, waits for them, and re-layouts  1.08 us (2%)
  other arithmetic  0.88 us (2%)
    pallas_call x10, Pallas kernels, call(): pl.pallas_call(body, out_shape=list(outs), in_specs=list(specs or [VMEM]...  17.8 us
    ppermute x10, waiting for transfers between devices, flip(): return lax.ppermute(value, 'rows', pairs)  10.6 us
    ppermute x10, starting transfers between devices, flip(): return lax.ppermute(value, 'rows', pairs)  9.11 us
    ppermute x1, waiting for transfers between devices, flip(): return lax.ppermute(value, ('rows', 'probe'), pairs)  5.53 us
    ppermute x1, starting transfers between devices, flip(): return lax.ppermute(value, 'probe', pairs)  1.58 us
  transfers between devices with their start and end apart: 12, of which 5 were waited for; matrix products, arithmetic and copies ran while one was open for 2% of the time, Pallas kernels for 7%

profile of v7, /device:TPU:0, one launch (start us, length us, event | category | flops | bytes accessed | tf_op | source)
XLA Modules:
  0.0 49.1 jit_solution(14066478323065199703)
XLA Ops:
  0.6 0.0 copy-start
  0.6 0.8 %fusion.2 = bf16[1,144,128]{2,1,0:T(8,128)(2,1)S(1)} fusion(bf16[3,128]{1,0:T(4,128)(2,1)} %param.6, bf16[128,128]{1,0:T(8,128)(2,1)} %param.7), kind=kLoop, calls=%fused_computation.4 | loop fusion | flops 110592 | bytes 70400 | tf_op jit(solution)/shard_map/broadcast_in_dim | solution.py:389
  1.4 3.1 %collective-permute-start = (bf16[1,144,128]{2,1,0:T(8,128)(2,1)S(1)}, bf16[1,144,128]{2,1,0:T(8,128)(2,1)S(1)}, u32[]{:S(2)}, u32[]{:S(2)}) collective-permute-start(bf16[1,144,128]{2,1,0:T(8,128)(2,1)S(1)} %fusion.2), channel_id=1, source_target_pairs={{0,8},{2,10},{4,12},{6,14},{8,0},{10,2},{12,4},{14,6},{16,24},{18,... | collective-permute-start | bytes 110600 | tf_op jit(solution)/shard_map/ppermute | solution.py:357
  4.5 2.6 %collective-permute-start.1 = (bf16[1,144,128]{2,1,0:T(8,128)(2,1)S(1)}, bf16[1,144,128]{2,1,0:T(8,128)(2,1)S(1)}, u32[]{:S(2)}, u32[]{:S(2)}) collective-permute-start(bf16[1,144,128]{2,1,0:T(8,128)(2,1)S(1)} %fusion.2), channel_id=1, source_target_pairs={{0,16},{2,18},{4,20},{6,22},{8,24},{10,26},{12,28},{14,30},{16,0},... | collective-permute-start | bytes 110600 | tf_op jit(solution)/shard_map/ppermute | solution.py:357
  7.1 0.0 collective-permute-start.2
  7.1 2.9 %collective-permute-done.1 = bf16[1,144,128]{2,1,0:T(8,128)(2,1)S(1)} collective-permute-done((bf16[1,144,128]{2,1,0:T(8,128)(2,1)S(1)}, bf16[1,144,128]{2,1,0:T(8,128)(2,1)S(1)}, u32[]{:S(2)}, u32[]{:S(2)}) %collective-permute-start.1) | collective-permute-done | bytes 36896 | tf_op jit(solution)/shard_map/ppermute | solution.py:357
  10.0 2.8 %collective-permute-done.2 = bf16[1,144,128]{2,1,0:T(8,128)(2,1)S(1)} collective-permute-done((bf16[1,144,128]{2,1,0:T(8,128)(2,1)S(1)}, bf16[1,144,128]{2,1,0:T(8,128)(2,1)S(1)}, u32[]{:S(2)}, u32[]{:S(2)}) %collective-permute-start.2) | collective-permute-done | bytes 36896 | tf_op jit(solution)/shard_map/ppermute | solution.py:357
  12.9 1.6 %collective-permute-start.8 = (bf16[4,128,128]{2,1,0:T(8,128)(2,1)S(1)}, bf16[4,128,128]{2,1,0:T(8,128)(2,1)S(1)}, u32[]{:S(2)}, u32[]{:S(2)}) collective-permute-start(bf16[4,128,128]{2,1,0:T(8,128)(2,1)S(1)} %slice.4), channel_id=1, source_target_pairs={{0,1},{1,0},{2,3},{3,2},{4,5},{5,4},{6,7},{7,6},{8,9},{9,8},{10,11... | collective-permute-start | bytes 393224 | tf_op jit(solution)/shard_map/ppermute | solution.py:360
  15.8 0.1 pad.12.clone
  15.8 0.1 pad.13.clone
  15.9 0.1 pad.14.clone
  16.0 1.5 %collective-permute-start.5 = (bf16[4,144,128]{2,1,0:T(8,128)(2,1)S(1)}, bf16[4,144,128]{2,1,0:T(8,128)(2,1)S(1)}, u32[]{:S(2)}, u32[]{:S(2)}) collective-permute-start(bf16[4,144,128]{2,1,0:T(8,128)(2,1)S(1)} %pad_maximum_fusion.refs_1_.refs_0_), channel_id=1, source_target_pairs={{0,4},{2,6},{4,0},{6,2},{8,12},{10,14},{12,8},{14,10},{16,20},{18,... | collective-permute-start | bytes 442376 | tf_op jit(solution)/shard_map/ppermute | solution.py:357
  17.5 0.5 collective-permute-start.3
  18.0 0.2 collective-permute-start.9
  18.2 0.1 maximum_maximum_fusion.refs_0_.refs_1_.points_ref
  18.3 0.5 %shard_map.69.refs_4_.refs_3_ = bf16[4,256,128]{2,1,0:T(8,128)(2,1)S(1)} custom-call(f32[8,128]{1,0:T(8,128)S(1)} %maximum_maximum_fusion.refs_0_.refs_1_.points_ref, bf16[4,144,128]{2,1,0:T(8,128)(2,1)S(1)} %pad_maximum_fusion.refs_1_.refs_0_), custom_call_target="tpu_custom_call" | custom-call | flops 262144000 | bytes 413696 | tf_op jit(solution)/shard_map/pallas_call | solution.py:342
  18.8 5.5 %collective-permute-done.3.refs_2_ = bf16[4,128,128]{2,1,0:T(8,128)(2,1)S(1)} collective-permute-done((bf16[4,128,128]{2,1,0:T(8,128)(2,1)S(1)}, bf16[4,128,128]{2,1,0:T(8,128)(2,1)S(1)}, u32[]{:S(2)}, u32[]{:S(2)}) %collective-permute-start.3) | collective-permute-done | bytes 131104 | tf_op jit(solution)/shard_map/ppermute | solution.py:366
  24.3 0.5 %collective-permute-start.6 = (bf16[4,144,128]{2,1,0:T(8,128)(2,1)S(1)}, bf16[4,144,128]{2,1,0:T(8,128)(2,1)S(1)}, u32[]{:S(2)}, u32[]{:S(2)}) collective-permute-start(bf16[4,144,128]{2,1,0:T(8,128)(2,1)S(1)} %collective-permute-done.5.refs_1_.refs_2_), channel_id=1, source_target_pairs={{0,2},{2,0},{4,6},{6,4},{8,10},{10,8},{12,14},{14,12},{16,18},{18,... | collective-permute-start | bytes 442376 | tf_op jit(solution)/shard_map/ppermute | solution.py:357
  24.8 0.5 shard_map.71.refs_6_.refs_5_
  25.3 0.5 shard_map.70.refs_5_.refs_4_
  25.8 0.4 shard_map.73.refs_5_
  26.3 0.5 shard_map.68.refs_7_.refs_3_
  26.8 0.5 shard_map.72.refs_4_
  27.2 5.8 %shard_map.74 = (f32[256,256]{1,0:T(8,128)S(1)}, f32[256,256]{1,0:T(8,128)S(1)}, f32[256,256]{1,0:T(8,128)S(1)}) custom-call(s32[1]{0:T(128)} %bitcast.2.refs_0_, f32[8,128]{1,0:T(8,128)S(1)} %maximum_maximum_fusion.refs_0_.refs_1_.points_ref, bf16[4,128,128]{2,1,0:T(8,128)(2,1)S(1)} %collective-permute-done.4.refs_2_, ...), custom_call_target="tpu_custom_call" | custom-call | flops 16777216 | bytes 1445892 | tf_op jit(solution)/shard_map/pallas_call | solution.py:342
  33.1 0.1 collective-permute-start.10
  33.2 1.5 %collective-permute-done.10.other_ref = f32[256,256]{1,0:T(8,128)S(1)} collective-permute-done((f32[256,256]{1,0:T(8,128)S(1)}, f32[256,256]{1,0:T(8,128)S(1)}, u32[]{:S(2)}, u32[]{:S(2)}) %collective-permute-start.10) | collective-permute-done | bytes 262176 | tf_op jit(solution)/shard_map/ppermute | solution.py:357
  34.7 3.0 %shard_map.76 = (f32[256,256]{1,0:T(8,128)S(1)}, f32[264,128]{1,0:T(8,128)S(1)}) custom-call(f32[256,256]{1,0:T(8,128)S(1)} %get-tuple-element.9.own_ref, f32[256,256]{1,0:T(8,128)S(1)} %collective-permute-done.10.other_ref), custom_call_target="tpu_custom_call" | custom-call | flops 16777216 | bytes 921600 | tf_op jit(solution)/shard_map/pallas_call | solution.py:342
  37.6 1.1 %collective-permute-start.11 = (f32[264,128]{1,0:T(8,128)S(1)}, f32[264,128]{1,0:T(8,128)S(1)}, u32[]{:S(2)}, u32[]{:S(2)}) collective-permute-start(f32[264,128]{1,0:T(8,128)S(1)} %get-tuple-element.11), channel_id=1, source_target_pairs={{0,4},{2,6},{4,0},{6,2},{8,12},{10,14},{12,8},{14,10},{16,20},{18,... | collective-permute-start | bytes 405512 | tf_op jit(solution)/shard_map/ppermute | solution.py:357
  38.8 0.4 shard_map.75
  39.2 0.8 %reshape.9 = f32[256,2,128]{2,1,0:T(2,128)} reshape(f32[256,256]{1,0:T(8,128)S(1)} %shard_map.75) | data formatting | bytes 524288 | tf_op jit(solution)/shard_map/reshape | solution.py:430
  40.1 3.3 %collective-permute-done.11.other_ref = f32[264,128]{1,0:T(8,128)S(1)} collective-permute-done((f32[264,128]{1,0:T(8,128)S(1)}, f32[264,128]{1,0:T(8,128)S(1)}, u32[]{:S(2)}, u32[]{:S(2)}) %collective-permute-start.11) | collective-permute-done | bytes 135200 | tf_op jit(solution)/shard_map/ppermute | solution.py:357
  43.3 5.7 %shard_map.77 = f32[256,256]{1,0:T(8,128)} custom-call(f32[256,256]{1,0:T(8,128)S(1)} %get-tuple-element.10.own_ref, f32[264,128]{1,0:T(8,128)S(1)} %collective-permute-done.11.other_ref), custom_call_target="tpu_custom_call" | custom-call | flops 16777216 | bytes 659456 | tf_op jit(solution)/shard_map/pallas_call | solution.py:342
  (14 shorter events, 0.1 us)
Async XLA Ops:
  0.6 15.4 %copy-start = (f32[3,256]{1,0:T(4,128)S(1)}, f32[3,256]{1,0:T(4,128)}, u32[]{:S(2)}) copy-start(f32[3,256]{1,0:T(4,128)} %param.5) | copy-start | bytes 9220
  1.4 5.6 %collective-permute-start = (bf16[1,144,128]{2,1,0:T(8,128)(2,1)S(1)}, bf16[1,144,128]{2,1,0:T(8,128)(2,1)S(1)}, u32[]{:S(2)}, u32[]{:S(2)}) collective-permute-start(bf16[1,144,128]{2,1,0:T(8,128)(2,1)S(1)} %fusion.2), channel_id=1, source_target_pairs={{0,8},{2,10},{4,12},{6,14},{8,0},{10,2},{12,4},{14,6},{16,24},{18,... | collective-permute-start | bytes 110600 | tf_op jit(solution)/shard_map/ppermute | solution.py:357
  4.5 5.5 %collective-permute-start.1 = (bf16[1,144,128]{2,1,0:T(8,128)(2,1)S(1)}, bf16[1,144,128]{2,1,0:T(8,128)(2,1)S(1)}, u32[]{:S(2)}, u32[]{:S(2)}) collective-permute-start(bf16[1,144,128]{2,1,0:T(8,128)(2,1)S(1)} %fusion.2), channel_id=1, source_target_pairs={{0,16},{2,18},{4,20},{6,22},{8,24},{10,26},{12,28},{14,30},{16,0},... | collective-permute-start | bytes 110600 | tf_op jit(solution)/shard_map/ppermute | solution.py:357
  7.1 5.8 %collective-permute-start.2 = (bf16[1,144,128]{2,1,0:T(8,128)(2,1)S(1)}, bf16[1,144,128]{2,1,0:T(8,128)(2,1)S(1)}, u32[]{:S(2)}, u32[]{:S(2)}) collective-permute-start(bf16[1,144,128]{2,1,0:T(8,128)(2,1)S(1)} %fusion.2), channel_id=1, source_target_pairs={{0,24},{2,26},{4,28},{6,30},{8,16},{10,18},{12,20},{14,22},{16,8},... | collective-permute-start | bytes 110600 | tf_op jit(solution)/shard_map/ppermute | solution.py:357
  12.9 5.1 %collective-permute-start.8 = (bf16[4,128,128]{2,1,0:T(8,128)(2,1)S(1)}, bf16[4,128,128]{2,1,0:T(8,128)(2,1)S(1)}, u32[]{:S(2)}, u32[]{:S(2)}) collective-permute-start(bf16[4,128,128]{2,1,0:T(8,128)(2,1)S(1)} %slice.4), channel_id=1, source_target_pairs={{0,1},{1,0},{2,3},{3,2},{4,5},{5,4},{6,7},{7,6},{8,9},{9,8},{10,11... | collective-permute-start | bytes 393224 | tf_op jit(solution)/shard_map/ppermute | solution.py:360
  16.0 8.3 %collective-permute-start.5 = (bf16[4,144,128]{2,1,0:T(8,128)(2,1)S(1)}, bf16[4,144,128]{2,1,0:T(8,128)(2,1)S(1)}, u32[]{:S(2)}, u32[]{:S(2)}) collective-permute-start(bf16[4,144,128]{2,1,0:T(8,128)(2,1)S(1)} %pad_maximum_fusion.refs_1_.refs_0_), channel_id=1, source_target_pairs={{0,4},{2,6},{4,0},{6,2},{8,12},{10,14},{12,8},{14,10},{16,20},{18,... | collective-permute-start | bytes 442376 | tf_op jit(solution)/shard_map/ppermute | solution.py:357
  17.5 7.8 %collective-permute-start.7 = (bf16[4,144,128]{2,1,0:T(8,128)(2,1)S(1)}, bf16[4,144,128]{2,1,0:T(8,128)(2,1)S(1)}, u32[]{:S(2)}, u32[]{:S(2)}) collective-permute-start(bf16[4,144,128]{2,1,0:T(8,128)(2,1)S(1)} %pad_maximum_fusion.refs_1_.refs_0_), channel_id=1, source_target_pairs={{0,2},{2,0},{4,6},{6,4},{8,10},{10,8},{12,14},{14,12},{16,18},{18,... | collective-permute-start | bytes 442376 | tf_op jit(solution)/shard_map/ppermute | solution.py:357
  17.5 6.8 %collective-permute-start.3 = (bf16[4,128,128]{2,1,0:T(8,128)(2,1)S(1)}, bf16[4,128,128]{2,1,0:T(8,128)(2,1)S(1)}, u32[]{:S(2)}, u32[]{:S(2)}) collective-permute-start(bf16[4,128,128]{2,1,0:T(8,128)(2,1)S(1)} %slice.4), channel_id=1, source_target_pairs={{0,5},{1,4},{2,7},{3,6},{4,1},{5,0},{6,3},{7,2},{8,13},{9,12},{10,... | collective-permute-start | bytes 393224 | tf_op jit(solution)/shard_map/ppermute | solution.py:366
  18.0 7.8 %collective-permute-start.9 = (bf16[4,128,128]{2,1,0:T(8,128)(2,1)S(1)}, bf16[4,128,128]{2,1,0:T(8,128)(2,1)S(1)}, u32[]{:S(2)}, u32[]{:S(2)}) collective-permute-start(bf16[4,128,128]{2,1,0:T(8,128)(2,1)S(1)} %collective-permute-done.8.refs_0_), channel_id=1, source_target_pairs={{0,2},{2,0},{4,6},{6,4},{8,10},{10,8},{12,14},{14,12},{16,18},{18,... | collective-permute-start | bytes 393224 | tf_op jit(solution)/shard_map/ppermute | solution.py:357
  24.3 2.9 %collective-permute-start.4 = (bf16[4,128,128]{2,1,0:T(8,128)(2,1)S(1)}, bf16[4,128,128]{2,1,0:T(8,128)(2,1)S(1)}, u32[]{:S(2)}, u32[]{:S(2)}) collective-permute-start(bf16[4,128,128]{2,1,0:T(8,128)(2,1)S(1)} %collective-permute-done.3.refs_2_), channel_id=1, source_target_pairs={{0,2},{2,0},{4,6},{6,4},{8,10},{10,8},{12,14},{14,12},{16,18},{18,... | collective-permute-start | bytes 393224 | tf_op jit(solution)/shard_map/ppermute | solution.py:357
  24.3 1.9 %collective-permute-start.6 = (bf16[4,144,128]{2,1,0:T(8,128)(2,1)S(1)}, bf16[4,144,128]{2,1,0:T(8,128)(2,1)S(1)}, u32[]{:S(2)}, u32[]{:S(2)}) collective-permute-start(bf16[4,144,128]{2,1,0:T(8,128)(2,1)S(1)} %collective-permute-done.5.refs_1_.refs_2_), channel_id=1, source_target_pairs={{0,2},{2,0},{4,6},{6,4},{8,10},{10,8},{12,14},{14,12},{16,18},{18,... | collective-permute-start | bytes 442376 | tf_op jit(solution)/shard_map/ppermute | solution.py:357
  33.1 1.6 %collective-permute-start.10 = (f32[256,256]{1,0:T(8,128)S(1)}, f32[256,256]{1,0:T(8,128)S(1)}, u32[]{:S(2)}, u32[]{:S(2)}) collective-permute-start(f32[256,256]{1,0:T(8,128)S(1)} %get-tuple-element.9.own_ref), channel_id=1, source_target_pairs={{0,2},{2,0},{4,6},{6,4},{8,10},{10,8},{12,14},{14,12},{16,18},{18,... | collective-permute-start | bytes 786440 | tf_op jit(solution)/shard_map/ppermute | solution.py:357
  37.6 5.7 %collective-permute-start.11 = (f32[264,128]{1,0:T(8,128)S(1)}, f32[264,128]{1,0:T(8,128)S(1)}, u32[]{:S(2)}, u32[]{:S(2)}) collective-permute-start(f32[264,128]{1,0:T(8,128)S(1)} %get-tuple-element.11), channel_id=1, source_target_pairs={{0,4},{2,6},{4,0},{6,2},{8,12},{10,14},{12,8},{14,10},{16,20},{18,... | collective-permute-start | bytes 405512 | tf_op jit(solution)/shard_map/ppermute | solution.py:357

commit v8 on v7

--- a/solution.py
+++ b/solution.py
@@ -254,7 +254,7 @@
 def sample_body(groups, *refs):
     out_ref = refs[-1]
     high, n = out_ref.shape
-    total = jnp.zeros((high, n), F32)
+    total = refs[2 * groups][...] if len(refs) == 2 * groups + 2 else jnp.zeros((high, n), F32)
     for g in range(groups):
         total = accumulate(refs[g], refs[groups + g], high, total)
     out_ref[...] = total
@@ -411,10 +411,14 @@
                 for x in (near, far):
                     values += evaluate([x])
         count = len(held) - (o == probe_size - 1)
-        samples += call(
-            lambda *refs, count=count: sample_body(count, *refs), [block],
-            [*held[:count], *values[:count]], flops=200 * high * n * n,
-        )
+        cuts = (0, 2, count) if o == 0 and count > 2 else (0, count)
+        total = []
+        for low, top in zip(cuts, cuts[1:]):
+            total = call(
+                lambda *refs, count=top - low: sample_body(count, *refs), [block],
+                [*held[low:top], *values[low:top], *total], flops=200 * high * n * n,
+            )
+        samples += total
     scratch = [pltpu.VMEM((n, n), F32)]
     h, m, t = call(
         lambda *refs: leaf_body(probe_size, *refs), [square] * 3,

time: 49.3 us -> 48.7 us (0.988)
  waiting for transfers between devices: 16.1 us -> 15.6 us
    ppermute x1, waiting for transfers between devices: 0.01 us -> 6.15 us  [flip(): return lax.ppermute(value, 'probe', pairs)]
    ppermute x1, waiting for transfers between devices: 5.53 us -> 0.01 us  [flip(): return lax.ppermute(value, ('rows', 'probe'), pairs)]
    ppermute x10, waiting for transfers between devices: 10.6 us -> 9.46 us  [flip(): return lax.ppermute(value, 'rows', pairs)]
    pallas_call x10 -> x11, Pallas kernels: 17.8 us -> 17.9 us  [call(): pl.pallas_call(body, out_shape=list(outs), in_specs=list(specs or [VMEM]...]
where the time goes in v8:
time: 48.7 us; the launch traced here: 48.5 us
  Pallas kernels  17.9 us (37%)
  waiting for transfers between devices  15.6 us (32%)
  starting transfers between devices  10.9 us (22%)
  between operations  2.06 us (4%)
  local copies, waits for them, and re-layouts  1.08 us (2%)
  other arithmetic  0.88 us (2%)
    pallas_call x11, Pallas kernels, call(): pl.pallas_call(body, out_shape=list(outs), in_specs=list(specs or [VMEM]...  17.9 us
    ppermute x10, waiting for transfers between devices, flip(): return lax.ppermute(value, 'rows', pairs)  9.46 us
    ppermute x10, starting transfers between devices, flip(): return lax.ppermute(value, 'rows', pairs)  8.89 us
    ppermute x1, waiting for transfers between devices, flip(): return lax.ppermute(value, 'probe', pairs)  6.15 us
    ppermute x1, starting transfers between devices, flip(): return lax.ppermute(value, 'probe', pairs)  1.58 us
  transfers between devices with their start and end apart: 12, of which 5 were waited for; matrix products, arithmetic and copies ran while one was open for 2% of the time, Pallas kernels for 7%

profile of v8, /device:TPU:0, one launch (start us, length us, event | category | flops | bytes accessed | tf_op | source)
XLA Modules:
  0.0 48.5 jit_solution(14522115587415832151)
XLA Ops:
  0.6 0.0 copy-start
  0.6 0.8 %fusion.2 = bf16[1,144,128]{2,1,0:T(8,128)(2,1)S(1)} fusion(bf16[3,128]{1,0:T(4,128)(2,1)} %param.6, bf16[128,128]{1,0:T(8,128)(2,1)} %param.7), kind=kLoop, calls=%fused_computation.4 | loop fusion | flops 110592 | bytes 70400 | tf_op jit(solution)/shard_map/broadcast_in_dim | solution.py:389
  1.4 3.1 %collective-permute-start = (bf16[1,144,128]{2,1,0:T(8,128)(2,1)S(1)}, bf16[1,144,128]{2,1,0:T(8,128)(2,1)S(1)}, u32[]{:S(2)}, u32[]{:S(2)}) collective-permute-start(bf16[1,144,128]{2,1,0:T(8,128)(2,1)S(1)} %fusion.2), channel_id=1, source_target_pairs={{0,8},{2,10},{4,12},{6,14},{8,0},{10,2},{12,4},{14,6},{16,24},{18,... | collective-permute-start | bytes 110600 | tf_op jit(solution)/shard_map/ppermute | solution.py:357
  4.5 2.6 %collective-permute-start.1 = (bf16[1,144,128]{2,1,0:T(8,128)(2,1)S(1)}, bf16[1,144,128]{2,1,0:T(8,128)(2,1)S(1)}, u32[]{:S(2)}, u32[]{:S(2)}) collective-permute-start(bf16[1,144,128]{2,1,0:T(8,128)(2,1)S(1)} %fusion.2), channel_id=1, source_target_pairs={{0,16},{2,18},{4,20},{6,22},{8,24},{10,26},{12,28},{14,30},{16,0},... | collective-permute-start | bytes 110600 | tf_op jit(solution)/shard_map/ppermute | solution.py:357
  8.4 0.1 pad.12.clone
  8.5 0.1 pad.13.clone
  8.5 0.1 pad.14.clone
  8.6 1.4 %collective-permute-done.1 = bf16[1,144,128]{2,1,0:T(8,128)(2,1)S(1)} collective-permute-done((bf16[1,144,128]{2,1,0:T(8,128)(2,1)S(1)}, bf16[1,144,128]{2,1,0:T(8,128)(2,1)S(1)}, u32[]{:S(2)}, u32[]{:S(2)}) %collective-permute-start.1) | collective-permute-done | bytes 36896 | tf_op jit(solution)/shard_map/ppermute | solution.py:357
  10.0 2.8 %collective-permute-done.2 = bf16[1,144,128]{2,1,0:T(8,128)(2,1)S(1)} collective-permute-done((bf16[1,144,128]{2,1,0:T(8,128)(2,1)S(1)}, bf16[1,144,128]{2,1,0:T(8,128)(2,1)S(1)}, u32[]{:S(2)}, u32[]{:S(2)}) %collective-permute-start.2) | collective-permute-done | bytes 36896 | tf_op jit(solution)/shard_map/ppermute | solution.py:357
  12.9 1.6 %collective-permute-start.5 = (bf16[4,144,128]{2,1,0:T(8,128)(2,1)S(1)}, bf16[4,144,128]{2,1,0:T(8,128)(2,1)S(1)}, u32[]{:S(2)}, u32[]{:S(2)}) collective-permute-start(bf16[4,144,128]{2,1,0:T(8,128)(2,1)S(1)} %pad_maximum_fusion.refs_1_.refs_0_), channel_id=1, source_target_pairs={{0,4},{2,6},{4,0},{6,2},{8,12},{10,14},{12,8},{14,10},{16,20},{18,... | collective-permute-start | bytes 442376 | tf_op jit(solution)/shard_map/ppermute | solution.py:357
  14.4 1.6 %collective-permute-start.8 = (bf16[4,128,128]{2,1,0:T(8,128)(2,1)S(1)}, bf16[4,128,128]{2,1,0:T(8,128)(2,1)S(1)}, u32[]{:S(2)}, u32[]{:S(2)}) collective-permute-start(bf16[4,128,128]{2,1,0:T(8,128)(2,1)S(1)} %slice.4), channel_id=1, source_target_pairs={{0,1},{1,0},{2,3},{3,2},{4,5},{5,4},{6,7},{7,6},{8,9},{9,8},{10,11... | collective-permute-start | bytes 393224 | tf_op jit(solution)/shard_map/ppermute | solution.py:360
  16.0 0.5 collective-permute-start.3
  16.5 0.1 maximum_maximum_fusion.refs_0_.refs_1_.points_ref
  16.6 0.5 %shard_map.70.refs_2_.refs_3_ = bf16[4,256,128]{2,1,0:T(8,128)(2,1)S(1)} custom-call(f32[8,128]{1,0:T(8,128)S(1)} %maximum_maximum_fusion.refs_0_.refs_1_.points_ref, bf16[4,144,128]{2,1,0:T(8,128)(2,1)S(1)} %pad_maximum_fusion.refs_1_.refs_0_), custom_call_target="tpu_custom_call" | custom-call | flops 262144000 | bytes 413696 | tf_op jit(solution)/shard_map/pallas_call | solution.py:342
  17.1 6.1 %collective-permute-done.8.refs_0_ = bf16[4,128,128]{2,1,0:T(8,128)(2,1)S(1)} collective-permute-done((bf16[4,128,128]{2,1,0:T(8,128)(2,1)S(1)}, bf16[4,128,128]{2,1,0:T(8,128)(2,1)S(1)}, u32[]{:S(2)}, u32[]{:S(2)}) %collective-permute-start.8) | collective-permute-done | bytes 131104 | tf_op jit(solution)/shard_map/ppermute | solution.py:360
  23.2 0.5 %collective-permute-start.4 = (bf16[4,128,128]{2,1,0:T(8,128)(2,1)S(1)}, bf16[4,128,128]{2,1,0:T(8,128)(2,1)S(1)}, u32[]{:S(2)}, u32[]{:S(2)}) collective-permute-start(bf16[4,128,128]{2,1,0:T(8,128)(2,1)S(1)} %collective-permute-done.3.refs_2_), channel_id=1, source_target_pairs={{0,2},{2,0},{4,6},{6,4},{8,10},{10,8},{12,14},{14,12},{16,18},{18,... | collective-permute-start | bytes 393224 | tf_op jit(solution)/shard_map/ppermute | solution.py:357
  23.7 0.1 collective-permute-start.6
  23.8 0.5 %shard_map.69.refs_2_.refs_5_ = bf16[4,256,128]{2,1,0:T(8,128)(2,1)S(1)} custom-call(f32[8,128]{1,0:T(8,128)S(1)} %maximum_maximum_fusion.refs_0_.refs_1_.points_ref, bf16[4,144,128]{2,1,0:T(8,128)(2,1)S(1)} %collective-permute-done.5.refs_1_.refs_0_), custom_call_target="tpu_custom_call" | custom-call | flops 262144000 | bytes 413696 | tf_op jit(solution)/shard_map/pallas_call | solution.py:342
  24.3 0.5 %shard_map.71.refs_3_.refs_4_ = bf16[4,256,128]{2,1,0:T(8,128)(2,1)S(1)} custom-call(f32[8,128]{1,0:T(8,128)S(1)} %maximum_maximum_fusion.refs_0_.refs_1_.points_ref, bf16[4,144,128]{2,1,0:T(8,128)(2,1)S(1)} %collective-permute-done.7.refs_1_), custom_call_target="tpu_custom_call" | custom-call | flops 262144000 | bytes 413696 | tf_op jit(solution)/shard_map/pallas_call | solution.py:342
  24.8 0.3 shard_map.72.refs_4_
  25.1 0.4 shard_map.74.refs_5_
  25.5 0.5 %shard_map.68.refs_3_ = bf16[4,256,128]{2,1,0:T(8,128)(2,1)S(1)} custom-call(f32[8,128]{1,0:T(8,128)S(1)} %maximum_maximum_fusion.refs_0_.refs_1_.points_ref, bf16[4,144,128]{2,1,0:T(8,128)(2,1)S(1)} %collective-permute-done.6.refs_1_), custom_call_target="tpu_custom_call" | custom-call | flops 262144000 | bytes 413696 | tf_op jit(solution)/shard_map/pallas_call | solution.py:342
  26.0 0.3 shard_map.73.refs_4_
  26.4 5.8 %shard_map.75 = (f32[256,256]{1,0:T(8,128)S(1)}, f32[256,256]{1,0:T(8,128)S(1)}, f32[256,256]{1,0:T(8,128)S(1)}) custom-call(s32[1]{0:T(128)} %bitcast.2.refs_0_, f32[8,128]{1,0:T(8,128)S(1)} %maximum_maximum_fusion.refs_0_.refs_1_.points_ref, bf16[4,128,128]{2,1,0:T(8,128)(2,1)S(1)} %collective-permute-done.4.refs_2_, ...), custom_call_target="tpu_custom_call" | custom-call | flops 16777216 | bytes 1445892 | tf_op jit(solution)/shard_map/pallas_call | solution.py:342
  32.2 0.5 %collective-permute-start.10 = (f32[256,256]{1,0:T(8,128)S(1)}, f32[256,256]{1,0:T(8,128)S(1)}, u32[]{:S(2)}, u32[]{:S(2)}) collective-permute-start(f32[256,256]{1,0:T(8,128)S(1)} %get-tuple-element.9.own_ref), channel_id=1, source_target_pairs={{0,2},{2,0},{4,6},{6,4},{8,10},{10,8},{12,14},{14,12},{16,18},{18,... | collective-permute-start | bytes 786440 | tf_op jit(solution)/shard_map/ppermute | solution.py:357
  32.7 1.2 %collective-permute-done.10.other_ref = f32[256,256]{1,0:T(8,128)S(1)} collective-permute-done((f32[256,256]{1,0:T(8,128)S(1)}, f32[256,256]{1,0:T(8,128)S(1)}, u32[]{:S(2)}, u32[]{:S(2)}) %collective-permute-start.10) | collective-permute-done | bytes 262176 | tf_op jit(solution)/shard_map/ppermute | solution.py:357
  33.9 3.0 %shard_map.77 = (f32[256,256]{1,0:T(8,128)S(1)}, f32[264,128]{1,0:T(8,128)S(1)}) custom-call(f32[256,256]{1,0:T(8,128)S(1)} %get-tuple-element.9.own_ref, f32[256,256]{1,0:T(8,128)S(1)} %collective-permute-done.10.other_ref), custom_call_target="tpu_custom_call" | custom-call | flops 16777216 | bytes 921600 | tf_op jit(solution)/shard_map/pallas_call | solution.py:342
  36.8 0.6 %collective-permute-start.11 = (f32[264,128]{1,0:T(8,128)S(1)}, f32[264,128]{1,0:T(8,128)S(1)}, u32[]{:S(2)}, u32[]{:S(2)}) collective-permute-start(f32[264,128]{1,0:T(8,128)S(1)} %get-tuple-element.11), channel_id=1, source_target_pairs={{0,4},{2,6},{4,0},{6,2},{8,12},{10,14},{12,8},{14,10},{16,20},{18,... | collective-permute-start | bytes 405512 | tf_op jit(solution)/shard_map/ppermute | solution.py:357
  37.4 0.4 shard_map.76
  37.9 0.8 %reshape.9 = f32[256,2,128]{2,1,0:T(2,128)} reshape(f32[256,256]{1,0:T(8,128)S(1)} %shard_map.76) | data formatting | bytes 524288 | tf_op jit(solution)/shard_map/reshape | solution.py:434
  38.7 4.1 %collective-permute-done.11.other_ref = f32[264,128]{1,0:T(8,128)S(1)} collective-permute-done((f32[264,128]{1,0:T(8,128)S(1)}, f32[264,128]{1,0:T(8,128)S(1)}, u32[]{:S(2)}, u32[]{:S(2)}) %collective-permute-start.11) | collective-permute-done | bytes 135200 | tf_op jit(solution)/shard_map/ppermute | solution.py:357
  42.8 5.7 %shard_map.78 = f32[256,256]{1,0:T(8,128)} custom-call(f32[256,256]{1,0:T(8,128)S(1)} %get-tuple-element.10.own_ref, f32[264,128]{1,0:T(8,128)S(1)} %collective-permute-done.11.other_ref), custom_call_target="tpu_custom_call" | custom-call | flops 16777216 | bytes 659456 | tf_op jit(solution)/shard_map/pallas_call | solution.py:342
  (15 shorter events, 0.1 us)
Async XLA Ops:
  0.6 6.4 %copy-start = (f32[3,256]{1,0:T(4,128)S(1)}, f32[3,256]{1,0:T(4,128)}, u32[]{:S(2)}) copy-start(f32[3,256]{1,0:T(4,128)} %param.5) | copy-start | bytes 9220
  1.4 7.2 %collective-permute-start = (bf16[1,144,128]{2,1,0:T(8,128)(2,1)S(1)}, bf16[1,144,128]{2,1,0:T(8,128)(2,1)S(1)}, u32[]{:S(2)}, u32[]{:S(2)}) collective-permute-start(bf16[1,144,128]{2,1,0:T(8,128)(2,1)S(1)} %fusion.2), channel_id=1, source_target_pairs={{0,8},{2,10},{4,12},{6,14},{8,0},{10,2},{12,4},{14,6},{16,24},{18,... | collective-permute-start | bytes 110600 | tf_op jit(solution)/shard_map/ppermute | solution.py:357
  4.5 5.5 %collective-permute-start.1 = (bf16[1,144,128]{2,1,0:T(8,128)(2,1)S(1)}, bf16[1,144,128]{2,1,0:T(8,128)(2,1)S(1)}, u32[]{:S(2)}, u32[]{:S(2)}) collective-permute-start(bf16[1,144,128]{2,1,0:T(8,128)(2,1)S(1)} %fusion.2), channel_id=1, source_target_pairs={{0,16},{2,18},{4,20},{6,22},{8,24},{10,26},{12,28},{14,30},{16,0},... | collective-permute-start | bytes 110600 | tf_op jit(solution)/shard_map/ppermute | solution.py:357
  7.1 5.8 %collective-permute-start.2 = (bf16[1,144,128]{2,1,0:T(8,128)(2,1)S(1)}, bf16[1,144,128]{2,1,0:T(8,128)(2,1)S(1)}, u32[]{:S(2)}, u32[]{:S(2)}) collective-permute-start(bf16[1,144,128]{2,1,0:T(8,128)(2,1)S(1)} %fusion.2), channel_id=1, source_target_pairs={{0,24},{2,26},{4,28},{6,30},{8,16},{10,18},{12,20},{14,22},{16,8},... | collective-permute-start | bytes 110600 | tf_op jit(solution)/shard_map/ppermute | solution.py:357
  12.9 10.9 %collective-permute-start.5 = (bf16[4,144,128]{2,1,0:T(8,128)(2,1)S(1)}, bf16[4,144,128]{2,1,0:T(8,128)(2,1)S(1)}, u32[]{:S(2)}, u32[]{:S(2)}) collective-permute-start(bf16[4,144,128]{2,1,0:T(8,128)(2,1)S(1)} %pad_maximum_fusion.refs_1_.refs_0_), channel_id=1, source_target_pairs={{0,4},{2,6},{4,0},{6,2},{8,12},{10,14},{12,8},{14,10},{16,20},{18,... | collective-permute-start | bytes 442376 | tf_op jit(solution)/shard_map/ppermute | solution.py:357
  14.4 9.9 %collective-permute-start.7 = (bf16[4,144,128]{2,1,0:T(8,128)(2,1)S(1)}, bf16[4,144,128]{2,1,0:T(8,128)(2,1)S(1)}, u32[]{:S(2)}, u32[]{:S(2)}) collective-permute-start(bf16[4,144,128]{2,1,0:T(8,128)(2,1)S(1)} %pad_maximum_fusion.refs_1_.refs_0_), channel_id=1, source_target_pairs={{0,2},{2,0},{4,6},{6,4},{8,10},{10,8},{12,14},{14,12},{16,18},{18,... | collective-permute-start | bytes 442376 | tf_op jit(solution)/shard_map/ppermute | solution.py:357
  14.4 8.8 %collective-permute-start.8 = (bf16[4,128,128]{2,1,0:T(8,128)(2,1)S(1)}, bf16[4,128,128]{2,1,0:T(8,128)(2,1)S(1)}, u32[]{:S(2)}, u32[]{:S(2)}) collective-permute-start(bf16[4,128,128]{2,1,0:T(8,128)(2,1)S(1)} %slice.4), channel_id=1, source_target_pairs={{0,1},{1,0},{2,3},{3,2},{4,5},{5,4},{6,7},{7,6},{8,9},{9,8},{10,11... | collective-permute-start | bytes 393224 | tf_op jit(solution)/shard_map/ppermute | solution.py:360
  16.0 7.2 %collective-permute-start.3 = (bf16[4,128,128]{2,1,0:T(8,128)(2,1)S(1)}, bf16[4,128,128]{2,1,0:T(8,128)(2,1)S(1)}, u32[]{:S(2)}, u32[]{:S(2)}) collective-permute-start(bf16[4,128,128]{2,1,0:T(8,128)(2,1)S(1)} %slice.4), channel_id=1, source_target_pairs={{0,5},{1,4},{2,7},{3,6},{4,1},{5,0},{6,3},{7,2},{8,13},{9,12},{10,... | collective-permute-start | bytes 393224 | tf_op jit(solution)/shard_map/ppermute | solution.py:366
  23.2 1.9 %collective-permute-start.9 = (bf16[4,128,128]{2,1,0:T(8,128)(2,1)S(1)}, bf16[4,128,128]{2,1,0:T(8,128)(2,1)S(1)}, u32[]{:S(2)}, u32[]{:S(2)}) collective-permute-start(bf16[4,128,128]{2,1,0:T(8,128)(2,1)S(1)} %collective-permute-done.8.refs_0_), channel_id=1, source_target_pairs={{0,2},{2,0},{4,6},{6,4},{8,10},{10,8},{12,14},{14,12},{16,18},{18,... | collective-permute-start | bytes 393224 | tf_op jit(solution)/shard_map/ppermute | solution.py:357
  23.2 3.1 %collective-permute-start.4 = (bf16[4,128,128]{2,1,0:T(8,128)(2,1)S(1)}, bf16[4,128,128]{2,1,0:T(8,128)(2,1)S(1)}, u32[]{:S(2)}, u32[]{:S(2)}) collective-permute-start(bf16[4,128,128]{2,1,0:T(8,128)(2,1)S(1)} %collective-permute-done.3.refs_2_), channel_id=1, source_target_pairs={{0,2},{2,0},{4,6},{6,4},{8,10},{10,8},{12,14},{14,12},{16,18},{18,... | collective-permute-start | bytes 393224 | tf_op jit(solution)/shard_map/ppermute | solution.py:357
  23.7 1.8 %collective-permute-start.6 = (bf16[4,144,128]{2,1,0:T(8,128)(2,1)S(1)}, bf16[4,144,128]{2,1,0:T(8,128)(2,1)S(1)}, u32[]{:S(2)}, u32[]{:S(2)}) collective-permute-start(bf16[4,144,128]{2,1,0:T(8,128)(2,1)S(1)} %collective-permute-done.5.refs_1_.refs_0_), channel_id=1, source_target_pairs={{0,2},{2,0},{4,6},{6,4},{8,10},{10,8},{12,14},{14,12},{16,18},{18,... | collective-permute-start | bytes 442376 | tf_op jit(solution)/shard_map/ppermute | solution.py:357
  32.2 1.7 %collective-permute-start.10 = (f32[256,256]{1,0:T(8,128)S(1)}, f32[256,256]{1,0:T(8,128)S(1)}, u32[]{:S(2)}, u32[]{:S(2)}) collective-permute-start(f32[256,256]{1,0:T(8,128)S(1)} %get-tuple-element.9.own_ref), channel_id=1, source_target_pairs={{0,2},{2,0},{4,6},{6,4},{8,10},{10,8},{12,14},{14,12},{16,18},{18,... | collective-permute-start | bytes 786440 | tf_op jit(solution)/shard_map/ppermute | solution.py:357
  36.8 5.9 %collective-permute-start.11 = (f32[264,128]{1,0:T(8,128)S(1)}, f32[264,128]{1,0:T(8,128)S(1)}, u32[]{:S(2)}, u32[]{:S(2)}) collective-permute-start(f32[264,128]{1,0:T(8,128)S(1)} %get-tuple-element.11), channel_id=1, source_target_pairs={{0,4},{2,6},{4,0},{6,2},{8,12},{10,14},{12,8},{14,10},{16,20},{18,... | collective-permute-start | bytes 405512 | tf_op jit(solution)/shard_map/ppermute | solution.py:357

commit v9 on v8

--- a/solution.py
+++ b/solution.py
@@ -42,14 +42,6 @@
     return mxu(lh, rh, dims) + (mxu(lh, rl, dims) + mxu(ll, rh, dims))
 
 
-def rows_gram(value):
-    n = value.shape[1]
-    high, low = split_bf16(value)
-    turned = jnp.concatenate([high, low], axis=1).T
-    first = mxu(turned, high, NN)
-    return first[:n] + (first[n:] + mxu(turned[:n], low, NN))
-
-
 def pick_lane(tile, lane):
     where = jnp.full(tile.shape, lane, jnp.int32)
     return jnp.take_along_axis(tile, where, axis=1, mode="promise_in_bounds")
@@ -59,7 +51,7 @@
     return jnp.broadcast_to(tile[row : row + 1, :], tile.shape)
 
 
-def sweep(t_ref):
+def sweep(t_ref, begin=0, stop=None):
     n = t_ref.shape[0]
     tiles = n // LANES
     steps = PANEL // 8
@@ -67,7 +59,7 @@
     row = lax.broadcasted_iota(jnp.int32, (8, LANES), 0)
     along_lanes = [jnp.zeros((8, LANES), F32) for _ in range(tiles)]
     along_rows = []
-    for start in range(0, n, PANEL):
+    for start in range(begin, stop or n, PANEL):
         at, low = divmod(start, LANES)
         block = [
             [t_ref[start + 8 * i : start + 8 * i + 8, LANES * t : LANES * (t + 1)] for t in range(tiles)]
@@ -261,7 +253,7 @@
 
 
 def leaf_body(blocks, place_ref, points_ref, probe_ref, kernel_ref, *refs):
-    h_ref, m_ref, t_ref = refs[blocks:]
+    h_ref, m_ref, a_ref = refs[blocks:]
     n = h_ref.shape[0]
     rows, cols = grids(n)
     high = n // blocks
@@ -275,10 +267,24 @@
     inside = (cols - jnp.where(cols >= half, half, 0)).astype(F32) < points_ref[3:4, 0:1]
     matrix = jnp.where(inside, m_ref[...], 0.0)
     m_ref[...] = matrix
-    shift, by_row, by_col = factorize(dot3(matrix, matrix, NT), t_ref)
-    in_rank = rows.astype(F32) < points_ref[4:5, 0:1]
-    value = jnp.where(in_rank, projected_rows(t_ref, by_row, by_col), 0.0)
-    h_ref[...] = rows_gram(value) * shift
+    gram = dot3(matrix, matrix, NT)
+    shift = trace(gram) / n
+    scaled = gram / shift
+    unit = jnp.where(rows == cols, 1.0, 0.0)
+    a_ref[...] = scaled + unit
+    rank = points_ref[4:5, 0:1]
+    kept_row = rows.astype(F32) < rank
+    kept_col = cols.astype(F32) < rank
+    inner = jnp.where(kept_row & kept_col, scaled, 0.0)
+    turned = inverse(inner + unit)
+    outer = jnp.where(kept_row & (cols.astype(F32) >= rank), scaled, 0.0)
+    solved = jnp.where(kept_row, jnp.where(kept_col, unit - turned, dot3(turned, outer, NN)), 0.0)
+    h_ref[...] = dot3(jnp.where(kept_col, scaled, 0.0), solved, NN) * shift
+
+
+def sweep_body(begin, stop, a_ref, t_ref):
+    t_ref[...] = a_ref[...]
+    sweep(t_ref, begin, stop)
 
 
 def basis_body(points_ref, t_ref, m_ref, b_ref):
@@ -426,6 +432,12 @@
         specs=[SMEM] + [VMEM] * (3 + len(samples)), flops=n**3,
     )
     other = flip(h, 1)
+    cuts = (0, PANEL, n)
+    for begin, stop in zip(cuts, cuts[1:]):
+        t = call(
+            lambda *refs, begin=begin, stop=stop: sweep_body(begin, stop, *refs), [square], [t],
+            flops=200 * n**3,
+        )[0]
     basis = call(basis_body, [square], [points, t, m], flops=60 * n**3)[0]
     packed = jax.ShapeDtypeStruct((n + 8, n // 2), F32)
     h, sent = call(node_body, [square, packed], [h, other], flops=n**3)

time: 48.7 us -> 47.3 us (0.971)
  waiting for transfers between devices: 15.6 us -> 10.9 us
  Pallas kernels: 17.9 us -> 21.2 us
    ppermute x10, waiting for transfers between devices: 9.46 us -> 4.73 us  [flip(): return lax.ppermute(value, 'rows', pairs)]
    pallas_call x11 -> x13, Pallas kernels: 17.9 us -> 21.2 us  [call(): pl.pallas_call(body, out_shape=list(outs), in_specs=list(specs or [VMEM]...]
  transfers between devices with their start and end apart: 12 -> 12, of which waited for: 5 -> 4; matrix products, arithmetic and copies ran while one was open for 2% -> 2% of each run, Pallas kernels for 7% -> 17%
where the time goes in v9:
time: 47.3 us; the launch traced here: 47.1 us
  Pallas kernels  21.2 us (45%)
  starting transfers between devices  10.9 us (23%)
  waiting for transfers between devices  10.9 us (23%)
  between operations  2.08 us (4%)
  local copies, waits for them, and re-layouts  1.08 us (2%)
  other arithmetic  0.88 us (2%)
    pallas_call x13, Pallas kernels, call(): pl.pallas_call(body, out_shape=list(outs), in_specs=list(specs or [VMEM]...  21.2 us
    ppermute x10, starting transfers between devices, flip(): return lax.ppermute(value, 'rows', pairs)  8.89 us
    ppermute x1, waiting for transfers between devices, flip(): return lax.ppermute(value, 'probe', pairs)  6.15 us
    ppermute x10, waiting for transfers between devices, flip(): return lax.ppermute(value, 'rows', pairs)  4.73 us
    ppermute x1, starting transfers between devices, flip(): return lax.ppermute(value, 'probe', pairs)  1.58 us
  transfers between devices with their start and end apart: 12, of which 4 were waited for; matrix products, arithmetic and copies ran while one was open for 2% of the time, Pallas kernels for 17%

profile of v9, /device:TPU:0, one launch (start us, length us, event | category | flops | bytes accessed | tf_op | source)
XLA Modules:
  0.0 47.1 jit_solution(4853388982018731259)
XLA Ops:
  0.6 0.8 %fusion.2 = bf16[1,144,128]{2,1,0:T(8,128)(2,1)S(1)} fusion(bf16[3,128]{1,0:T(4,128)(2,1)} %param.6, bf16[128,128]{1,0:T(8,128)(2,1)} %param.7), kind=kLoop, calls=%fused_computation.4 | loop fusion | flops 110592 | bytes 70400 | tf_op jit(solution)/shard_map/broadcast_in_dim | solution.py:395
  1.4 3.1 %collective-permute-start = (bf16[1,144,128]{2,1,0:T(8,128)(2,1)S(1)}, bf16[1,144,128]{2,1,0:T(8,128)(2,1)S(1)}, u32[]{:S(2)}, u32[]{:S(2)}) collective-permute-start(bf16[1,144,128]{2,1,0:T(8,128)(2,1)S(1)} %fusion.2), channel_id=1, source_target_pairs={{0,8},{2,10},{4,12},{6,14},{8,0},{10,2},{12,4},{14,6},{16,24},{18,... | collective-permute-start | bytes 110600 | tf_op jit(solution)/shard_map/ppermute | solution.py:363
  4.5 2.6 %collective-permute-start.1 = (bf16[1,144,128]{2,1,0:T(8,128)(2,1)S(1)}, bf16[1,144,128]{2,1,0:T(8,128)(2,1)S(1)}, u32[]{:S(2)}, u32[]{:S(2)}) collective-permute-start(bf16[1,144,128]{2,1,0:T(8,128)(2,1)S(1)} %fusion.2), channel_id=1, source_target_pairs={{0,16},{2,18},{4,20},{6,22},{8,24},{10,26},{12,28},{14,30},{16,0},... | collective-permute-start | bytes 110600 | tf_op jit(solution)/shard_map/ppermute | solution.py:363
  8.4 0.1 pad.12.clone
  8.5 0.1 pad.13.clone
  8.5 0.1 pad.14.clone
  8.6 1.4 %collective-permute-done.1 = bf16[1,144,128]{2,1,0:T(8,128)(2,1)S(1)} collective-permute-done((bf16[1,144,128]{2,1,0:T(8,128)(2,1)S(1)}, bf16[1,144,128]{2,1,0:T(8,128)(2,1)S(1)}, u32[]{:S(2)}, u32[]{:S(2)}) %collective-permute-start.1) | collective-permute-done | bytes 36896 | tf_op jit(solution)/shard_map/ppermute | solution.py:363
  10.0 2.8 %collective-permute-done.2 = bf16[1,144,128]{2,1,0:T(8,128)(2,1)S(1)} collective-permute-done((bf16[1,144,128]{2,1,0:T(8,128)(2,1)S(1)}, bf16[1,144,128]{2,1,0:T(8,128)(2,1)S(1)}, u32[]{:S(2)}, u32[]{:S(2)}) %collective-permute-start.2) | collective-permute-done | bytes 36896 | tf_op jit(solution)/shard_map/ppermute | solution.py:363
  12.9 1.6 %collective-permute-start.5 = (bf16[4,144,128]{2,1,0:T(8,128)(2,1)S(1)}, bf16[4,144,128]{2,1,0:T(8,128)(2,1)S(1)}, u32[]{:S(2)}, u32[]{:S(2)}) collective-permute-start(bf16[4,144,128]{2,1,0:T(8,128)(2,1)S(1)} %pad_maximum_fusion.refs_1_.refs_0_), channel_id=1, source_target_pairs={{0,4},{2,6},{4,0},{6,2},{8,12},{10,14},{12,8},{14,10},{16,20},{18,... | collective-permute-start | bytes 442376 | tf_op jit(solution)/shard_map/ppermute | solution.py:363
  14.4 1.6 %collective-permute-start.8 = (bf16[4,128,128]{2,1,0:T(8,128)(2,1)S(1)}, bf16[4,128,128]{2,1,0:T(8,128)(2,1)S(1)}, u32[]{:S(2)}, u32[]{:S(2)}) collective-permute-start(bf16[4,128,128]{2,1,0:T(8,128)(2,1)S(1)} %slice.4), channel_id=1, source_target_pairs={{0,1},{1,0},{2,3},{3,2},{4,5},{5,4},{6,7},{7,6},{8,9},{9,8},{10,11... | collective-permute-start | bytes 393224 | tf_op jit(solution)/shard_map/ppermute | solution.py:366
  16.0 0.5 %collective-permute-start.3 = (bf16[4,128,128]{2,1,0:T(8,128)(2,1)S(1)}, bf16[4,128,128]{2,1,0:T(8,128)(2,1)S(1)}, u32[]{:S(2)}, u32[]{:S(2)}) collective-permute-start(bf16[4,128,128]{2,1,0:T(8,128)(2,1)S(1)} %slice.4), channel_id=1, source_target_pairs={{0,5},{1,4},{2,7},{3,6},{4,1},{5,0},{6,3},{7,2},{8,13},{9,12},{10,... | collective-permute-start | bytes 393224 | tf_op jit(solution)/shard_map/ppermute | solution.py:372
  16.5 0.1 maximum_maximum_fusion.refs_0_.refs_1_.points_ref
  16.6 0.5 %shard_map.70.refs_2_.refs_3_ = bf16[4,256,128]{2,1,0:T(8,128)(2,1)S(1)} custom-call(f32[8,128]{1,0:T(8,128)S(1)} %maximum_maximum_fusion.refs_0_.refs_1_.points_ref, bf16[4,144,128]{2,1,0:T(8,128)(2,1)S(1)} %pad_maximum_fusion.refs_1_.refs_0_), custom_call_target="tpu_custom_call" | custom-call | flops 262144000 | bytes 413696 | tf_op jit(solution)/shard_map/pallas_call | solution.py:348
  17.1 6.1 %collective-permute-done.8.refs_0_ = bf16[4,128,128]{2,1,0:T(8,128)(2,1)S(1)} collective-permute-done((bf16[4,128,128]{2,1,0:T(8,128)(2,1)S(1)}, bf16[4,128,128]{2,1,0:T(8,128)(2,1)S(1)}, u32[]{:S(2)}, u32[]{:S(2)}) %collective-permute-start.8) | collective-permute-done | bytes 131104 | tf_op jit(solution)/shard_map/ppermute | solution.py:366
  23.2 0.5 %collective-permute-start.4 = (bf16[4,128,128]{2,1,0:T(8,128)(2,1)S(1)}, bf16[4,128,128]{2,1,0:T(8,128)(2,1)S(1)}, u32[]{:S(2)}, u32[]{:S(2)}) collective-permute-start(bf16[4,128,128]{2,1,0:T(8,128)(2,1)S(1)} %collective-permute-done.3.refs_2_), channel_id=1, source_target_pairs={{0,2},{2,0},{4,6},{6,4},{8,10},{10,8},{12,14},{14,12},{16,18},{18,... | collective-permute-start | bytes 393224 | tf_op jit(solution)/shard_map/ppermute | solution.py:363
  23.7 0.1 collective-permute-start.6
  23.8 0.5 %shard_map.69.refs_2_.refs_5_ = bf16[4,256,128]{2,1,0:T(8,128)(2,1)S(1)} custom-call(f32[8,128]{1,0:T(8,128)S(1)} %maximum_maximum_fusion.refs_0_.refs_1_.points_ref, bf16[4,144,128]{2,1,0:T(8,128)(2,1)S(1)} %collective-permute-done.5.refs_1_.refs_0_), custom_call_target="tpu_custom_call" | custom-call | flops 262144000 | bytes 413696 | tf_op jit(solution)/shard_map/pallas_call | solution.py:348
  24.3 0.5 %shard_map.71.refs_3_.refs_4_ = bf16[4,256,128]{2,1,0:T(8,128)(2,1)S(1)} custom-call(f32[8,128]{1,0:T(8,128)S(1)} %maximum_maximum_fusion.refs_0_.refs_1_.points_ref, bf16[4,144,128]{2,1,0:T(8,128)(2,1)S(1)} %collective-permute-done.7.refs_1_), custom_call_target="tpu_custom_call" | custom-call | flops 262144000 | bytes 413696 | tf_op jit(solution)/shard_map/pallas_call | solution.py:348
  24.8 0.3 shard_map.72.refs_4_
  25.1 0.4 shard_map.74.refs_5_
  25.5 0.5 %shard_map.68.refs_3_ = bf16[4,256,128]{2,1,0:T(8,128)(2,1)S(1)} custom-call(f32[8,128]{1,0:T(8,128)S(1)} %maximum_maximum_fusion.refs_0_.refs_1_.points_ref, bf16[4,144,128]{2,1,0:T(8,128)(2,1)S(1)} %collective-permute-done.6.refs_1_), custom_call_target="tpu_custom_call" | custom-call | flops 262144000 | bytes 413696 | tf_op jit(solution)/shard_map/pallas_call | solution.py:348
  26.0 0.3 shard_map.73.refs_4_
  26.4 4.2 %shard_map.75 = (f32[256,256]{1,0:T(8,128)S(1)}, f32[256,256]{1,0:T(8,128)S(1)}, f32[256,256]{1,0:T(8,128)S(1)}) custom-call(s32[1]{0:T(128)} %bitcast.2.refs_0_, f32[8,128]{1,0:T(8,128)S(1)} %maximum_maximum_fusion.refs_0_.refs_1_.points_ref, bf16[4,128,128]{2,1,0:T(8,128)(2,1)S(1)} %collective-permute-done.4.refs_2_, ...), custom_call_target="tpu_custom_call" | custom-call | flops 16777216 | bytes 1445892 | tf_op jit(solution)/shard_map/pallas_call | solution.py:348
  30.6 0.5 %collective-permute-start.10 = (f32[256,256]{1,0:T(8,128)S(1)}, f32[256,256]{1,0:T(8,128)S(1)}, u32[]{:S(2)}, u32[]{:S(2)}) collective-permute-start(f32[256,256]{1,0:T(8,128)S(1)} %get-tuple-element.9.own_ref), channel_id=1, source_target_pairs={{0,2},{2,0},{4,6},{6,4},{8,10},{10,8},{12,14},{14,12},{16,18},{18,... | collective-permute-start | bytes 786440 | tf_op jit(solution)/shard_map/ppermute | solution.py:363
  31.1 1.3 %shard_map.76.refs_0_ = f32[256,256]{1,0:T(8,128)S(1)} custom-call(f32[256,256]{1,0:T(8,128)S(1)} %get-tuple-element.7.refs_0_), custom_call_target="tpu_custom_call" | custom-call | flops 3355443200 | bytes 524288 | tf_op jit(solution)/shard_map/pallas_call | solution.py:348
  32.4 3.0 %shard_map.79 = (f32[256,256]{1,0:T(8,128)S(1)}, f32[264,128]{1,0:T(8,128)S(1)}) custom-call(f32[256,256]{1,0:T(8,128)S(1)} %get-tuple-element.9.own_ref, f32[256,256]{1,0:T(8,128)S(1)} %collective-permute-done.10.other_ref), custom_call_target="tpu_custom_call" | custom-call | flops 16777216 | bytes 921600 | tf_op jit(solution)/shard_map/pallas_call | solution.py:348
  35.3 0.6 %collective-permute-start.11 = (f32[264,128]{1,0:T(8,128)S(1)}, f32[264,128]{1,0:T(8,128)S(1)}, u32[]{:S(2)}, u32[]{:S(2)}) collective-permute-start(f32[264,128]{1,0:T(8,128)S(1)} %get-tuple-element.11), channel_id=1, source_target_pairs={{0,4},{2,6},{4,0},{6,2},{8,12},{10,14},{12,8},{14,10},{16,20},{18,... | collective-permute-start | bytes 405512 | tf_op jit(solution)/shard_map/ppermute | solution.py:363
  35.9 3.5 %shard_map.77.t_ref = f32[256,256]{1,0:T(8,128)S(1)} custom-call(f32[256,256]{1,0:T(8,128)S(1)} %shard_map.76.refs_0_), custom_call_target="tpu_custom_call" | custom-call | flops 3355443200 | bytes 524288 | tf_op jit(solution)/shard_map/pallas_call | solution.py:348
  39.4 0.4 shard_map.78
  39.8 0.8 %reshape.9 = f32[256,2,128]{2,1,0:T(2,128)} reshape(f32[256,256]{1,0:T(8,128)S(1)} %shard_map.78) | data formatting | bytes 524288 | tf_op jit(solution)/shard_map/reshape | solution.py:446
  40.7 0.5 %collective-permute-done.11.other_ref = f32[264,128]{1,0:T(8,128)S(1)} collective-permute-done((f32[264,128]{1,0:T(8,128)S(1)}, f32[264,128]{1,0:T(8,128)S(1)}, u32[]{:S(2)}, u32[]{:S(2)}) %collective-permute-start.11) | collective-permute-done | bytes 135200 | tf_op jit(solution)/shard_map/ppermute | solution.py:363
  41.2 5.9 %shard_map.80 = f32[256,256]{1,0:T(8,128)} custom-call(f32[256,256]{1,0:T(8,128)S(1)} %get-tuple-element.10.own_ref, f32[264,128]{1,0:T(8,128)S(1)} %collective-permute-done.11.other_ref), custom_call_target="tpu_custom_call" | custom-call | flops 16777216 | bytes 659456 | tf_op jit(solution)/shard_map/pallas_call | solution.py:348
  (17 shorter events, 0.1 us)
Async XLA Ops:
  0.6 6.4 %copy-start = (f32[3,256]{1,0:T(4,128)S(1)}, f32[3,256]{1,0:T(4,128)}, u32[]{:S(2)}) copy-start(f32[3,256]{1,0:T(4,128)} %param.5) | copy-start | bytes 9220
  1.4 7.2 %collective-permute-start = (bf16[1,144,128]{2,1,0:T(8,128)(2,1)S(1)}, bf16[1,144,128]{2,1,0:T(8,128)(2,1)S(1)}, u32[]{:S(2)}, u32[]{:S(2)}) collective-permute-start(bf16[1,144,128]{2,1,0:T(8,128)(2,1)S(1)} %fusion.2), channel_id=1, source_target_pairs={{0,8},{2,10},{4,12},{6,14},{8,0},{10,2},{12,4},{14,6},{16,24},{18,... | collective-permute-start | bytes 110600 | tf_op jit(solution)/shard_map/ppermute | solution.py:363
  4.5 5.5 %collective-permute-start.1 = (bf16[1,144,128]{2,1,0:T(8,128)(2,1)S(1)}, bf16[1,144,128]{2,1,0:T(8,128)(2,1)S(1)}, u32[]{:S(2)}, u32[]{:S(2)}) collective-permute-start(bf16[1,144,128]{2,1,0:T(8,128)(2,1)S(1)} %fusion.2), channel_id=1, source_target_pairs={{0,16},{2,18},{4,20},{6,22},{8,24},{10,26},{12,28},{14,30},{16,0},... | collective-permute-start | bytes 110600 | tf_op jit(solution)/shard_map/ppermute | solution.py:363
  7.1 5.8 %collective-permute-start.2 = (bf16[1,144,128]{2,1,0:T(8,128)(2,1)S(1)}, bf16[1,144,128]{2,1,0:T(8,128)(2,1)S(1)}, u32[]{:S(2)}, u32[]{:S(2)}) collective-permute-start(bf16[1,144,128]{2,1,0:T(8,128)(2,1)S(1)} %fusion.2), channel_id=1, source_target_pairs={{0,24},{2,26},{4,28},{6,30},{8,16},{10,18},{12,20},{14,22},{16,8},... | collective-permute-start | bytes 110600 | tf_op jit(solution)/shard_map/ppermute | solution.py:363
  12.9 10.9 %collective-permute-start.5 = (bf16[4,144,128]{2,1,0:T(8,128)(2,1)S(1)}, bf16[4,144,128]{2,1,0:T(8,128)(2,1)S(1)}, u32[]{:S(2)}, u32[]{:S(2)}) collective-permute-start(bf16[4,144,128]{2,1,0:T(8,128)(2,1)S(1)} %pad_maximum_fusion.refs_1_.refs_0_), channel_id=1, source_target_pairs={{0,4},{2,6},{4,0},{6,2},{8,12},{10,14},{12,8},{14,10},{16,20},{18,... | collective-permute-start | bytes 442376 | tf_op jit(solution)/shard_map/ppermute | solution.py:363
  14.4 9.9 %collective-permute-start.7 = (bf16[4,144,128]{2,1,0:T(8,128)(2,1)S(1)}, bf16[4,144,128]{2,1,0:T(8,128)(2,1)S(1)}, u32[]{:S(2)}, u32[]{:S(2)}) collective-permute-start(bf16[4,144,128]{2,1,0:T(8,128)(2,1)S(1)} %pad_maximum_fusion.refs_1_.refs_0_), channel_id=1, source_target_pairs={{0,2},{2,0},{4,6},{6,4},{8,10},{10,8},{12,14},{14,12},{16,18},{18,... | collective-permute-start | bytes 442376 | tf_op jit(solution)/shard_map/ppermute | solution.py:363
  14.4 8.8 %collective-permute-start.8 = (bf16[4,128,128]{2,1,0:T(8,128)(2,1)S(1)}, bf16[4,128,128]{2,1,0:T(8,128)(2,1)S(1)}, u32[]{:S(2)}, u32[]{:S(2)}) collective-permute-start(bf16[4,128,128]{2,1,0:T(8,128)(2,1)S(1)} %slice.4), channel_id=1, source_target_pairs={{0,1},{1,0},{2,3},{3,2},{4,5},{5,4},{6,7},{7,6},{8,9},{9,8},{10,11... | collective-permute-start | bytes 393224 | tf_op jit(solution)/shard_map/ppermute | solution.py:366
  16.0 7.2 %collective-permute-start.3 = (bf16[4,128,128]{2,1,0:T(8,128)(2,1)S(1)}, bf16[4,128,128]{2,1,0:T(8,128)(2,1)S(1)}, u32[]{:S(2)}, u32[]{:S(2)}) collective-permute-start(bf16[4,128,128]{2,1,0:T(8,128)(2,1)S(1)} %slice.4), channel_id=1, source_target_pairs={{0,5},{1,4},{2,7},{3,6},{4,1},{5,0},{6,3},{7,2},{8,13},{9,12},{10,... | collective-permute-start | bytes 393224 | tf_op jit(solution)/shard_map/ppermute | solution.py:372
  23.2 1.9 %collective-permute-start.9 = (bf16[4,128,128]{2,1,0:T(8,128)(2,1)S(1)}, bf16[4,128,128]{2,1,0:T(8,128)(2,1)S(1)}, u32[]{:S(2)}, u32[]{:S(2)}) collective-permute-start(bf16[4,128,128]{2,1,0:T(8,128)(2,1)S(1)} %collective-permute-done.8.refs_0_), channel_id=1, source_target_pairs={{0,2},{2,0},{4,6},{6,4},{8,10},{10,8},{12,14},{14,12},{16,18},{18,... | collective-permute-start | bytes 393224 | tf_op jit(solution)/shard_map/ppermute | solution.py:363
  23.2 3.1 %collective-permute-start.4 = (bf16[4,128,128]{2,1,0:T(8,128)(2,1)S(1)}, bf16[4,128,128]{2,1,0:T(8,128)(2,1)S(1)}, u32[]{:S(2)}, u32[]{:S(2)}) collective-permute-start(bf16[4,128,128]{2,1,0:T(8,128)(2,1)S(1)} %collective-permute-done.3.refs_2_), channel_id=1, source_target_pairs={{0,2},{2,0},{4,6},{6,4},{8,10},{10,8},{12,14},{14,12},{16,18},{18,... | collective-permute-start | bytes 393224 | tf_op jit(solution)/shard_map/ppermute | solution.py:363
  23.7 1.8 %collective-permute-start.6 = (bf16[4,144,128]{2,1,0:T(8,128)(2,1)S(1)}, bf16[4,144,128]{2,1,0:T(8,128)(2,1)S(1)}, u32[]{:S(2)}, u32[]{:S(2)}) collective-permute-start(bf16[4,144,128]{2,1,0:T(8,128)(2,1)S(1)} %collective-permute-done.5.refs_1_.refs_0_), channel_id=1, source_target_pairs={{0,2},{2,0},{4,6},{6,4},{8,10},{10,8},{12,14},{14,12},{16,18},{18,... | collective-permute-start | bytes 442376 | tf_op jit(solution)/shard_map/ppermute | solution.py:363
  30.6 1.8 %collective-permute-start.10 = (f32[256,256]{1,0:T(8,128)S(1)}, f32[256,256]{1,0:T(8,128)S(1)}, u32[]{:S(2)}, u32[]{:S(2)}) collective-permute-start(f32[256,256]{1,0:T(8,128)S(1)} %get-tuple-element.9.own_ref), channel_id=1, source_target_pairs={{0,2},{2,0},{4,6},{6,4},{8,10},{10,8},{12,14},{14,12},{16,18},{18,... | collective-permute-start | bytes 786440 | tf_op jit(solution)/shard_map/ppermute | solution.py:363
  35.3 5.8 %collective-permute-start.11 = (f32[264,128]{1,0:T(8,128)S(1)}, f32[264,128]{1,0:T(8,128)S(1)}, u32[]{:S(2)}, u32[]{:S(2)}) collective-permute-start(f32[264,128]{1,0:T(8,128)S(1)} %get-tuple-element.11), channel_id=1, source_target_pairs={{0,4},{2,6},{4,0},{6,2},{8,12},{10,14},{12,8},{14,10},{16,20},{18,... | collective-permute-start | bytes 405512 | tf_op jit(solution)/shard_map/ppermute | solution.py:363

commit v10 on v9

--- a/solution.py
+++ b/solution.py
@@ -298,7 +298,10 @@
     by_col = jnp.sum(diagonal, axis=0, keepdims=True)
     inverse = jnp.where(rows > cols, held / by_col, jnp.where(rows == cols, 1.0, 0.0))
     scale = jnp.where(rows.astype(F32) < points_ref[4:5, 0:1], lax.rsqrt(by_row * shift), 0.0)
-    b_ref[...] = dot3(inverse * scale, matrix, NN)
+    basis = dot3(inverse * scale, matrix, NN)
+    half = b_ref.shape[2]
+    for c in range(2):
+        b_ref[:, c, :] = basis[:, c * half : (c + 1) * half]
 
 
 def inverse(matrix):
@@ -337,19 +340,22 @@
     fold(h_ref, packed_ref)
 
 
-def top_body(own_ref, other_ref, z_ref, t_ref):
+def top_body(own_ref, other_ref, basis_ref, z_ref, out_ref, t_ref, sem):
+    copy = pltpu.make_async_copy(basis_ref, out_ref, sem)
+    copy.start()
     shift, by_row, by_col = factorize(unfold_add(other_ref, own_ref), t_ref)
     value = projected_rows(t_ref, by_row, by_col)
     z_ref[...] = (value * jnp.sqrt(shift)).T
-
-
-def call(body, outs, operands, specs=None, scratch=(), flops=0):
+    copy.wait()
+
+
+def call(body, outs, operands, specs=None, scratch=(), flops=0, out_specs=None):
     bytes_used = sum(x.size * x.dtype.itemsize for x in (*outs, *operands))
     return pl.pallas_call(
         body,
         out_shape=list(outs),
         in_specs=list(specs or [VMEM] * len(operands)),
-        out_specs=[VMEM] * len(outs),
+        out_specs=list(out_specs or [VMEM] * len(outs)),
         scratch_shapes=list(scratch),
         cost_estimate=pl.CostEstimate(flops=flops, bytes_accessed=bytes_used, transcendentals=0),
         compiler_params=pltpu.CompilerParams(vmem_limit_bytes=2 * bytes_used + (6 << 20)),
@@ -438,12 +444,16 @@
             lambda *refs, begin=begin, stop=stop: sweep_body(begin, stop, *refs), [square], [t],
             flops=200 * n**3,
         )[0]
-    basis = call(basis_body, [square], [points, t, m], flops=60 * n**3)[0]
+    parts = jax.ShapeDtypeStruct((n, 2, leaf_rows), F32)
+    basis = call(basis_body, [parts], [points, t, m], flops=60 * n**3)[0]
     packed = jax.ShapeDtypeStruct((n + 8, n // 2), F32)
     h, sent = call(node_body, [square, packed], [h, other], flops=n**3)
     other = flip(sent, 2)
-    top = call(top_body, [square], [h, other], scratch=scratch, flops=n**3)[0]
-    return (basis.reshape(n, 2, leaf_rows), top[None])
+    top, basis = call(
+        top_body, [square, parts], [h, other, basis], scratch=[*scratch, pltpu.SemaphoreType.DMA],
+        flops=n**3, out_specs=[VMEM, pl.BlockSpec(memory_space=pl.ANY)],
+    )
+    return (basis, top[None])
 
 
 def solution(mesh):

time: 47.3 us -> 47.4 us (level)
  local copies, waits for them, and re-layouts: 1.08 us -> 0.25 us
  waiting for transfers between devices: 10.9 us -> 11.6 us
    reshape x1 -> x0, local copies, waits for them, and re-layouts: 0.83 us -> none  [per_device(): return (basis.reshape(n, 2, leaf_rows), top[None])]
    ppermute x10, waiting for transfers between devices: 4.73 us -> 5.48 us  [flip(): return lax.ppermute(value, 'rows', pairs)]
  transfers between devices with their start and end apart: 12 -> 12, of which waited for: 4 -> 4; matrix products, arithmetic and copies ran while one was open for 2% -> 1% of each run, Pallas kernels for 17% -> 17%
where the time goes in v10:
time: 47.4 us; the launch traced here: 47.2 us
  Pallas kernels  21.3 us (45%)
  waiting for transfers between devices  11.6 us (24%)
  starting transfers between devices  10.9 us (23%)
  between operations  2.24 us (5%)
  other arithmetic  0.88 us (2%)
    pallas_call x13, Pallas kernels, call(): pl.pallas_call(body, out_shape=list(outs), in_specs=list(specs or [VMEM]...  21.3 us
    ppermute x10, starting transfers between devices, flip(): return lax.ppermute(value, 'rows', pairs)  8.89 us
    ppermute x1, waiting for transfers between devices, flip(): return lax.ppermute(value, 'probe', pairs)  6.15 us
    ppermute x10, waiting for transfers between devices, flip(): return lax.ppermute(value, 'rows', pairs)  5.48 us
    ppermute x1, starting transfers between devices, flip(): return lax.ppermute(value, 'probe', pairs)  1.58 us
  transfers between devices with their start and end apart: 12, of which 4 were waited for; matrix products, arithmetic and copies ran while one was open for 1% of the time, Pallas kernels for 17%

profile of v10, /device:TPU:0, one launch (start us, length us, event | category | flops | bytes accessed | tf_op | source)
XLA Modules:
  0.0 47.2 jit_solution(14703631055699984568)
XLA Ops:
  0.6 0.0 copy-start
  0.6 0.8 %fusion.2 = bf16[1,144,128]{2,1,0:T(8,128)(2,1)S(1)} fusion(bf16[3,128]{1,0:T(4,128)(2,1)} %param.6, bf16[128,128]{1,0:T(8,128)(2,1)} %param.7), kind=kLoop, calls=%fused_computation.4 | loop fusion | flops 110592 | bytes 70400 | tf_op jit(solution)/shard_map/broadcast_in_dim | solution.py:401
  1.4 3.1 %collective-permute-start = (bf16[1,144,128]{2,1,0:T(8,128)(2,1)S(1)}, bf16[1,144,128]{2,1,0:T(8,128)(2,1)S(1)}, u32[]{:S(2)}, u32[]{:S(2)}) collective-permute-start(bf16[1,144,128]{2,1,0:T(8,128)(2,1)S(1)} %fusion.2), channel_id=1, source_target_pairs={{0,8},{2,10},{4,12},{6,14},{8,0},{10,2},{12,4},{14,6},{16,24},{18,... | collective-permute-start | bytes 110600 | tf_op jit(solution)/shard_map/ppermute | solution.py:369
  4.5 2.6 %collective-permute-start.1 = (bf16[1,144,128]{2,1,0:T(8,128)(2,1)S(1)}, bf16[1,144,128]{2,1,0:T(8,128)(2,1)S(1)}, u32[]{:S(2)}, u32[]{:S(2)}) collective-permute-start(bf16[1,144,128]{2,1,0:T(8,128)(2,1)S(1)} %fusion.2), channel_id=1, source_target_pairs={{0,16},{2,18},{4,20},{6,22},{8,24},{10,26},{12,28},{14,30},{16,0},... | collective-permute-start | bytes 110600 | tf_op jit(solution)/shard_map/ppermute | solution.py:369
  8.4 0.1 pad.12.clone
  8.5 0.1 pad.13.clone
  8.5 0.1 pad.14.clone
  8.6 1.4 %collective-permute-done.1 = bf16[1,144,128]{2,1,0:T(8,128)(2,1)S(1)} collective-permute-done((bf16[1,144,128]{2,1,0:T(8,128)(2,1)S(1)}, bf16[1,144,128]{2,1,0:T(8,128)(2,1)S(1)}, u32[]{:S(2)}, u32[]{:S(2)}) %collective-permute-start.1) | collective-permute-done | bytes 36896 | tf_op jit(solution)/shard_map/ppermute | solution.py:369
  10.0 2.8 %collective-permute-done.2 = bf16[1,144,128]{2,1,0:T(8,128)(2,1)S(1)} collective-permute-done((bf16[1,144,128]{2,1,0:T(8,128)(2,1)S(1)}, bf16[1,144,128]{2,1,0:T(8,128)(2,1)S(1)}, u32[]{:S(2)}, u32[]{:S(2)}) %collective-permute-start.2) | collective-permute-done | bytes 36896 | tf_op jit(solution)/shard_map/ppermute | solution.py:369
  12.9 1.6 %collective-permute-start.5 = (bf16[4,144,128]{2,1,0:T(8,128)(2,1)S(1)}, bf16[4,144,128]{2,1,0:T(8,128)(2,1)S(1)}, u32[]{:S(2)}, u32[]{:S(2)}) collective-permute-start(bf16[4,144,128]{2,1,0:T(8,128)(2,1)S(1)} %pad_maximum_fusion.refs_1_.refs_0_), channel_id=1, source_target_pairs={{0,4},{2,6},{4,0},{6,2},{8,12},{10,14},{12,8},{14,10},{16,20},{18,... | collective-permute-start | bytes 442376 | tf_op jit(solution)/shard_map/ppermute | solution.py:369
  14.4 1.6 %collective-permute-start.8 = (bf16[4,128,128]{2,1,0:T(8,128)(2,1)S(1)}, bf16[4,128,128]{2,1,0:T(8,128)(2,1)S(1)}, u32[]{:S(2)}, u32[]{:S(2)}) collective-permute-start(bf16[4,128,128]{2,1,0:T(8,128)(2,1)S(1)} %slice.4), channel_id=1, source_target_pairs={{0,1},{1,0},{2,3},{3,2},{4,5},{5,4},{6,7},{7,6},{8,9},{9,8},{10,11... | collective-permute-start | bytes 393224 | tf_op jit(solution)/shard_map/ppermute | solution.py:372
  16.0 0.5 %collective-permute-start.3 = (bf16[4,128,128]{2,1,0:T(8,128)(2,1)S(1)}, bf16[4,128,128]{2,1,0:T(8,128)(2,1)S(1)}, u32[]{:S(2)}, u32[]{:S(2)}) collective-permute-start(bf16[4,128,128]{2,1,0:T(8,128)(2,1)S(1)} %slice.4), channel_id=1, source_target_pairs={{0,5},{1,4},{2,7},{3,6},{4,1},{5,0},{6,3},{7,2},{8,13},{9,12},{10,... | collective-permute-start | bytes 393224 | tf_op jit(solution)/shard_map/ppermute | solution.py:378
  16.5 0.1 maximum_maximum_fusion.refs_0_.refs_1_.points_ref
  16.6 0.5 %shard_map.70.refs_2_.refs_3_ = bf16[4,256,128]{2,1,0:T(8,128)(2,1)S(1)} custom-call(f32[8,128]{1,0:T(8,128)S(1)} %maximum_maximum_fusion.refs_0_.refs_1_.points_ref, bf16[4,144,128]{2,1,0:T(8,128)(2,1)S(1)} %pad_maximum_fusion.refs_1_.refs_0_), custom_call_target="tpu_custom_call" | custom-call | flops 262144000 | bytes 413696 | tf_op jit(solution)/shard_map/pallas_call | solution.py:354
  17.1 6.1 %collective-permute-done.8.refs_0_ = bf16[4,128,128]{2,1,0:T(8,128)(2,1)S(1)} collective-permute-done((bf16[4,128,128]{2,1,0:T(8,128)(2,1)S(1)}, bf16[4,128,128]{2,1,0:T(8,128)(2,1)S(1)}, u32[]{:S(2)}, u32[]{:S(2)}) %collective-permute-start.8) | collective-permute-done | bytes 131104 | tf_op jit(solution)/shard_map/ppermute | solution.py:372
  23.2 0.5 %collective-permute-start.4 = (bf16[4,128,128]{2,1,0:T(8,128)(2,1)S(1)}, bf16[4,128,128]{2,1,0:T(8,128)(2,1)S(1)}, u32[]{:S(2)}, u32[]{:S(2)}) collective-permute-start(bf16[4,128,128]{2,1,0:T(8,128)(2,1)S(1)} %collective-permute-done.3.refs_2_), channel_id=1, source_target_pairs={{0,2},{2,0},{4,6},{6,4},{8,10},{10,8},{12,14},{14,12},{16,18},{18,... | collective-permute-start | bytes 393224 | tf_op jit(solution)/shard_map/ppermute | solution.py:369
  23.7 0.1 collective-permute-start.6
  23.8 0.5 %shard_map.69.refs_2_.refs_5_ = bf16[4,256,128]{2,1,0:T(8,128)(2,1)S(1)} custom-call(f32[8,128]{1,0:T(8,128)S(1)} %maximum_maximum_fusion.refs_0_.refs_1_.points_ref, bf16[4,144,128]{2,1,0:T(8,128)(2,1)S(1)} %collective-permute-done.5.refs_1_.refs_0_), custom_call_target="tpu_custom_call" | custom-call | flops 262144000 | bytes 413696 | tf_op jit(solution)/shard_map/pallas_call | solution.py:354
  24.3 0.5 %shard_map.71.refs_3_.refs_4_ = bf16[4,256,128]{2,1,0:T(8,128)(2,1)S(1)} custom-call(f32[8,128]{1,0:T(8,128)S(1)} %maximum_maximum_fusion.refs_0_.refs_1_.points_ref, bf16[4,144,128]{2,1,0:T(8,128)(2,1)S(1)} %collective-permute-done.7.refs_1_), custom_call_target="tpu_custom_call" | custom-call | flops 262144000 | bytes 413696 | tf_op jit(solution)/shard_map/pallas_call | solution.py:354
  24.8 0.3 shard_map.72.refs_4_
  25.1 0.4 shard_map.74.refs_5_
  25.5 0.5 %shard_map.68.refs_3_ = bf16[4,256,128]{2,1,0:T(8,128)(2,1)S(1)} custom-call(f32[8,128]{1,0:T(8,128)S(1)} %maximum_maximum_fusion.refs_0_.refs_1_.points_ref, bf16[4,144,128]{2,1,0:T(8,128)(2,1)S(1)} %collective-permute-done.6.refs_1_), custom_call_target="tpu_custom_call" | custom-call | flops 262144000 | bytes 413696 | tf_op jit(solution)/shard_map/pallas_call | solution.py:354
  26.0 0.3 shard_map.73.refs_4_
  26.4 4.2 %shard_map.75 = (f32[256,256]{1,0:T(8,128)S(1)}, f32[256,256]{1,0:T(8,128)S(1)}, f32[256,256]{1,0:T(8,128)S(1)}) custom-call(s32[1]{0:T(128)} %bitcast.refs_0_, f32[8,128]{1,0:T(8,128)S(1)} %maximum_maximum_fusion.refs_0_.refs_1_.points_ref, bf16[4,128,128]{2,1,0:T(8,128)(2,1)S(1)} %collective-permute-done.4.refs_2_, ...), custom_call_target="tpu_custom_call" | custom-call | flops 16777216 | bytes 1445892 | tf_op jit(solution)/shard_map/pallas_call | solution.py:354
  30.6 0.5 %collective-permute-start.10 = (f32[256,256]{1,0:T(8,128)S(1)}, f32[256,256]{1,0:T(8,128)S(1)}, u32[]{:S(2)}, u32[]{:S(2)}) collective-permute-start(f32[256,256]{1,0:T(8,128)S(1)} %get-tuple-element.9.own_ref), channel_id=1, source_target_pairs={{0,2},{2,0},{4,6},{6,4},{8,10},{10,8},{12,14},{14,12},{16,18},{18,... | collective-permute-start | bytes 786440 | tf_op jit(solution)/shard_map/ppermute | solution.py:369
  31.1 1.3 %shard_map.77.refs_0_ = f32[256,256]{1,0:T(8,128)S(1)} custom-call(f32[256,256]{1,0:T(8,128)S(1)} %get-tuple-element.12.refs_0_), custom_call_target="tpu_custom_call" | custom-call | flops 3355443200 | bytes 524288 | tf_op jit(solution)/shard_map/pallas_call | solution.py:354
  32.4 3.0 %shard_map.76 = (f32[256,256]{1,0:T(8,128)S(1)}, f32[264,128]{1,0:T(8,128)S(1)}) custom-call(f32[256,256]{1,0:T(8,128)S(1)} %get-tuple-element.9.own_ref, f32[256,256]{1,0:T(8,128)S(1)} %collective-permute-done.10.other_ref), custom_call_target="tpu_custom_call" | custom-call | flops 16777216 | bytes 921600 | tf_op jit(solution)/shard_map/pallas_call | solution.py:354
  35.3 0.6 %collective-permute-start.11 = (f32[264,128]{1,0:T(8,128)S(1)}, f32[264,128]{1,0:T(8,128)S(1)}, u32[]{:S(2)}, u32[]{:S(2)}) collective-permute-start(f32[264,128]{1,0:T(8,128)S(1)} %get-tuple-element.11), channel_id=1, source_target_pairs={{0,4},{2,6},{4,0},{6,2},{8,12},{10,14},{12,8},{14,10},{16,20},{18,... | collective-permute-start | bytes 405512 | tf_op jit(solution)/shard_map/ppermute | solution.py:369
  35.9 3.4 %shard_map.78.t_ref = f32[256,256]{1,0:T(8,128)S(1)} custom-call(f32[256,256]{1,0:T(8,128)S(1)} %shard_map.77.refs_0_), custom_call_target="tpu_custom_call" | custom-call | flops 3355443200 | bytes 524288 | tf_op jit(solution)/shard_map/pallas_call | solution.py:354
  39.4 0.5 %shard_map.79.basis_ref = f32[256,2,128]{2,1,0:T(2,128)S(1)} custom-call(f32[8,128]{1,0:T(8,128)S(1)} %maximum_maximum_fusion.refs_0_.refs_1_.points_ref, f32[256,256]{1,0:T(8,128)S(1)} %shard_map.78.t_ref, f32[256,256]{1,0:T(8,128)S(1)} %get-tuple-element.13.m_ref), custom_call_target="tpu_custom_call" | custom-call | flops 1006632960 | bytes 790528 | tf_op jit(solution)/shard_map/pallas_call | solution.py:354
  39.9 1.2 %collective-permute-done.11.other_ref = f32[264,128]{1,0:T(8,128)S(1)} collective-permute-done((f32[264,128]{1,0:T(8,128)S(1)}, f32[264,128]{1,0:T(8,128)S(1)}, u32[]{:S(2)}, u32[]{:S(2)}) %collective-permute-start.11) | collective-permute-done | bytes 135200 | tf_op jit(solution)/shard_map/ppermute | solution.py:369
  41.2 5.9 %shard_map.80 = (f32[256,256]{1,0:T(8,128)}, f32[256,2,128]{2,1,0:T(2,128)}) custom-call(f32[256,256]{1,0:T(8,128)S(1)} %get-tuple-element.10.own_ref, f32[264,128]{1,0:T(8,128)S(1)} %collective-permute-done.11.other_ref, f32[256,2,128]{2,1,0:T(2,128)S(1)} %shard_map.79.basis_ref), custom_call_target="tpu_custom_call" | custom-call | flops 16777216 | bytes 1183744 | tf_op jit(solution)/shard_map/pallas_call | solution.py:354
  (16 shorter events, 0.1 us)
Async XLA Ops:
  0.6 6.4 %copy-start = (f32[3,256]{1,0:T(4,128)S(1)}, f32[3,256]{1,0:T(4,128)}, u32[]{:S(2)}) copy-start(f32[3,256]{1,0:T(4,128)} %param.5) | copy-start | bytes 9220
  1.4 7.2 %collective-permute-start = (bf16[1,144,128]{2,1,0:T(8,128)(2,1)S(1)}, bf16[1,144,128]{2,1,0:T(8,128)(2,1)S(1)}, u32[]{:S(2)}, u32[]{:S(2)}) collective-permute-start(bf16[1,144,128]{2,1,0:T(8,128)(2,1)S(1)} %fusion.2), channel_id=1, source_target_pairs={{0,8},{2,10},{4,12},{6,14},{8,0},{10,2},{12,4},{14,6},{16,24},{18,... | collective-permute-start | bytes 110600 | tf_op jit(solution)/shard_map/ppermute | solution.py:369
  4.5 5.5 %collective-permute-start.1 = (bf16[1,144,128]{2,1,0:T(8,128)(2,1)S(1)}, bf16[1,144,128]{2,1,0:T(8,128)(2,1)S(1)}, u32[]{:S(2)}, u32[]{:S(2)}) collective-permute-start(bf16[1,144,128]{2,1,0:T(8,128)(2,1)S(1)} %fusion.2), channel_id=1, source_target_pairs={{0,16},{2,18},{4,20},{6,22},{8,24},{10,26},{12,28},{14,30},{16,0},... | collective-permute-start | bytes 110600 | tf_op jit(solution)/shard_map/ppermute | solution.py:369
  7.1 5.8 %collective-permute-start.2 = (bf16[1,144,128]{2,1,0:T(8,128)(2,1)S(1)}, bf16[1,144,128]{2,1,0:T(8,128)(2,1)S(1)}, u32[]{:S(2)}, u32[]{:S(2)}) collective-permute-start(bf16[1,144,128]{2,1,0:T(8,128)(2,1)S(1)} %fusion.2), channel_id=1, source_target_pairs={{0,24},{2,26},{4,28},{6,30},{8,16},{10,18},{12,20},{14,22},{16,8},... | collective-permute-start | bytes 110600 | tf_op jit(solution)/shard_map/ppermute | solution.py:369
  12.9 10.9 %collective-permute-start.5 = (bf16[4,144,128]{2,1,0:T(8,128)(2,1)S(1)}, bf16[4,144,128]{2,1,0:T(8,128)(2,1)S(1)}, u32[]{:S(2)}, u32[]{:S(2)}) collective-permute-start(bf16[4,144,128]{2,1,0:T(8,128)(2,1)S(1)} %pad_maximum_fusion.refs_1_.refs_0_), channel_id=1, source_target_pairs={{0,4},{2,6},{4,0},{6,2},{8,12},{10,14},{12,8},{14,10},{16,20},{18,... | collective-permute-start | bytes 442376 | tf_op jit(solution)/shard_map/ppermute | solution.py:369
  14.4 9.9 %collective-permute-start.7 = (bf16[4,144,128]{2,1,0:T(8,128)(2,1)S(1)}, bf16[4,144,128]{2,1,0:T(8,128)(2,1)S(1)}, u32[]{:S(2)}, u32[]{:S(2)}) collective-permute-start(bf16[4,144,128]{2,1,0:T(8,128)(2,1)S(1)} %pad_maximum_fusion.refs_1_.refs_0_), channel_id=1, source_target_pairs={{0,2},{2,0},{4,6},{6,4},{8,10},{10,8},{12,14},{14,12},{16,18},{18,... | collective-permute-start | bytes 442376 | tf_op jit(solution)/shard_map/ppermute | solution.py:369
  14.4 8.8 %collective-permute-start.8 = (bf16[4,128,128]{2,1,0:T(8,128)(2,1)S(1)}, bf16[4,128,128]{2,1,0:T(8,128)(2,1)S(1)}, u32[]{:S(2)}, u32[]{:S(2)}) collective-permute-start(bf16[4,128,128]{2,1,0:T(8,128)(2,1)S(1)} %slice.4), channel_id=1, source_target_pairs={{0,1},{1,0},{2,3},{3,2},{4,5},{5,4},{6,7},{7,6},{8,9},{9,8},{10,11... | collective-permute-start | bytes 393224 | tf_op jit(solution)/shard_map/ppermute | solution.py:372
  16.0 7.2 %collective-permute-start.3 = (bf16[4,128,128]{2,1,0:T(8,128)(2,1)S(1)}, bf16[4,128,128]{2,1,0:T(8,128)(2,1)S(1)}, u32[]{:S(2)}, u32[]{:S(2)}) collective-permute-start(bf16[4,128,128]{2,1,0:T(8,128)(2,1)S(1)} %slice.4), channel_id=1, source_target_pairs={{0,5},{1,4},{2,7},{3,6},{4,1},{5,0},{6,3},{7,2},{8,13},{9,12},{10,... | collective-permute-start | bytes 393224 | tf_op jit(solution)/shard_map/ppermute | solution.py:378
  23.2 1.9 %collective-permute-start.9 = (bf16[4,128,128]{2,1,0:T(8,128)(2,1)S(1)}, bf16[4,128,128]{2,1,0:T(8,128)(2,1)S(1)}, u32[]{:S(2)}, u32[]{:S(2)}) collective-permute-start(bf16[4,128,128]{2,1,0:T(8,128)(2,1)S(1)} %collective-permute-done.8.refs_0_), channel_id=1, source_target_pairs={{0,2},{2,0},{4,6},{6,4},{8,10},{10,8},{12,14},{14,12},{16,18},{18,... | collective-permute-start | bytes 393224 | tf_op jit(solution)/shard_map/ppermute | solution.py:369
  23.2 3.1 %collective-permute-start.4 = (bf16[4,128,128]{2,1,0:T(8,128)(2,1)S(1)}, bf16[4,128,128]{2,1,0:T(8,128)(2,1)S(1)}, u32[]{:S(2)}, u32[]{:S(2)}) collective-permute-start(bf16[4,128,128]{2,1,0:T(8,128)(2,1)S(1)} %collective-permute-done.3.refs_2_), channel_id=1, source_target_pairs={{0,2},{2,0},{4,6},{6,4},{8,10},{10,8},{12,14},{14,12},{16,18},{18,... | collective-permute-start | bytes 393224 | tf_op jit(solution)/shard_map/ppermute | solution.py:369
  23.7 1.8 %collective-permute-start.6 = (bf16[4,144,128]{2,1,0:T(8,128)(2,1)S(1)}, bf16[4,144,128]{2,1,0:T(8,128)(2,1)S(1)}, u32[]{:S(2)}, u32[]{:S(2)}) collective-permute-start(bf16[4,144,128]{2,1,0:T(8,128)(2,1)S(1)} %collective-permute-done.5.refs_1_.refs_0_), channel_id=1, source_target_pairs={{0,2},{2,0},{4,6},{6,4},{8,10},{10,8},{12,14},{14,12},{16,18},{18,... | collective-permute-start | bytes 442376 | tf_op jit(solution)/shard_map/ppermute | solution.py:369
  30.6 1.8 %collective-permute-start.10 = (f32[256,256]{1,0:T(8,128)S(1)}, f32[256,256]{1,0:T(8,128)S(1)}, u32[]{:S(2)}, u32[]{:S(2)}) collective-permute-start(f32[256,256]{1,0:T(8,128)S(1)} %get-tuple-element.9.own_ref), channel_id=1, source_target_pairs={{0,2},{2,0},{4,6},{6,4},{8,10},{10,8},{12,14},{14,12},{16,18},{18,... | collective-permute-start | bytes 786440 | tf_op jit(solution)/shard_map/ppermute | solution.py:369
  35.3 5.8 %collective-permute-start.11 = (f32[264,128]{1,0:T(8,128)S(1)}, f32[264,128]{1,0:T(8,128)S(1)}, u32[]{:S(2)}, u32[]{:S(2)}) collective-permute-start(f32[264,128]{1,0:T(8,128)S(1)} %get-tuple-element.11), channel_id=1, source_target_pairs={{0,4},{2,6},{4,0},{6,2},{8,12},{10,14},{12,8},{14,10},{16,20},{18,... | collective-permute-start | bytes 405512 | tf_op jit(solution)/shard_map/ppermute | solution.py:369

commit v11 on v10

--- a/solution.py
+++ b/solution.py
@@ -24,7 +24,8 @@
 LANES = 128
 PANEL = 64
 CHUNK = 256
-COARSE = 0.2
+COARSE = 0.15
+NARROW = 40.0
 
 
 def split_bf16(value):
@@ -276,7 +277,7 @@
     kept_row = rows.astype(F32) < rank
     kept_col = cols.astype(F32) < rank
     inner = jnp.where(kept_row & kept_col, scaled, 0.0)
-    turned = inverse(inner + unit)
+    turned = inverse(inner + unit, h_ref)
     outer = jnp.where(kept_row & (cols.astype(F32) >= rank), scaled, 0.0)
     solved = jnp.where(kept_row, jnp.where(kept_col, unit - turned, dot3(turned, outer, NN)), 0.0)
     h_ref[...] = dot3(jnp.where(kept_col, scaled, 0.0), solved, NN) * shift
@@ -304,15 +305,30 @@
         b_ref[:, c, :] = basis[:, c * half : (c + 1) * half]
 
 
-def inverse(matrix):
+def inverse(matrix, x_ref):
+    n = matrix.shape[0]
+    bound = jnp.max(jnp.sum(jnp.abs(matrix), axis=0, keepdims=True))
+
+    @pl.when(bound <= NARROW)
+    def _():
+        x_ref[...] = iterate(matrix, NARROW)
+
+    @pl.when(jnp.logical_not(bound <= NARROW))
+    def _():
+        x_ref[...] = iterate(matrix, 1.001 * (n + 1.0))
+
+    return x_ref[...]
+
+
+def iterate(matrix, most):
     n = matrix.shape[0]
     rows, cols = grids(n)
     high, low = split_bf16(matrix)
-    least, most = 1.0, 1.001 * (n + 1.0)
+    least = 1.0
     scale = 2.0 / (least + most)
     guess = jnp.where(rows == cols, 2.0 * scale, 0.0) - scale * scale * matrix
     spread = (most - least) / (most + least)
-    while spread > 1e-3:
+    while spread > 0.013:
         least = 1.0 - spread * spread
         scale = 2.0 / (1.0 + least)
         spread = (1.0 - least) / (1.0 + least)
@@ -336,7 +352,7 @@
     shift = trace(gram) / n
     scaled = gram / shift
     start = scaled + jnp.where(rows == cols, 1.0, 0.0)
-    h_ref[...] = (scaled - jnp.where(rows == cols, 1.0, 0.0) + inverse(start)) * shift
+    h_ref[...] = (scaled - jnp.where(rows == cols, 1.0, 0.0) + inverse(start, h_ref)) * shift
     fold(h_ref, packed_ref)
 
 

time: 47.4 us -> 47.9 us (1.011)
  Pallas kernels: 21.3 us -> 21.8 us
    pallas_call x13, Pallas kernels: 21.3 us -> 21.8 us  [call(): pl.pallas_call(body, out_shape=list(outs), in_specs=list(specs or [VMEM]...]
where the time goes in v11:
time: 47.9 us; the launch traced here: 47.7 us
  Pallas kernels  21.8 us (46%)
  waiting for transfers between devices  11.8 us (25%)
  starting transfers between devices  10.8 us (23%)
  between operations  2.24 us (5%)
  other arithmetic  0.88 us (2%)
    pallas_call x13, Pallas kernels, call(): pl.pallas_call(body, out_shape=list(outs), in_specs=list(specs or [VMEM]...  21.8 us
    ppermute x10, starting transfers between devices, flip(): return lax.ppermute(value, 'rows', pairs)  8.7 us
    ppermute x1, waiting for transfers between devices, flip(): return lax.ppermute(value, 'probe', pairs)  6.15 us
    ppermute x10, waiting for transfers between devices, flip(): return lax.ppermute(value, 'rows', pairs)  5.65 us
    ppermute x1, starting transfers between devices, flip(): return lax.ppermute(value, 'probe', pairs)  1.58 us
  transfers between devices with their start and end apart: 12, of which 4 were waited for; matrix products, arithmetic and copies ran while one was open for 1% of the time, Pallas kernels for 17%

profile of v11, /device:TPU:0, one launch (start us, length us, event | category | flops | bytes accessed | tf_op | source)
XLA Modules:
  0.0 47.7 jit_solution(6433616682547639268)
XLA Ops:
  0.6 0.0 copy-start
  0.6 0.8 %fusion.2 = bf16[1,144,128]{2,1,0:T(8,128)(2,1)S(1)} fusion(bf16[3,128]{1,0:T(4,128)(2,1)} %param.6, bf16[128,128]{1,0:T(8,128)(2,1)} %param.7), kind=kLoop, calls=%fused_computation.4 | loop fusion | flops 110592 | bytes 70400 | tf_op jit(solution)/shard_map/broadcast_in_dim | solution.py:417
  1.4 3.1 %collective-permute-start = (bf16[1,144,128]{2,1,0:T(8,128)(2,1)S(1)}, bf16[1,144,128]{2,1,0:T(8,128)(2,1)S(1)}, u32[]{:S(2)}, u32[]{:S(2)}) collective-permute-start(bf16[1,144,128]{2,1,0:T(8,128)(2,1)S(1)} %fusion.2), channel_id=1, source_target_pairs={{0,8},{2,10},{4,12},{6,14},{8,0},{10,2},{12,4},{14,6},{16,24},{18,... | collective-permute-start | bytes 110600 | tf_op jit(solution)/shard_map/ppermute | solution.py:385
  4.5 2.6 %collective-permute-start.1 = (bf16[1,144,128]{2,1,0:T(8,128)(2,1)S(1)}, bf16[1,144,128]{2,1,0:T(8,128)(2,1)S(1)}, u32[]{:S(2)}, u32[]{:S(2)}) collective-permute-start(bf16[1,144,128]{2,1,0:T(8,128)(2,1)S(1)} %fusion.2), channel_id=1, source_target_pairs={{0,16},{2,18},{4,20},{6,22},{8,24},{10,26},{12,28},{14,30},{16,0},... | collective-permute-start | bytes 110600 | tf_op jit(solution)/shard_map/ppermute | solution.py:385
  8.4 0.1 pad.12.clone
  8.5 0.1 pad.13.clone
  8.5 0.1 pad.14.clone
  8.6 1.4 %collective-permute-done.1 = bf16[1,144,128]{2,1,0:T(8,128)(2,1)S(1)} collective-permute-done((bf16[1,144,128]{2,1,0:T(8,128)(2,1)S(1)}, bf16[1,144,128]{2,1,0:T(8,128)(2,1)S(1)}, u32[]{:S(2)}, u32[]{:S(2)}) %collective-permute-start.1) | collective-permute-done | bytes 36896 | tf_op jit(solution)/shard_map/ppermute | solution.py:385
  10.0 2.8 %collective-permute-done.2 = bf16[1,144,128]{2,1,0:T(8,128)(2,1)S(1)} collective-permute-done((bf16[1,144,128]{2,1,0:T(8,128)(2,1)S(1)}, bf16[1,144,128]{2,1,0:T(8,128)(2,1)S(1)}, u32[]{:S(2)}, u32[]{:S(2)}) %collective-permute-start.2) | collective-permute-done | bytes 36896 | tf_op jit(solution)/shard_map/ppermute | solution.py:385
  12.9 1.6 %collective-permute-start.5 = (bf16[4,144,128]{2,1,0:T(8,128)(2,1)S(1)}, bf16[4,144,128]{2,1,0:T(8,128)(2,1)S(1)}, u32[]{:S(2)}, u32[]{:S(2)}) collective-permute-start(bf16[4,144,128]{2,1,0:T(8,128)(2,1)S(1)} %pad_maximum_fusion.refs_1_.refs_0_), channel_id=1, source_target_pairs={{0,4},{2,6},{4,0},{6,2},{8,12},{10,14},{12,8},{14,10},{16,20},{18,... | collective-permute-start | bytes 442376 | tf_op jit(solution)/shard_map/ppermute | solution.py:385
  14.4 1.6 %collective-permute-start.8 = (bf16[4,128,128]{2,1,0:T(8,128)(2,1)S(1)}, bf16[4,128,128]{2,1,0:T(8,128)(2,1)S(1)}, u32[]{:S(2)}, u32[]{:S(2)}) collective-permute-start(bf16[4,128,128]{2,1,0:T(8,128)(2,1)S(1)} %slice.4), channel_id=1, source_target_pairs={{0,1},{1,0},{2,3},{3,2},{4,5},{5,4},{6,7},{7,6},{8,9},{9,8},{10,11... | collective-permute-start | bytes 393224 | tf_op jit(solution)/shard_map/ppermute | solution.py:388
  16.0 0.5 %collective-permute-start.3 = (bf16[4,128,128]{2,1,0:T(8,128)(2,1)S(1)}, bf16[4,128,128]{2,1,0:T(8,128)(2,1)S(1)}, u32[]{:S(2)}, u32[]{:S(2)}) collective-permute-start(bf16[4,128,128]{2,1,0:T(8,128)(2,1)S(1)} %slice.4), channel_id=1, source_target_pairs={{0,5},{1,4},{2,7},{3,6},{4,1},{5,0},{6,3},{7,2},{8,13},{9,12},{10,... | collective-permute-start | bytes 393224 | tf_op jit(solution)/shard_map/ppermute | solution.py:394
  16.5 0.1 maximum_maximum_fusion.refs_0_.refs_1_.points_ref
  16.6 0.5 %shard_map.70.refs_2_.refs_3_ = bf16[4,256,128]{2,1,0:T(8,128)(2,1)S(1)} custom-call(f32[8,128]{1,0:T(8,128)S(1)} %maximum_maximum_fusion.refs_0_.refs_1_.points_ref, bf16[4,144,128]{2,1,0:T(8,128)(2,1)S(1)} %pad_maximum_fusion.refs_1_.refs_0_), custom_call_target="tpu_custom_call" | custom-call | flops 262144000 | bytes 413696 | tf_op jit(solution)/shard_map/pallas_call | solution.py:370
  17.1 6.1 %collective-permute-done.8.refs_0_ = bf16[4,128,128]{2,1,0:T(8,128)(2,1)S(1)} collective-permute-done((bf16[4,128,128]{2,1,0:T(8,128)(2,1)S(1)}, bf16[4,128,128]{2,1,0:T(8,128)(2,1)S(1)}, u32[]{:S(2)}, u32[]{:S(2)}) %collective-permute-start.8) | collective-permute-done | bytes 131104 | tf_op jit(solution)/shard_map/ppermute | solution.py:388
  23.2 0.5 %collective-permute-start.4 = (bf16[4,128,128]{2,1,0:T(8,128)(2,1)S(1)}, bf16[4,128,128]{2,1,0:T(8,128)(2,1)S(1)}, u32[]{:S(2)}, u32[]{:S(2)}) collective-permute-start(bf16[4,128,128]{2,1,0:T(8,128)(2,1)S(1)} %collective-permute-done.3.refs_2_), channel_id=1, source_target_pairs={{0,2},{2,0},{4,6},{6,4},{8,10},{10,8},{12,14},{14,12},{16,18},{18,... | collective-permute-start | bytes 393224 | tf_op jit(solution)/shard_map/ppermute | solution.py:385
  23.7 0.1 collective-permute-start.6
  23.8 0.5 %shard_map.69.refs_2_.refs_5_ = bf16[4,256,128]{2,1,0:T(8,128)(2,1)S(1)} custom-call(f32[8,128]{1,0:T(8,128)S(1)} %maximum_maximum_fusion.refs_0_.refs_1_.points_ref, bf16[4,144,128]{2,1,0:T(8,128)(2,1)S(1)} %collective-permute-done.5.refs_1_.refs_0_), custom_call_target="tpu_custom_call" | custom-call | flops 262144000 | bytes 413696 | tf_op jit(solution)/shard_map/pallas_call | solution.py:370
  24.3 0.5 %shard_map.71.refs_3_.refs_4_ = bf16[4,256,128]{2,1,0:T(8,128)(2,1)S(1)} custom-call(f32[8,128]{1,0:T(8,128)S(1)} %maximum_maximum_fusion.refs_0_.refs_1_.points_ref, bf16[4,144,128]{2,1,0:T(8,128)(2,1)S(1)} %collective-permute-done.7.refs_1_), custom_call_target="tpu_custom_call" | custom-call | flops 262144000 | bytes 413696 | tf_op jit(solution)/shard_map/pallas_call | solution.py:370
  24.8 0.3 shard_map.72.refs_4_
  25.1 0.4 shard_map.74.refs_5_
  25.5 0.5 %shard_map.68.refs_3_ = bf16[4,256,128]{2,1,0:T(8,128)(2,1)S(1)} custom-call(f32[8,128]{1,0:T(8,128)S(1)} %maximum_maximum_fusion.refs_0_.refs_1_.points_ref, bf16[4,144,128]{2,1,0:T(8,128)(2,1)S(1)} %collective-permute-done.6.refs_1_), custom_call_target="tpu_custom_call" | custom-call | flops 262144000 | bytes 413696 | tf_op jit(solution)/shard_map/pallas_call | solution.py:370
  26.0 0.3 shard_map.73.refs_4_
  26.4 4.5 %shard_map.75 = (f32[256,256]{1,0:T(8,128)S(1)}, f32[256,256]{1,0:T(8,128)S(1)}, f32[256,256]{1,0:T(8,128)S(1)}) custom-call(s32[1]{0:T(128)} %bitcast.refs_0_, f32[8,128]{1,0:T(8,128)S(1)} %maximum_maximum_fusion.refs_0_.refs_1_.points_ref, bf16[4,128,128]{2,1,0:T(8,128)(2,1)S(1)} %collective-permute-done.4.refs_2_, ...), custom_call_target="tpu_custom_call" | custom-call | flops 16777216 | bytes 1445892 | tf_op jit(solution)/shard_map/pallas_call | solution.py:370
  30.8 0.5 %collective-permute-start.10 = (f32[256,256]{1,0:T(8,128)S(1)}, f32[256,256]{1,0:T(8,128)S(1)}, u32[]{:S(2)}, u32[]{:S(2)}) collective-permute-start(f32[256,256]{1,0:T(8,128)S(1)} %get-tuple-element.9.own_ref), channel_id=1, source_target_pairs={{0,2},{2,0},{4,6},{6,4},{8,10},{10,8},{12,14},{14,12},{16,18},{18,... | collective-permute-start | bytes 786440 | tf_op jit(solution)/shard_map/ppermute | solution.py:385
  31.4 1.3 %shard_map.77.refs_0_ = f32[256,256]{1,0:T(8,128)S(1)} custom-call(f32[256,256]{1,0:T(8,128)S(1)} %get-tuple-element.12.refs_0_), custom_call_target="tpu_custom_call" | custom-call | flops 3355443200 | bytes 524288 | tf_op jit(solution)/shard_map/pallas_call | solution.py:370
  32.6 3.4 %shard_map.76 = (f32[256,256]{1,0:T(8,128)S(1)}, f32[264,128]{1,0:T(8,128)S(1)}) custom-call(f32[256,256]{1,0:T(8,128)S(1)} %get-tuple-element.9.own_ref, f32[256,256]{1,0:T(8,128)S(1)} %collective-permute-done.10.other_ref), custom_call_target="tpu_custom_call" | custom-call | flops 16777216 | bytes 921600 | tf_op jit(solution)/shard_map/pallas_call | solution.py:370
  36.0 0.4 collective-permute-start.11
  36.4 3.4 %shard_map.78.t_ref = f32[256,256]{1,0:T(8,128)S(1)} custom-call(f32[256,256]{1,0:T(8,128)S(1)} %shard_map.77.refs_0_), custom_call_target="tpu_custom_call" | custom-call | flops 3355443200 | bytes 524288 | tf_op jit(solution)/shard_map/pallas_call | solution.py:370
  39.9 0.5 %shard_map.79.basis_ref = f32[256,2,128]{2,1,0:T(2,128)S(1)} custom-call(f32[8,128]{1,0:T(8,128)S(1)} %maximum_maximum_fusion.refs_0_.refs_1_.points_ref, f32[256,256]{1,0:T(8,128)S(1)} %shard_map.78.t_ref, f32[256,256]{1,0:T(8,128)S(1)} %get-tuple-element.13.m_ref), custom_call_target="tpu_custom_call" | custom-call | flops 1006632960 | bytes 790528 | tf_op jit(solution)/shard_map/pallas_call | solution.py:370
  40.4 1.4 %collective-permute-done.11.other_ref = f32[264,128]{1,0:T(8,128)S(1)} collective-permute-done((f32[264,128]{1,0:T(8,128)S(1)}, f32[264,128]{1,0:T(8,128)S(1)}, u32[]{:S(2)}, u32[]{:S(2)}) %collective-permute-start.11) | collective-permute-done | bytes 135200 | tf_op jit(solution)/shard_map/ppermute | solution.py:385
  41.8 5.7 %shard_map.80 = (f32[256,256]{1,0:T(8,128)}, f32[256,2,128]{2,1,0:T(2,128)}) custom-call(f32[256,256]{1,0:T(8,128)S(1)} %get-tuple-element.10.own_ref, f32[264,128]{1,0:T(8,128)S(1)} %collective-permute-done.11.other_ref, f32[256,2,128]{2,1,0:T(2,128)S(1)} %shard_map.79.basis_ref), custom_call_target="tpu_custom_call" | custom-call | flops 16777216 | bytes 1183744 | tf_op jit(solution)/shard_map/pallas_call | solution.py:370
  (16 shorter events, 0.1 us)
Async XLA Ops:
  0.6 6.4 %copy-start = (f32[3,256]{1,0:T(4,128)S(1)}, f32[3,256]{1,0:T(4,128)}, u32[]{:S(2)}) copy-start(f32[3,256]{1,0:T(4,128)} %param.5) | copy-start | bytes 9220
  1.4 7.2 %collective-permute-start = (bf16[1,144,128]{2,1,0:T(8,128)(2,1)S(1)}, bf16[1,144,128]{2,1,0:T(8,128)(2,1)S(1)}, u32[]{:S(2)}, u32[]{:S(2)}) collective-permute-start(bf16[1,144,128]{2,1,0:T(8,128)(2,1)S(1)} %fusion.2), channel_id=1, source_target_pairs={{0,8},{2,10},{4,12},{6,14},{8,0},{10,2},{12,4},{14,6},{16,24},{18,... | collective-permute-start | bytes 110600 | tf_op jit(solution)/shard_map/ppermute | solution.py:385
  4.5 5.5 %collective-permute-start.1 = (bf16[1,144,128]{2,1,0:T(8,128)(2,1)S(1)}, bf16[1,144,128]{2,1,0:T(8,128)(2,1)S(1)}, u32[]{:S(2)}, u32[]{:S(2)}) collective-permute-start(bf16[1,144,128]{2,1,0:T(8,128)(2,1)S(1)} %fusion.2), channel_id=1, source_target_pairs={{0,16},{2,18},{4,20},{6,22},{8,24},{10,26},{12,28},{14,30},{16,0},... | collective-permute-start | bytes 110600 | tf_op jit(solution)/shard_map/ppermute | solution.py:385
  7.1 5.8 %collective-permute-start.2 = (bf16[1,144,128]{2,1,0:T(8,128)(2,1)S(1)}, bf16[1,144,128]{2,1,0:T(8,128)(2,1)S(1)}, u32[]{:S(2)}, u32[]{:S(2)}) collective-permute-start(bf16[1,144,128]{2,1,0:T(8,128)(2,1)S(1)} %fusion.2), channel_id=1, source_target_pairs={{0,24},{2,26},{4,28},{6,30},{8,16},{10,18},{12,20},{14,22},{16,8},... | collective-permute-start | bytes 110600 | tf_op jit(solution)/shard_map/ppermute | solution.py:385
  12.9 10.9 %collective-permute-start.5 = (bf16[4,144,128]{2,1,0:T(8,128)(2,1)S(1)}, bf16[4,144,128]{2,1,0:T(8,128)(2,1)S(1)}, u32[]{:S(2)}, u32[]{:S(2)}) collective-permute-start(bf16[4,144,128]{2,1,0:T(8,128)(2,1)S(1)} %pad_maximum_fusion.refs_1_.refs_0_), channel_id=1, source_target_pairs={{0,4},{2,6},{4,0},{6,2},{8,12},{10,14},{12,8},{14,10},{16,20},{18,... | collective-permute-start | bytes 442376 | tf_op jit(solution)/shard_map/ppermute | solution.py:385
  14.4 9.9 %collective-permute-start.7 = (bf16[4,144,128]{2,1,0:T(8,128)(2,1)S(1)}, bf16[4,144,128]{2,1,0:T(8,128)(2,1)S(1)}, u32[]{:S(2)}, u32[]{:S(2)}) collective-permute-start(bf16[4,144,128]{2,1,0:T(8,128)(2,1)S(1)} %pad_maximum_fusion.refs_1_.refs_0_), channel_id=1, source_target_pairs={{0,2},{2,0},{4,6},{6,4},{8,10},{10,8},{12,14},{14,12},{16,18},{18,... | collective-permute-start | bytes 442376 | tf_op jit(solution)/shard_map/ppermute | solution.py:385
  14.4 8.8 %collective-permute-start.8 = (bf16[4,128,128]{2,1,0:T(8,128)(2,1)S(1)}, bf16[4,128,128]{2,1,0:T(8,128)(2,1)S(1)}, u32[]{:S(2)}, u32[]{:S(2)}) collective-permute-start(bf16[4,128,128]{2,1,0:T(8,128)(2,1)S(1)} %slice.4), channel_id=1, source_target_pairs={{0,1},{1,0},{2,3},{3,2},{4,5},{5,4},{6,7},{7,6},{8,9},{9,8},{10,11... | collective-permute-start | bytes 393224 | tf_op jit(solution)/shard_map/ppermute | solution.py:388
  16.0 7.2 %collective-permute-start.3 = (bf16[4,128,128]{2,1,0:T(8,128)(2,1)S(1)}, bf16[4,128,128]{2,1,0:T(8,128)(2,1)S(1)}, u32[]{:S(2)}, u32[]{:S(2)}) collective-permute-start(bf16[4,128,128]{2,1,0:T(8,128)(2,1)S(1)} %slice.4), channel_id=1, source_target_pairs={{0,5},{1,4},{2,7},{3,6},{4,1},{5,0},{6,3},{7,2},{8,13},{9,12},{10,... | collective-permute-start | bytes 393224 | tf_op jit(solution)/shard_map/ppermute | solution.py:394
  23.2 1.9 %collective-permute-start.9 = (bf16[4,128,128]{2,1,0:T(8,128)(2,1)S(1)}, bf16[4,128,128]{2,1,0:T(8,128)(2,1)S(1)}, u32[]{:S(2)}, u32[]{:S(2)}) collective-permute-start(bf16[4,128,128]{2,1,0:T(8,128)(2,1)S(1)} %collective-permute-done.8.refs_0_), channel_id=1, source_target_pairs={{0,2},{2,0},{4,6},{6,4},{8,10},{10,8},{12,14},{14,12},{16,18},{18,... | collective-permute-start | bytes 393224 | tf_op jit(solution)/shard_map/ppermute | solution.py:385
  23.2 3.1 %collective-permute-start.4 = (bf16[4,128,128]{2,1,0:T(8,128)(2,1)S(1)}, bf16[4,128,128]{2,1,0:T(8,128)(2,1)S(1)}, u32[]{:S(2)}, u32[]{:S(2)}) collective-permute-start(bf16[4,128,128]{2,1,0:T(8,128)(2,1)S(1)} %collective-permute-done.3.refs_2_), channel_id=1, source_target_pairs={{0,2},{2,0},{4,6},{6,4},{8,10},{10,8},{12,14},{14,12},{16,18},{18,... | collective-permute-start | bytes 393224 | tf_op jit(solution)/shard_map/ppermute | solution.py:385
  23.7 1.8 %collective-permute-start.6 = (bf16[4,144,128]{2,1,0:T(8,128)(2,1)S(1)}, bf16[4,144,128]{2,1,0:T(8,128)(2,1)S(1)}, u32[]{:S(2)}, u32[]{:S(2)}) collective-permute-start(bf16[4,144,128]{2,1,0:T(8,128)(2,1)S(1)} %collective-permute-done.5.refs_1_.refs_0_), channel_id=1, source_target_pairs={{0,2},{2,0},{4,6},{6,4},{8,10},{10,8},{12,14},{14,12},{16,18},{18,... | collective-permute-start | bytes 442376 | tf_op jit(solution)/shard_map/ppermute | solution.py:385
  30.8 1.8 %collective-permute-start.10 = (f32[256,256]{1,0:T(8,128)S(1)}, f32[256,256]{1,0:T(8,128)S(1)}, u32[]{:S(2)}, u32[]{:S(2)}) collective-permute-start(f32[256,256]{1,0:T(8,128)S(1)} %get-tuple-element.9.own_ref), channel_id=1, source_target_pairs={{0,2},{2,0},{4,6},{6,4},{8,10},{10,8},{12,14},{14,12},{16,18},{18,... | collective-permute-start | bytes 786440 | tf_op jit(solution)/shard_map/ppermute | solution.py:385
  36.0 5.8 %collective-permute-start.11 = (f32[264,128]{1,0:T(8,128)S(1)}, f32[264,128]{1,0:T(8,128)S(1)}, u32[]{:S(2)}, u32[]{:S(2)}) collective-permute-start(f32[264,128]{1,0:T(8,128)S(1)} %get-tuple-element.11), channel_id=1, source_target_pairs={{0,4},{2,6},{4,0},{6,2},{8,12},{10,14},{12,8},{14,10},{16,20},{18,... | collective-permute-start | bytes 405512 | tf_op jit(solution)/shard_map/ppermute | solution.py:385
